TPU v7x, 32 devices: a whole 2x2x4 slice. The times are simulated.
32 devices in a mesh: section: 4 (over z), seq: 8 (over y, x, core).
Axes of the slice: x: 2, y: 2, z: 4, core: 2. Of those that a mesh axis runs over, the one named last changes fastest.
Arguments:
- forward_input: bfloat16 [4, 1024, 1024], P('section', 'seq'), may hold values from -6 to 6
- stored_input: bfloat16 [4, 1024, 1024], P('section', 'seq'), may hold values from -6 to 6
- output_cotangent: bfloat16 [4, 1024, 1024], P('section', 'seq'), may hold values from -6 to 6
- norm_gain: float32 [4, 1024], P('section'), may hold values from 0.5 to 2
- query_weight: bfloat16 [4, 1024, 512], P('section'), may hold values from -0.325 to 0.325
- key_weight: bfloat16 [4, 1024, 128], P('section'), may hold values from -7.3125 to 7.3125
- value_weight: bfloat16 [4, 1024, 128], P('section'), may hold values from -0.1875 to 0.1875
- output_weight: bfloat16 [4, 512, 1024], P('section'), may hold values from -0.25 to 0.25
- frame_index: int32 [1024], replicated, may hold values from 0 to 3, as said below
- valid_counts: int32 [8], replicated, may hold values from 32 to 128
Outputs:
- forward_next: bfloat16 [4, 1024, 1024], P('section', 'seq')
- backward_next: bfloat16 [4, 1024, 1024], P('section', 'seq')
Inputs may be any that keep to these rules, and one draw needn't show every extreme that they name: `frame_index`: frame numbers start at 0, never fall along the sequence, and every number up to the largest occurs.
All inputs are finite; a program needn't handle non-finite values.
Results may differ from a plain program's by a relative error of at most 0.028.
The roundings to bfloat16 on the way count: a program that leaves them out, or rounds other values in their place, can miss the bound.
Values may be sent and summed in bfloat16 or wider, within the bound.
No kernel may reach another device: no remote copies, remote signals or barrier semaphores. Data moves between devices by JAX's collectives and lax.ppermute only.
A program may use at most 64 MiB of HBM per device.

v0:
```python
from functools import partial
import math

import jax
import jax.numpy as jnp
from jax import lax
from jax.sharding import PartitionSpec as P

HEADS = 8
KV_HEADS = 2
HEAD_DIM = 64


NORM_EPSILON = 1e-05
MASKED_SCORE = -1e30


def shifted(block, axis, distance):
    devices = range(lax.axis_size(axis))
    route = [((i - distance) % len(devices), i) for i in devices]
    return lax.ppermute(block, axis, route)


def normalize(inputs, norm_scale):
    widened = inputs.astype(jnp.float32)
    inverse = lax.rsqrt(jnp.mean(widened * widened, axis=-1, keepdims=True) + NORM_EPSILON)
    return ((widened * inverse * norm_scale).astype(jnp.bfloat16), inverse)


def project(normed, weight):
    return jnp.dot(normed, weight, preferred_element_type=jnp.float32).astype(jnp.bfloat16)


def project_back(gradient, weight):
    return lax.dot_general(
        gradient, weight, (((1,), (1,)), ((), ())), preferred_element_type=jnp.float32
    )


def valid_table(valid_counts, slice_rows):
    inside = jnp.arange(slice_rows, dtype=jnp.int32)
    return (inside[None, :] < valid_counts[:, None]).reshape(-1)


def key_visible(query_frames, frame_index, valid_flags, first_row, key_rows):
    key_frames = lax.dynamic_slice_in_dim(frame_index, first_row, key_rows)
    key_valid = lax.dynamic_slice_in_dim(valid_flags, first_row, key_rows)
    return key_valid[None, :] & (key_frames[None, :] <= query_frames[:, None])


def fold_blocks(update, carried, members, first_row):
    row_count = members[0].shape[0]
    block_rows = math.gcd(row_count, 512)
    blocks = row_count // block_rows
    stacked = tuple((member.reshape((blocks, block_rows) + member.shape[1:]) for member in members))

    def fold_advance(state, item):
        block_index, pieces = item
        return (update(state, pieces, first_row + block_index * block_rows, block_rows), None)

    carried, _ = lax.scan(fold_advance, carried, (jnp.arange(blocks, dtype=jnp.int32), stacked))
    return carried


def attend(
    queries,
    query_frames,
    frame_index,
    valid_flags,
    score_scale,
    state,
    pieces,
    first_row,
    block_rows,
):

    def attend_compute(state):
        running_max, running_sum, weighted = state
        key_block, value_block = pieces
        groups = queries.shape[1]
        key_heads = key_block.reshape(block_rows, groups, -1)
        value_heads = value_block.reshape(block_rows, groups, -1)
        scores = (
            jnp.einsum("cgrd,kgd->grck", queries, key_heads, preferred_element_type=jnp.float32)
            * score_scale
        )
        visible = key_visible(query_frames, frame_index, valid_flags, first_row, block_rows)
        scores = jnp.where(visible, scores, MASKED_SCORE)
        new_max = jnp.maximum(running_max, jnp.max(scores, axis=-1))
        weights = jnp.where(visible, jnp.exp(scores - new_max[..., None]), 0.0)
        factor = jnp.exp(running_max - new_max)
        running_sum = running_sum * factor + jnp.sum(weights, axis=-1)
        weighted = weighted * factor[..., None] + jnp.einsum(
            "grck,kgd->grcd",
            weights.astype(jnp.bfloat16),
            value_heads,
            preferred_element_type=jnp.float32,
        )
        return (new_max, running_sum, weighted)

    beyond = frame_index[first_row] > query_frames[-1]
    return lax.cond(beyond, lambda state: state, attend_compute, state)


def finish(state, slice_rows):
    running_max, running_sum, weighted = state
    attended = weighted / running_sum[..., None]
    return (
        attended.transpose(2, 0, 1, 3).reshape(slice_rows, -1).astype(jnp.bfloat16),
        running_max + jnp.log(running_sum),
    )


def local_backward(
    query_heads,
    dout_heads,
    log_sums,
    deltas,
    query_frames,
    frame_index,
    valid_flags,
    score_scale,
    all_keys,
    all_values,
):
    row_count = all_keys.shape[0]
    block_rows = math.gcd(row_count, 512)
    blocks = row_count // block_rows
    groups = query_heads.shape[1]
    key_stack = all_keys.reshape(blocks, block_rows, groups, -1)
    value_stack = all_values.reshape(blocks, block_rows, groups, -1)
    head_size = key_stack.shape[-1]

    def local_advance(query_grad, item):
        block_index, key_heads, value_heads = item
        first_row = block_index * block_rows

        def local_compute(query_grad):
            scores = (
                jnp.einsum(
                    "cgrd,kgd->grck", query_heads, key_heads, preferred_element_type=jnp.float32
                )
                * score_scale
            )
            visible = key_visible(query_frames, frame_index, valid_flags, first_row, block_rows)
            scores = jnp.where(visible, scores, MASKED_SCORE)
            probability = jnp.where(visible, jnp.exp(scores - log_sums[..., None]), 0.0)
            prob_grads = jnp.einsum(
                "cgrd,kgd->grck", dout_heads, value_heads, preferred_element_type=jnp.float32
            )
            score_grads = (probability * (prob_grads - deltas[..., None])).astype(jnp.bfloat16)
            query_grad = query_grad + jnp.einsum(
                "grck,kgd->cgrd", score_grads, key_heads, preferred_element_type=jnp.float32
            )
            key_grad = (
                jnp.einsum(
                    "grck,cgrd->kgd", score_grads, query_heads, preferred_element_type=jnp.float32
                )
                * score_scale
            )
            value_grad = jnp.einsum(
                "grck,cgrd->kgd",
                probability.astype(jnp.bfloat16),
                dout_heads,
                preferred_element_type=jnp.float32,
            )
            return (
                query_grad,
                (key_grad.reshape(block_rows, -1), value_grad.reshape(block_rows, -1)),
            )

        def skipped(query_grad):
            empty = jnp.zeros((block_rows, groups * head_size), jnp.float32)
            return (query_grad, (empty, empty))

        beyond = frame_index[first_row] > query_frames[-1]
        return lax.cond(beyond, skipped, local_compute, query_grad)

    start_grad = jnp.zeros(query_heads.shape, jnp.float32)
    query_grad, terms = lax.scan(
        local_advance, start_grad, (jnp.arange(blocks, dtype=jnp.int32), key_stack, value_stack)
    )
    return (query_grad, (terms[0].reshape(row_count, -1), terms[1].reshape(row_count, -1)))


def on_device(
    forward_input,
    stored_input,
    output_cotangent,
    norm_gain,
    query_weight,
    key_weight,
    value_weight,
    output_weight,
    frame_index,
    valid_counts,
):
    slice_rows = forward_input.shape[1]
    group_size = HEADS // KV_HEADS
    score_scale = 1.0 / math.sqrt(HEAD_DIM)
    norm_scale = norm_gain[0]
    query_proj = query_weight[0]
    key_proj = key_weight[0]
    value_proj = value_weight[0]
    out_proj = output_weight[0]
    own_first = lax.axis_index("seq") * slice_rows
    query_frames = lax.dynamic_slice_in_dim(frame_index, own_first, slice_rows)
    valid_flags = valid_table(valid_counts, slice_rows)
    fwd_inputs = forward_input[0]
    normed_fwd, _ = normalize(fwd_inputs, norm_scale)
    query_fwd = project(normed_fwd, query_proj).reshape(slice_rows, KV_HEADS, group_size, HEAD_DIM)
    keys_fwd = project(normed_fwd, key_proj)
    values_fwd = project(normed_fwd, value_proj)
    bwd_inputs = stored_input[0]
    normed_bwd, inverse_bwd = normalize(bwd_inputs, norm_scale)
    query_flat = project(normed_bwd, query_proj)
    query_bwd = query_flat.reshape(slice_rows, KV_HEADS, group_size, HEAD_DIM)
    keys_bwd = project(normed_bwd, key_proj)
    values_bwd = project(normed_bwd, value_proj)
    state_shape = (KV_HEADS, group_size, slice_rows)
    empty_state = (
        jnp.full(state_shape, MASKED_SCORE, jnp.float32),
        jnp.zeros(state_shape, jnp.float32),
        jnp.zeros(state_shape + (HEAD_DIM,), jnp.float32),
    )
    attend_fwd = partial(attend, query_fwd, query_frames, frame_index, valid_flags, score_scale)
    attend_bwd = partial(attend, query_bwd, query_frames, frame_index, valid_flags, score_scale)
    state_fwd = fold_blocks(
        attend_fwd,
        empty_state,
        (
            lax.all_gather(keys_fwd, "seq", axis=0, tiled=True),
            lax.all_gather(values_fwd, "seq", axis=0, tiled=True),
        ),
        jnp.int32(0),
    )
    all_keys_bwd, all_values_bwd = (
        lax.all_gather(keys_bwd, "seq", axis=0, tiled=True),
        lax.all_gather(values_bwd, "seq", axis=0, tiled=True),
    )
    attended_fwd, _ = finish(state_fwd, slice_rows)
    layer_out = (
        fwd_inputs.astype(jnp.float32)
        + jnp.dot(attended_fwd, out_proj, preferred_element_type=jnp.float32)
    ).astype(jnp.bfloat16)
    forward_next = shifted(layer_out, "section", 1)
    state_bwd = fold_blocks(attend_bwd, empty_state, (all_keys_bwd, all_values_bwd), 0)
    attended_bwd, log_sums = finish(state_bwd, slice_rows)
    cotangent = output_cotangent[0]
    dout = project_back(cotangent, out_proj).astype(jnp.bfloat16)
    dout_heads = dout.reshape(slice_rows, KV_HEADS, group_size, HEAD_DIM)
    attended_heads = attended_bwd.reshape(slice_rows, KV_HEADS, group_size, HEAD_DIM)
    deltas = jnp.sum(
        dout_heads.astype(jnp.float32) * attended_heads.astype(jnp.float32), axis=-1
    ).transpose(1, 2, 0)
    query_grad, key_value_terms = local_backward(
        query_bwd,
        dout_heads,
        log_sums,
        deltas,
        query_frames,
        frame_index,
        valid_flags,
        score_scale,
        all_keys_bwd,
        all_values_bwd,
    )
    key_grad, value_grad = lax.psum_scatter(key_value_terms, "seq", scatter_dimension=0, tiled=True)
    query_grad = (query_grad * score_scale).astype(jnp.bfloat16).reshape(slice_rows, -1)
    normed_grad = project_back(query_grad, query_proj)
    normed_grad = normed_grad + project_back(key_grad.astype(jnp.bfloat16), key_proj)
    normed_grad = normed_grad + project_back(value_grad.astype(jnp.bfloat16), value_proj)
    scaled_grad = normed_grad * norm_scale
    widened = bwd_inputs.astype(jnp.float32)
    input_grad = (
        cotangent.astype(jnp.float32)
        + inverse_bwd * scaled_grad
        - widened * inverse_bwd**3 * jnp.mean(widened * scaled_grad, axis=-1, keepdims=True)
    )
    backward_next = shifted(input_grad.astype(jnp.bfloat16), "section", -1)
    return (forward_next[None], backward_next[None])


def solution(mesh):
    return jax.shard_map(
        on_device,
        mesh=mesh,
        in_specs=(
            P("section", "seq", None),
            P("section", "seq", None),
            P("section", "seq", None),
            P("section", None),
            P("section", None, None),
            P("section", None, None),
            P("section", None, None),
            P("section", None, None),
            P(),
            P(),
        ),
        out_specs=(P("section", "seq", None), P("section", "seq", None)),
        check_vma=False,
    )
```

profile of v0, /device:TPU:0, one launch (start us, length us, event | category | flops | bytes accessed | tf_op | source)
XLA Modules:
  0.0 174.9 jit_solution(11860080970593083439)
XLA Ops:
  7.3 1.2 fusion.64
  9.0 1.3 convolution_convert_fusion.4
  10.3 10.8 %all_gather.14 = bf16[1024,128]{1,0:T(8,128)(2,1)S(1)} all-gather(bf16[128,128]{1,0:T(8,128)(2,1)S(1)} %convolution_convert_fusion.4), channel_id=1, replica_groups=mesh['section'=4,'seq'=8] {'seq'}, dimensions={0}, use_global_device_ids=true | all-gather | bytes 294912 | tf_op jit(solution)/shard_map/all_gather | solution.py:238
  21.9 9.3 %all_gather.15 = bf16[1024,128]{1,0:T(8,128)(2,1)S(1)} all-gather(bf16[128,128]{1,0:T(8,128)(2,1)S(1)} %convolution_convert_fusion.3), channel_id=1, replica_groups=mesh['section'=4,'seq'=8] {'seq'}, dimensions={0}, use_global_device_ids=true | all-gather | bytes 294912 | tf_op jit(solution)/shard_map/all_gather | solution.py:239
  31.2 1.1 reshape.260
  32.9 0.7 dynamic_slice.102
  34.2 16.0 %while.49 = (s32[]{:T(128)}, f32[2,4,128]{2,1,0:T(4,128)S(1)}, f32[2,4,128]{2,1,0:T(4,128)S(1)}, f32[2,4,128,64]{2,3,1,0:T(8,128)S(1)}, s32[2]{0:T(128)}, /*inde...) while((s32[]{:T(128)}, f32[2,4,128]{2,1,0:T(4,128)S(1)}, ...), condition=%wide.region_13.14_spmd.clone, body=%wide.region_8.13_spmd.clone.sunk | while | flops 141298688 | bytes 8070591 | solution.py:61
  34.2 1.3 dynamic_slice.133
  36.8 1.2 slice.16
  39.2 1.3 fusion.109
  40.5 3.4 %conditional.10 = (f32[2,4,128]{2,1,0:T(4,128)S(1)}, f32[2,4,128]{2,1,0:T(4,128)S(1)}, f32[2,4,128,64]{2,3,1,0:T(8,128)S(1)}) conditional(s32[]{:T(128)} %bitcast.233, (s32[]{:T(128)}, pred[1024]{0:T(1024)(128)(4,1)}, s32[1024]{0:T(1024)S(1)}, s32[128]{0:T(128)}, bf16[2,512,128]{1,2,0:T(8,128)(2,1)S(1)}, /*index=5*/s32[]{:T(128)}, ...), branch_computations={%region_9.11_spmd, %region_12.12_spmd} | conditional | flops 141297664 | bytes 8060998 | solution.py:102
  40.6 0.8 dynamic_slice.89
  41.3 0.9 compare_and_fusion.1
  43.3 0.6 convolution_add_fusion.1
  44.0 1.2 dynamic_slice.133
  46.5 1.2 slice.16
  48.9 1.3 fusion.109
  50.2 1.4 convolution_convert_fusion
  51.7 1.0 copy.42
  52.8 1.9 %copy.43 = bf16[2,512,2,64]{1,3,2,0:T(8,128)(2,1)} copy(bf16[2,512,2,64]{3,2,1,0:T(2,128)(2,1)} %reshape.260) | data formatting | bytes 524288
  54.8 19.0 %while.50 = (s32[]{:T(128)}, f32[128,2,4,64]{0,3,2,1:T(8,128)S(1)}, f32[2,512,128]{2,1,0:T(8,128)}, f32[2,512,128]{2,1,0:T(8,128)}, s32[2]{0:T(128)S(1)}, /*inde...) while((s32[]{:T(128)}, f32[128,2,4,64]{0,3,2,1:T(8,128)S(1)}, ...), condition=%wide.region_18.19_spmd.clone, body=%wide.region_15.18_spmd.clone.sunk | while | flops 340001792 | bytes 13651395 | solution.py:180
  54.8 0.6 dynamic_slice.135
  56.0 0.7 dynamic_slice.136
  56.7 1.3 slice.17
  59.3 0.7 fusion.110
  60.1 6.1 %conditional.11 = (f32[128,2,4,64]{0,3,2,1:T(8,128)S(1)}, f32[1,512,128]{1,2,0:T(8,128)S(1)}, f32[1,512,128]{1,2,0:T(8,128)S(1)}) conditional(s32[]{:T(128)} %bitcast.236, (s32[]{:T(128)}, pred[1024]{0:T(1024)(128)(4,1)S(1)}, s32[1024]{0:T(1024)S(1)}, s32[128]{0:T(128)}, bf16[2,512,2,64]{1,3,2,0:T(8,128)(2,1)}, /*index=5*/s32[]{:T(128)}, ...), branch_computations={%region_16.16_spmd, %region_17.17_spmd} | conditional | flops 340000768 | bytes 11552322 | solution.py:177
  60.2 0.9 compare_and_fusion.2
  61.1 1.6 fusion.32
  62.7 1.4 fusion.29
  64.1 1.2 fusion.34
  66.5 0.8 constant_dynamic-update-slice_fusion.3
  67.3 0.6 dynamic_slice.135
  68.5 0.7 dynamic_slice.136
  69.2 1.3 slice.17
  71.8 0.7 fusion.110
  72.9 0.9 constant_dynamic-update-slice_fusion.3
  73.8 0.7 reduce-scatter.3.cloned.1.call-update
  74.5 1.1 fusion.61
  75.6 1.3 convolution_convert_fusion.6
  77.0 1.3 convolution_convert_fusion.5
  78.3 1.0 convolution_convert_fusion.2
  79.3 17.9 %all_gather.12 = bf16[1024,128]{1,0:T(8,128)(2,1)S(1)} all-gather(bf16[128,128]{1,0:T(8,128)(2,1)S(1)} %convolution_convert_fusion.6), channel_id=1, replica_groups=mesh['section'=4,'seq'=8] {'seq'}, dimensions={0}, use_global_device_ids=true | all-gather | bytes 294912 | tf_op jit(solution)/shard_map/all_gather | solution.py:232
  97.3 10.0 %all_gather.13 = bf16[1024,128]{1,0:T(8,128)(2,1)S(1)} all-gather(bf16[128,128]{1,0:T(8,128)(2,1)S(1)} %convolution_convert_fusion.5), channel_id=1, replica_groups=mesh['section'=4,'seq'=8] {'seq'}, dimensions={0}, use_global_device_ids=true | all-gather | bytes 294912 | tf_op jit(solution)/shard_map/all_gather | solution.py:233
  107.5 1.0 copy.33
  109.2 16.4 %while.48 = (s32[]{:T(128)}, f32[2,4,128]{2,1,0:T(4,128)S(1)}, f32[2,4,128]{2,1,0:T(4,128)S(1)}, f32[2,4,128,64]{2,3,1,0:T(8,128)S(1)}, s32[2]{0:T(128)}, /*inde...) while((s32[]{:T(128)}, f32[2,4,128]{2,1,0:T(4,128)S(1)}, ...), condition=%wide.region_6.7_spmd.clone, body=%wide.region_1.6_spmd.clone.sunk | while | flops 141298688 | bytes 8070591 | solution.py:61
  109.2 1.3 dynamic_slice.131
  111.7 1.3 slice.15
  114.3 1.3 fusion.108
  115.6 3.4 %conditional.9 = (f32[2,4,128]{2,1,0:T(4,128)S(1)}, f32[2,4,128]{2,1,0:T(4,128)S(1)}, f32[2,4,128,64]{2,3,1,0:T(8,128)S(1)}) conditional(s32[]{:T(128)} %bitcast.230, (s32[]{:T(128)}, pred[1024]{0:T(1024)(128)(4,1)}, s32[1024]{0:T(1024)S(1)}, s32[128]{0:T(128)}, bf16[2,512,128]{1,2,0:T(8,128)(2,1)S(1)}, /*index=5*/s32[]{:T(128)}, ...), branch_computations={%region_2.4_spmd, %region_5.5_spmd} | conditional | flops 141297664 | bytes 8060998 | solution.py:102
  115.7 0.8 dynamic_slice.83
  116.4 0.9 compare_and_fusion
  118.4 0.6 convolution_add_fusion
  119.1 1.3 dynamic_slice.131
  121.6 1.3 slice.15
  124.2 1.3 fusion.108
  125.6 1.0 fusion.51
  126.6 1.5 collective-permute-start
  128.2 1.1 fusion.75
  129.3 26.0 %reduce-scatter.3.cloned.1.call-done = f32[128,128]{1,0:T(8,128)} async-done(((f32[1024,128]{1,0:T(8,128)}), f32[128,128]{1,0:T(8,128)}) %reduce-scatter.3.cloned.1.call-update) | async-done | bytes 65552 | tf_op jit(solution)/shard_map/reduce_scatter | solution.py:268
  155.4 1.1 fusion.79
  157.3 3.4 %collective-permute-start.1 = (bf16[128,1024]{1,0:T(8,128)(2,1)S(1)}, bf16[128,1024]{1,0:T(8,128)(2,1)S(1)}, u32[]{:S(2)}, u32[]{:S(2)}) collective-permute-start(bf16[128,1024]{1,0:T(8,128)(2,1)S(1)} %fusion.67), channel_id=1, source_target_pairs={{8,0},{16,8},{24,16},{0,24},{9,1},{17,9},{25,17},{1,25},{10,2},{18... | collective-permute-start | bytes 786440 | tf_op jit(solution)/shard_map/ppermute | solution.py:21
  160.7 5.0 %collective-permute-done.1 = bf16[128,1024]{1,0:T(8,128)(2,1)S(1)} collective-permute-done((bf16[128,1024]{1,0:T(8,128)(2,1)S(1)}, bf16[128,1024]{1,0:T(8,128)(2,1)S(1)}, u32[]{:S(2)}, u32[]{:S(2)}) %collective-permute-start.1) | collective-permute-done | bytes 262176 | tf_op jit(solution)/shard_map/ppermute | solution.py:21
  165.7 1.7 copy.133
  167.4 0.7 copy.134
  (102 shorter events, 10.9 us)
Async XLA Ops:
  7.2 25.2 %copy-start = (bf16[1,1024,512]{2,1,0:T(8,128)(2,1)S(1)}, bf16[1,1024,512]{2,1,0:T(8,128)(2,1)}, u32[]{:S(2)}) copy-start(bf16[1,1024,512]{2,1,0:T(8,128)(2,1)} %param.26) | copy-start | bytes 3145732
  7.2 14.4 %copy-start.2 = (bf16[1,128,1024]{2,1,0:T(8,128)(2,1)S(1)}, bf16[1,128,1024]{2,1,0:T(8,128)(2,1)}, u32[]{:S(2)}) copy-start(bf16[1,128,1024]{2,1,0:T(8,128)(2,1)} %param.23) | copy-start | bytes 786436
  7.2 14.4 %copy-start.10 = (f32[1,1024]{1,0:T(1,128)S(1)}, f32[1,1024]{1,0:T(1,128)}, u32[]{:S(2)}) copy-start(f32[1,1024]{1,0:T(1,128)} %param.25) | copy-start | bytes 12292
  7.2 14.3 %copy-start.6 = (bf16[1,1024,128]{2,1,0:T(8,128)(2,1)S(1)}, bf16[1,1024,128]{2,1,0:T(8,128)(2,1)}, u32[]{:S(2)}) copy-start(bf16[1,1024,128]{2,1,0:T(8,128)(2,1)} %param.28) | copy-start | bytes 786436
  7.2 121.0 %reduce-scatter.5.cloned.1.call-start = ((), (), s32[]{:S(2)}) async-start(), calls=%async_computation.3 | async-start | bytes 589824 | tf_op jit(solution)/shard_map/reduce_scatter | solution.py:268
  9.0 23.4 %copy-start.13 = (f32[128]{0:T(128)}, f32[128]{0:T(128)S(1)}, u32[]{:S(2)}) copy-start(f32[128]{0:T(128)S(1)} %get-tuple-element.745) | copy-start | bytes 1540
  21.6 11.3 %copy-start.9 = (s32[1024]{0:T(1024)S(1)}, s32[1024]{0:T(1024)}, u32[]{:S(2)}) copy-start(s32[1024]{0:T(1024)} %param.30) | copy-start | bytes 12292
  34.2 16.0 %copy-start.1 = (bf16[1,512,1024]{2,1,0:T(8,128)(2,1)S(1)}, bf16[1,512,1024]{2,1,0:T(8,128)(2,1)}, u32[]{:S(2)}) copy-start(bf16[1,512,1024]{2,1,0:T(8,128)(2,1)} %param.29) | copy-start | bytes 3145732
  54.8 20.8 %copy-start.11 = (f32[1,1024]{1,0:T(1,128)S(1)}, f32[1,1024]{1,0:T(1,128)}, u32[]{:S(2)}) copy-start(f32[1,1024]{1,0:T(1,128)} %param.25) | copy-start | bytes 12292
  73.7 4.5 %copy-start.4 = (bf16[1,128,1024]{2,1,0:T(8,128)(2,1)S(1)}, bf16[1,128,1024]{2,1,0:T(8,128)(2,1)}, u32[]{:S(2)}) copy-start(bf16[1,128,1024]{2,1,0:T(8,128)(2,1)} %param.22) | copy-start | bytes 786436
  73.8 81.6 %reduce-scatter.3.cloned.1.call-start = ((), (), s32[]{:S(2)}) async-start(), calls=%async_computation.2 | async-start | bytes 589824 | tf_op jit(solution)/shard_map/reduce_scatter | solution.py:268
  125.5 2.7 %copy-start.7 = (bf16[1,1024,128]{2,1,0:T(8,128)(2,1)S(1)}, bf16[1,1024,128]{2,1,0:T(8,128)(2,1)}, u32[]{:S(2)}) copy-start(bf16[1,1024,128]{2,1,0:T(8,128)(2,1)} %param.28) | copy-start | bytes 786436
  125.5 30.9 %copy-start.3 = (bf16[1,128,1024]{2,1,0:T(8,128)(2,1)S(1)}, bf16[1,128,1024]{2,1,0:T(8,128)(2,1)}, u32[]{:S(2)}) copy-start(bf16[1,128,1024]{2,1,0:T(8,128)(2,1)} %param.23) | copy-start | bytes 786436
  125.5 30.9 %copy-start.12 = (f32[1,1024]{1,0:T(1,128)S(1)}, f32[1,1024]{1,0:T(1,128)}, u32[]{:S(2)}) copy-start(f32[1,1024]{1,0:T(1,128)} %param.25) | copy-start | bytes 12292
  125.6 29.8 %copy-start.8 = (bf16[1,1024,128]{2,1,0:T(8,128)(2,1)S(1)}, bf16[1,1024,128]{2,1,0:T(8,128)(2,1)}, u32[]{:S(2)}) copy-start(bf16[1,1024,128]{2,1,0:T(8,128)(2,1)} %param.27) | copy-start | bytes 786436
  126.6 34.1 %collective-permute-start = (bf16[128,1024]{1,0:T(8,128)(2,1)}, bf16[128,1024]{1,0:T(8,128)(2,1)}, u32[]{:S(2)}, u32[]{:S(2)}) collective-permute-start(bf16[128,1024]{1,0:T(8,128)(2,1)} %fusion.51), channel_id=1, source_target_pairs={{24,0},{0,8},{8,16},{16,24},{25,1},{1,9},{9,17},{17,25},{26,2},{2,... | collective-permute-start | bytes 786440 | tf_op jit(solution)/shard_map/ppermute | solution.py:21
  129.3 27.8 %copy-start.5 = (bf16[1,128,1024]{2,1,0:T(8,128)(2,1)S(1)}, bf16[1,128,1024]{2,1,0:T(8,128)(2,1)}, u32[]{:S(2)}) copy-start(bf16[1,128,1024]{2,1,0:T(8,128)(2,1)} %param.24) | copy-start | bytes 786436
  129.3 27.8 %copy-start.14 = (f32[128]{0:T(128)S(1)}, f32[128]{0:T(128)}, u32[]{:S(2)}) copy-start(f32[128]{0:T(128)} %copy-done.13) | copy-start | bytes 1540
  129.3 27.8 %copy-start.15 = (f32[128]{0:T(128)S(1)}, f32[128]{0:T(128)}, u32[]{:S(2)}) copy-start(f32[128]{0:T(128)} %get-tuple-element.744) | copy-start | bytes 1540
  157.3 8.4 %collective-permute-start.1 = (bf16[128,1024]{1,0:T(8,128)(2,1)S(1)}, bf16[128,1024]{1,0:T(8,128)(2,1)S(1)}, u32[]{:S(2)}, u32[]{:S(2)}) collective-permute-start(bf16[128,1024]{1,0:T(8,128)(2,1)S(1)} %fusion.67), channel_id=1, source_target_pairs={{8,0},{16,8},{24,16},{0,24},{9,1},{17,9},{25,17},{1,25},{10,2},{18... | collective-permute-start | bytes 786440 | tf_op jit(solution)/shard_map/ppermute | solution.py:21
Sparse Core Ops, SparseCore 0:
  73.9 44.2 reduce-scatter.4
  121.2 34.0 reduce-scatter.2
where the time goes:
time: 176 us; the launch traced here: 175 us
  blocking collectives  48 us (27%)
  local copies, waits for them, and re-layouts  32.2 us (18%)
  waiting for transfers between devices  31.8 us (18%)
  matrix products  18.2 us (10%)
  between operations  14.5 us (8%)
  other arithmetic  13.5 us (8%)
  loops' own time  11.9 us (7%)
  starting transfers between devices  4.94 us (3%)
    reduce_scatter x2, waiting for transfers between devices, on_device(): lax.psum_scatter(key_value_terms, 'seq', scatter_dimension=0, tiled=True)  26.1 us
    all_gather x1, blocking collectives, on_device(): lax.all_gather(keys_fwd, 'seq', axis=0, tiled=True)  17.9 us
    all_gather x1, blocking collectives, on_device(): lax.all_gather(keys_bwd, 'seq', axis=0, tiled=True)  10.8 us
    all_gather x1, blocking collectives, on_device(): lax.all_gather(values_fwd, 'seq', axis=0, tiled=True)  10 us
    all_gather x1, blocking collectives, on_device(): lax.all_gather(values_bwd, 'seq', axis=0, tiled=True)  9.28 us
    another operation x2, loops' own time, fold_blocks(): lax.scan(fold_advance, carried, (jnp.arange(blocks, dtype=jnp.int32), sta...  7.78 us
    lt x6, other arithmetic, valid_table(): return (inside[None, :] < valid_counts[:, None]).reshape(-1)  6.62 us
    dynamic_slice x8, local copies, waits for them, and re-layouts, fold_blocks(): lax.scan(fold_advance, carried, (jnp.arange(blocks, dtype=jnp.int32), sta...  6.33 us
  transfers between devices with their start and end apart: 4, of which 2 were waited for; matrix products, arithmetic and copies ran while one was open for 13% of the time, Pallas kernels for 0%

commit v1 on v0

v1 whole, which is shorter than its diff:
```python
from functools import partial
import math

import jax
import jax.numpy as jnp
from jax import lax
from jax.experimental import pallas as pl
from jax.experimental.pallas import tpu as pltpu
from jax.sharding import PartitionSpec as P

HEADS = 8
KV_HEADS = 2
HEAD_DIM = 64
GROUP = HEADS // KV_HEADS
KV_COLS = KV_HEADS * HEAD_DIM
PAIRS = HEADS // 2

NORM_EPSILON = 1e-05
MASKED_SCORE = -1e30
F32 = jnp.float32
BF16 = jnp.bfloat16

NN = (((1,), (0,)), ((), ()))
NT = (((1,), (1,)), ((), ()))


def dot(a, b, dims=NN):
    return lax.dot_general(a, b, dims, preferred_element_type=F32)


def vmem(count):
    return [pl.BlockSpec(memory_space=pltpu.VMEM)] * count


def shape(dims, dtype):
    return jax.ShapeDtypeStruct(dims, dtype)


def rms(inputs, gain):
    widened = inputs.astype(F32)
    inverse = lax.rsqrt(jnp.mean(widened * widened, axis=-1, keepdims=True) + NORM_EPSILON)
    return (widened * inverse * gain).astype(BF16), inverse, widened


def project_kv(x_ref, gain_ref, wk_ref, wv_ref, kv_ref):
    normed, _, _ = rms(x_ref[...], gain_ref[...])
    kv_ref[:, :KV_COLS] = dot(normed, wk_ref[...]).astype(BF16)
    kv_ref[:, KV_COLS:] = dot(normed, wv_ref[...]).astype(BF16)


def spread_heads(flat, out_ref, scale):
    rows = flat.shape[0]
    flat = flat.astype(BF16).astype(F32) * scale
    lane = lax.broadcasted_iota(jnp.int32, (rows, KV_COLS), 1)
    for head in range(HEADS):
        tile = head // 2
        block = flat[:, tile * KV_COLS : (tile + 1) * KV_COLS]
        group = head // GROUP
        if head % 2 != group:
            block = pltpu.roll(block, HEAD_DIM, 1)
        block = jnp.where((lane // HEAD_DIM) == group, block, 0.0)
        out_ref[head * rows : (head + 1) * rows, :] = block.astype(BF16)


def prepare(
    order,
    me_ref,
    counts_ref,
    xf_ref,
    xb_ref,
    cot_ref,
    gain_ref,
    wq_ref,
    wk_ref,
    wv_ref,
    wo_ref,
    frames_ref,
    kvf_ref,
    qf_ref,
    qb_ref,
    dout_ref,
    bias_ref,
):
    gain = gain_ref[...]
    rows = xf_ref.shape[0]
    normed_f, _, _ = rms(xf_ref[...], gain)
    kvf_ref[:, :KV_COLS] = dot(normed_f, wk_ref[...]).astype(BF16)
    kvf_ref[:, KV_COLS:] = dot(normed_f, wv_ref[...]).astype(BF16)
    scale = 1.0 / math.sqrt(HEAD_DIM)
    spread_heads(dot(normed_f, wq_ref[...]), qf_ref, scale)
    normed_b, _, _ = rms(xb_ref[...], gain)
    spread_heads(dot(normed_b, wq_ref[...]), qb_ref, scale)
    spread_heads(dot(cot_ref[...], wo_ref[...], NT), dout_ref, 1.0)
    me = me_ref[0]
    row = lax.broadcasted_iota(jnp.int32, (rows, rows), 0)
    query_frames = jnp.broadcast_to(frames_ref[pl.ds(me, 1), :], (rows, rows))
    for place, step in enumerate(order):
        source = jnp.bitwise_xor(me, step)
        own = jnp.broadcast_to(frames_ref[pl.ds(source, 1), :], (rows, rows))
        key_frames = jnp.transpose(own.astype(F32)).astype(jnp.int32)
        visible = (key_frames <= query_frames) & (row < counts_ref[source])
        bias_ref[place * rows : (place + 1) * rows, :] = jnp.where(visible, 0.0, MASKED_SCORE)


def scores_of(keys_ref, q_rows, bias_ref, s_ref, chunk):
    total = keys_ref.shape[0]
    top = None
    for first in range(0, total, chunk):
        block = dot(keys_ref[first : first + chunk, :KV_COLS], q_rows, NT)
        bias = bias_ref[first : first + chunk, :]
        block = block + jnp.concatenate([bias, bias], axis=1)
        s_ref[first : first + chunk, :] = block
        part = jnp.max(block, axis=0, keepdims=True)
        top = part if top is None else jnp.maximum(top, part)
    return top


def attend_backward(count, *refs):
    pieces = refs[:count]
    q_ref, dout_ref, bias_ref = refs[count : count + 3]
    even_refs = refs[count + 3 : count + 3 + count // 2]
    odd_ref, dq_ref = refs[count + 3 + count // 2 : count + 5 + count // 2]
    kv_ref, s_ref, dp_ref, e_ref, u_ref, rs_ref, dqt_ref, qs_ref, ds_ref = refs[count + 5 + count // 2 :]
    rows = pieces[0].shape[0]
    total = rows * count
    chunk = 2 * rows
    for place, piece in enumerate(pieces):
        kv_ref[place * rows : (place + 1) * rows, :] = piece[...]
    keys_t = jnp.transpose(kv_ref[:, :KV_COLS])
    scale = 1.0 / math.sqrt(HEAD_DIM)
    wide = 2 * rows
    for pair in range(PAIRS):
        cols = slice(pair * wide, (pair + 1) * wide)
        q_rows = q_ref[cols, :]
        dout_rows = dout_ref[cols, :]
        top = scores_of(kv_ref, q_rows, bias_ref, s_ref, chunk)
        row_sum = jnp.zeros((1, wide), F32)
        mixed = jnp.zeros((1, wide), F32)
        for first in range(0, total, chunk):
            weights = jnp.exp(s_ref[first : first + chunk, :] - top)
            prob_grad = dot(kv_ref[first : first + chunk, KV_COLS:], dout_rows, NT)
            row_sum = row_sum + jnp.sum(weights, axis=0, keepdims=True)
            mixed = mixed + jnp.sum(weights * prob_grad, axis=0, keepdims=True)
            dp_ref[first : first + chunk, :] = prob_grad
            s_ref[first : first + chunk, :] = weights
        inverse_sum = 1.0 / row_sum
        delta = mixed * inverse_sum
        rs_ref[2 * pair : 2 * pair + 1, :] = inverse_sum[:, :rows]
        rs_ref[2 * pair + 1 : 2 * pair + 2, :] = inverse_sum[:, rows:]
        for first in range(0, total, chunk):
            weights = s_ref[first : first + chunk, :]
            e_ref[first : first + chunk, cols] = weights.astype(BF16)
            u_ref[first : first + chunk, cols] = (
                weights * (dp_ref[first : first + chunk, :] - delta)
            ).astype(BF16)
        query_grad = dot(keys_t, u_ref[:, cols]) * (inverse_sum * scale)
        group = (2 * pair) // GROUP
        part = query_grad[group * HEAD_DIM : (group + 1) * HEAD_DIM, :]
        dqt_ref[2 * pair * HEAD_DIM : (2 * pair + 1) * HEAD_DIM, :] = part[:, :rows]
        dqt_ref[(2 * pair + 1) * HEAD_DIM : (2 * pair + 2) * HEAD_DIM, :] = part[:, rows:]
    dq_ref[...] = jnp.transpose(dqt_ref[...]).astype(BF16)
    rs_t = jnp.transpose(rs_ref[...])
    for head in range(HEADS):
        lines = slice(head * rows, (head + 1) * rows)
        factor = rs_t[:, head : head + 1]
        qs_ref[lines, :] = (q_ref[lines, :].astype(F32) * factor).astype(BF16)
        ds_ref[lines, :] = (dout_ref[lines, :].astype(F32) * factor).astype(BF16)
    q_scaled = qs_ref[...]
    dout_scaled = ds_ref[...]
    for place in range(count):
        lines = slice(place * rows, (place + 1) * rows)
        key_grad = dot(u_ref[lines, :], q_scaled).astype(BF16)
        value_grad = dot(e_ref[lines, :], dout_scaled).astype(BF16)
        half = count // 2
        target = even_refs[place] if place < half else odd_ref.at[place - half]
        target[:, :KV_COLS] = key_grad
        target[:, KV_COLS:] = value_grad


def attend_forward(count, *refs):
    pieces = refs[:count]
    q_ref, bias_ref, x_ref, wo_ref, out_ref = refs[count : count + 5]
    kv_ref, s_ref, e_ref, at_ref = refs[count + 5 :]
    rows = pieces[0].shape[0]
    total = rows * count
    chunk = 2 * rows
    for place, piece in enumerate(pieces):
        kv_ref[place * rows : (place + 1) * rows, :] = piece[...]
    values_t = jnp.transpose(kv_ref[:, KV_COLS:])
    wide = 2 * rows
    for pair in range(PAIRS):
        q_rows = q_ref[pair * wide : (pair + 1) * wide, :]
        top = scores_of(kv_ref, q_rows, bias_ref, s_ref, chunk)
        row_sum = jnp.zeros((1, wide), F32)
        for first in range(0, total, chunk):
            weights = jnp.exp(s_ref[first : first + chunk, :] - top)
            row_sum = row_sum + jnp.sum(weights, axis=0, keepdims=True)
            e_ref[first : first + chunk, :] = weights.astype(BF16)
        mixed = dot(values_t, e_ref[...]) * (1.0 / row_sum)
        group = (2 * pair) // GROUP
        part = mixed[group * HEAD_DIM : (group + 1) * HEAD_DIM, :]
        at_ref[2 * pair * HEAD_DIM : (2 * pair + 1) * HEAD_DIM, :] = part[:, :rows]
        at_ref[(2 * pair + 1) * HEAD_DIM : (2 * pair + 2) * HEAD_DIM, :] = part[:, rows:]
    attended = jnp.transpose(at_ref[...]).astype(BF16)
    out_ref[...] = (x_ref[...].astype(F32) + dot(attended, wo_ref[...])).astype(BF16)


def query_back(dq_ref, wq_ref, out_ref):
    out_ref[...] = dot(dq_ref[...], wq_ref[...], NT)


def add_pieces(count, *refs):
    for place in range(count):
        left = refs[place][...].astype(F32)
        refs[count + 1 + place][...] = (left + refs[count][place].astype(F32)).astype(BF16)


def input_back(count, *refs):
    pieces = refs[:count]
    base_ref, x_ref, cot_ref, gain_ref, wk_ref, wv_ref, out_ref = refs[count:]
    grads = pieces[0][...].astype(F32)
    for piece in pieces[1:]:
        grads = grads + piece[...].astype(F32)
    grads = grads.astype(BF16)
    gain = gain_ref[...]
    normed_grad = base_ref[...] + dot(grads[:, :KV_COLS], wk_ref[...], NT)
    normed_grad = normed_grad + dot(grads[:, KV_COLS:], wv_ref[...], NT)
    _, inverse, widened = rms(x_ref[...], gain)
    scaled = normed_grad * gain
    mean = jnp.mean(widened * scaled, axis=-1, keepdims=True)
    grad = cot_ref[...].astype(F32) + inverse * scaled - widened * (inverse * inverse * inverse * mean)
    out_ref[...] = grad.astype(BF16)


def call(kernel, outs, args, scratch=(), smem=0, name=None):
    specs = [pl.BlockSpec(memory_space=pltpu.SMEM)] * smem + vmem(len(args) - smem)
    out_specs = vmem(len(outs)) if isinstance(outs, (list, tuple)) else vmem(1)[0]
    return pl.pallas_call(
        kernel, out_shape=outs, in_specs=specs, out_specs=out_specs, scratch_shapes=list(scratch), name=name
    )(*args)


def swap(block, step, size):
    return lax.ppermute(block, "seq", [(i, i ^ step) for i in range(size)])


def gather_pieces(block, size):
    if size > 8 or size % 2:
        everything = lax.all_gather(block, "seq", axis=0)
        me = lax.axis_index("seq")
        return [lax.dynamic_index_in_dim(everything, me ^ step, 0, False) for step in order_of(size)]
    near = [block] + [swap(block, step, size) for step in range(2, size, 2)]
    return near + [swap(piece, 1, size) for piece in near]


def order_of(size):
    return list(range(0, size, 2)) + list(range(1, size, 2))


def on_device(
    size,
    forward_input,
    stored_input,
    output_cotangent,
    norm_gain,
    query_weight,
    key_weight,
    value_weight,
    output_weight,
    frame_index,
    valid_counts,
):
    xf, xb, cot = forward_input[0], stored_input[0], output_cotangent[0]
    wq, wk, wv, wo = query_weight[0], key_weight[0], value_weight[0], output_weight[0]
    rows, width = xf.shape
    total = rows * size
    sections = lax.axis_size("section")
    order = order_of(size)
    half = size // 2
    kv_shape = shape((rows, 2 * KV_COLS), BF16)
    spread = shape((HEADS * rows, KV_COLS), BF16)
    wide = 2 * rows

    kvb = call(project_kv, kv_shape, (xb, norm_gain, wk, wv), name="project_kv")
    pieces_b = gather_pieces(kvb, size)
    me = lax.axis_index("seq").astype(jnp.int32).reshape(1)
    kvf, qf, qb, dout, bias = call(
        partial(prepare, order),
        (kv_shape, spread, spread, spread, shape((total, rows), F32)),
        (me, valid_counts, xf, xb, cot, norm_gain, wq, wk, wv, wo, frame_index.reshape(size, rows)),
        smem=2,
        name="prepare",
    )
    pieces_f = gather_pieces(kvf, size)
    *grads, dq = call(
        partial(attend_backward, size),
        (kv_shape,) * half + (shape((half, rows, 2 * KV_COLS), BF16), shape((rows, HEADS * HEAD_DIM), BF16)),
        (*pieces_b, qb, dout, bias),
        scratch=(
            pltpu.VMEM((total, 2 * KV_COLS), BF16),
            pltpu.VMEM((total, wide), F32),
            pltpu.VMEM((total, wide), F32),
            pltpu.VMEM((total, HEADS * rows), BF16),
            pltpu.VMEM((total, HEADS * rows), BF16),
            pltpu.VMEM((HEADS, rows), F32),
            pltpu.VMEM((HEADS * HEAD_DIM, rows), F32),
            pltpu.VMEM((HEADS * rows, KV_COLS), BF16),
            pltpu.VMEM((HEADS * rows, KV_COLS), BF16),
        ),
        name="attend_backward",
    )
    even, odd = grads[:half], grads[half]
    if size > 8 or size % 2:
        index = lax.axis_index("seq")
        both = jnp.stack(list(even) + [odd[i] for i in range(half)]).astype(F32)
        places = jnp.argsort(jnp.array(order, jnp.int32) ^ index)
        summed = lax.psum_scatter(both[places], "seq", scatter_dimension=0, tiled=True)
        received = [summed[0].astype(BF16)]
    else:
        other = swap(odd, 1, size)
        sums = call(partial(add_pieces, half), (kv_shape,) * half, (*even, other), name="add_pieces")
        received = [sums[0]] + [swap(sums[i], 2 * i, size) for i in range(1, half)]
    layer_out = call(
        partial(attend_forward, size),
        shape((rows, width), BF16),
        (*pieces_f, qf, bias, xf, wo),
        scratch=(
            pltpu.VMEM((total, 2 * KV_COLS), BF16),
            pltpu.VMEM((total, wide), F32),
            pltpu.VMEM((total, wide), BF16),
            pltpu.VMEM((HEADS * HEAD_DIM, rows), F32),
        ),
        name="attend_forward",
    )
    forward_next = lax.ppermute(layer_out, "section", [((i - 1) % sections, i) for i in range(sections)])
    base = call(query_back, shape((rows, width), F32), (dq, wq), name="query_back")
    input_grad = call(
        partial(input_back, len(received)),
        shape((rows, width), BF16),
        (*received, base, xb, cot, norm_gain, wk, wv),
        name="input_back",
    )
    backward_next = lax.ppermute(input_grad, "section", [((i + 1) % sections, i) for i in range(sections)])
    return (forward_next[None], backward_next[None])


def solution(mesh):
    return jax.shard_map(
        partial(on_device, mesh.shape["seq"]),
        mesh=mesh,
        in_specs=(
            P("section", "seq", None),
            P("section", "seq", None),
            P("section", "seq", None),
            P("section", None),
            P("section", None, None),
            P("section", None, None),
            P("section", None, None),
            P("section", None, None),
            P(),
            P(),
        ),
        out_specs=(P("section", "seq", None), P("section", "seq", None)),
        check_vma=False,
    )
```

time: 176 us -> 59.8 us (0.34)
  blocking collectives: 48 us -> 0 us
  local copies, waits for them, and re-layouts: 32.2 us -> 4.03 us
  Pallas kernels: 0 us -> 24.9 us
  waiting for transfers between devices: 31.8 us -> 13.5 us
  matrix products: 18.2 us -> 0 us
  between operations: 14.5 us -> 0.81 us
  other arithmetic: 13.5 us -> 0 us
  loops' own time: 11.9 us -> 0 us
  starting transfers between devices: 4.94 us -> 16.3 us
    all_gather x4 -> x0, blocking collectives: 48 us -> none  [the longest x1 17.9 us: on_device(): lax.all_gather(keys_fwd, 'seq', axis=0, tiled=True)]
    reduce_scatter x2 -> x0, waiting for transfers between devices: 26.1 us -> none  [on_device(): lax.psum_scatter(key_value_terms, 'seq', scatter_dimension=0, tiled=True)]
    pallas_call x0 -> x7, Pallas kernels: none -> 24.9 us  [call(): pl.pallas_call(kernel, out_shape=outs, in_specs=specs, out_specs=out_spec...]
    dot_general x20 -> x0, matrix products: 18.2 us -> none  [the longest x6 5.63 us: project(): jnp.dot(normed, weight, preferred_element_type=jnp.float32)]
    dynamic_slice x21 -> x0, local copies, waits for them, and re-layouts: 12.5 us -> none  [the longest x8 6.33 us: fold_blocks(): lax.scan(fold_advance, carried, (jnp.arange(blocks, dtype=jnp.int32), sta...]
    another operation x9 -> x0, loops' own time: 11.9 us -> none  [the longest x2 7.78 us: fold_blocks(): lax.scan(fold_advance, carried, (jnp.arange(blocks, dtype=jnp.int32), sta...]
    ppermute x2 -> x20, starting transfers between devices: 4.86 us -> 16.3 us  [the longest x18 12.5 us: swap(): return lax.ppermute(block, 'seq', [(i, i ^ step) for i in range(size)])]
    ppermute x2 -> x20, waiting for transfers between devices: 5.02 us -> 13.5 us  [the longest x18 8.1 us: swap(): return lax.ppermute(block, 'seq', [(i, i ^ step) for i in range(size)])]
  transfers between devices with their start and end apart: 4 -> 20, of which waited for: 2 -> 6; matrix products, arithmetic and copies ran while one was open for 13% -> 0% of each run, Pallas kernels for 0% -> 27%
where the time goes in v1:
time: 59.8 us; the launch traced here: 59.5 us
  Pallas kernels  24.9 us (42%)
  starting transfers between devices  16.3 us (27%)
  waiting for transfers between devices  13.5 us (23%)
  local copies, waits for them, and re-layouts  4.03 us (7%)
  between operations  0.81 us (1%)
    pallas_call x7, Pallas kernels, call(): pl.pallas_call(kernel, out_shape=outs, in_specs=specs, out_specs=out_spec...  24.9 us
    ppermute x18, starting transfers between devices, swap(): return lax.ppermute(block, 'seq', [(i, i ^ step) for i in range(size)])  12.5 us
    ppermute x18, waiting for transfers between devices, swap(): return lax.ppermute(block, 'seq', [(i, i ^ step) for i in range(size)])  8.1 us
    ppermute x1, waiting for transfers between devices, on_device(): lax.ppermute(input_grad, 'section', [((i + 1) % sections, i) for i in ran...  5.36 us
    unnamed x40, local copies, waits for them, and re-layouts  4.03 us
    ppermute x1, starting transfers between devices, on_device(): lax.ppermute(input_grad, 'section', [((i + 1) % sections, i) for i in ran...  2.75 us
  transfers between devices with their start and end apart: 20, of which 6 were waited for; matrix products, arithmetic and copies ran while one was open for 0% of the time, Pallas kernels for 27%

profile of v1, /device:TPU:0, one launch (start us, length us, event | category | flops | bytes accessed | tf_op | source)
XLA Modules:
  0.0 59.5 jit_solution(4449708179478199378)
XLA Ops:
  0.6 2.1 %project_kv.1.refs_0_ = bf16[128,256]{1,0:T(8,128)(2,1)} custom-call(bf16[128,1024]{1,0:T(8,128)(2,1)} %bitcast.15, f32[1,1024]{1,0:T(1,128)} %refs_7_.1, bf16[1024,128]{1,0:T(8,128)(2,1)} %bitcast.18, bf16[1024,128]{1,0:T(8,128)(2,1)} %bitcast.21), custom_call_target="tpu_custom_call" | custom-call | tf_op jit(solution)/shard_map/project_kv/pallas_call | solution.py:238
  2.8 3.0 %collective-permute-start.8 = (bf16[128,256]{1,0:T(8,128)(2,1)}, bf16[128,256]{1,0:T(8,128)(2,1)S(1)}, u32[]{:S(2)}, u32[]{:S(2)}) collective-permute-start(bf16[128,256]{1,0:T(8,128)(2,1)} %project_kv.1.refs_0_), channel_id=1, source_target_pairs={{0,2},{1,3},{2,0},{3,1},{4,6},{5,7},{6,4},{7,5},{8,10},{9,11},{10,... | collective-permute-start | bytes 196616 | tf_op jit(solution)/shard_map/ppermute | solution.py:244
  5.7 1.5 %collective-permute-start.9 = (bf16[128,256]{1,0:T(8,128)(2,1)}, bf16[128,256]{1,0:T(8,128)(2,1)S(1)}, u32[]{:S(2)}, u32[]{:S(2)}) collective-permute-start(bf16[128,256]{1,0:T(8,128)(2,1)} %project_kv.1.refs_0_), channel_id=1, source_target_pairs={{0,4},{1,5},{2,6},{3,7},{4,0},{5,1},{6,2},{7,3},{8,12},{9,13},{10,... | collective-permute-start | bytes 196616 | tf_op jit(solution)/shard_map/ppermute | solution.py:244
  7.3 0.0 collective-permute-start.10
  7.3 0.0 collective-permute-start.11
  7.3 1.1 %collective-permute-done.8.refs_1_ = bf16[128,256]{1,0:T(8,128)(2,1)S(1)} collective-permute-done((bf16[128,256]{1,0:T(8,128)(2,1)}, bf16[128,256]{1,0:T(8,128)(2,1)S(1)}, u32[]{:S(2)}, u32[]{:S(2)}) %collective-permute-start.8) | collective-permute-done | bytes 65568 | tf_op jit(solution)/shard_map/ppermute | solution.py:244
  8.4 0.0 collective-permute-start.12
  8.4 1.8 %collective-permute-done.9.refs_2_ = bf16[128,256]{1,0:T(8,128)(2,1)S(1)} collective-permute-done((bf16[128,256]{1,0:T(8,128)(2,1)}, bf16[128,256]{1,0:T(8,128)(2,1)S(1)}, u32[]{:S(2)}, u32[]{:S(2)}) %collective-permute-start.9) | collective-permute-done | bytes 65568 | tf_op jit(solution)/shard_map/ppermute | solution.py:244
  10.2 0.0 collective-permute-start.13
  10.2 2.4 %collective-permute-done.10.refs_3_ = bf16[128,256]{1,0:T(8,128)(2,1)S(1)} collective-permute-done((bf16[128,256]{1,0:T(8,128)(2,1)}, bf16[128,256]{1,0:T(8,128)(2,1)S(1)}, u32[]{:S(2)}, u32[]{:S(2)}) %collective-permute-start.10) | collective-permute-done | bytes 65568 | tf_op jit(solution)/shard_map/ppermute | solution.py:244
  12.6 0.0 collective-permute-start.14
  12.6 3.9 %prepare.1 = (bf16[128,256]{1,0:T(8,128)(2,1)}, bf16[1024,128]{1,0:T(8,128)(2,1)}, bf16[1024,128]{1,0:T(8,128)(2,1)}, bf16[1024,128]{1,0:T(8,128)(2,1)}, f32[1024,128]{1,0:T(8,128)}) custom-call(s32[1]{0:T(128)} %bitcast.me_ref, s32[8]{0:T(128)} %counts_ref.1, bf16[128,1024]{1,0:T(8,128)(2,1)} %bitcast.24, bf16[128,1024]{1,0:T(8,128)(2,1)} %bitcast.16, ...), custom_call_target="tpu_custom_call" | custom-call | tf_op jit(solution)/shard_map/prepare/pallas_call | solution.py:238
  16.6 0.0 copy-done.9
  16.6 0.0 collective-permute-done.11.refs_4_
  16.6 0.0 collective-permute-done.12.refs_5_
  16.6 0.0 collective-permute-done.13.refs_6_
  16.6 0.0 copy-start.16
  16.7 0.0 collective-permute-done.14.refs_7_
  16.7 0.5 copy-done.10
  17.2 0.0 copy-done.13
  17.2 0.0 copy-done.16
  17.3 0.0 copy-done.18
  17.3 6.7 %attend_backward.1 = (bf16[128,256]{1,0:T(8,128)(2,1)}, bf16[128,256]{1,0:T(8,128)(2,1)}, bf16[128,256]{1,0:T(8,128)(2,1)}, bf16[128,256]{1,0:T(8,128)(2,1)}, bf...) custom-call(bf16[128,256]{1,0:T(8,128)(2,1)} %project_kv.1.refs_0_, bf16[128,256]{1,0:T(8,128)(2,1)} %copy-done.6, ...), custom_call_target="tpu_custom_call" | custom-call | tf_op jit(solution)/shard_map/attend_backward/pallas_call | solution.py:238
  24.0 0.5 collective-permute-start.15
  24.5 0.5 collective-permute-start
  25.0 0.4 collective-permute-start.1
  25.4 2.6 %collective-permute-start.2 = (bf16[128,256]{1,0:T(8,128)(2,1)S(1)}, bf16[128,256]{1,0:T(8,128)(2,1)S(1)}, u32[]{:S(2)}, u32[]{:S(2)}) collective-permute-start(bf16[128,256]{1,0:T(8,128)(2,1)S(1)} %copy-done.1), channel_id=1, source_target_pairs={{0,6},{1,7},{2,4},{3,5},{4,2},{5,3},{6,0},{7,1},{8,14},{9,15},{10,... | collective-permute-start | bytes 196616 | tf_op jit(solution)/shard_map/ppermute | solution.py:244
  27.9 0.0 collective-permute-start.3
  27.9 0.9 %collective-permute-done.refs_1_ = bf16[128,256]{1,0:T(8,128)(2,1)S(1)} collective-permute-done((bf16[128,256]{1,0:T(8,128)(2,1)S(1)}, bf16[128,256]{1,0:T(8,128)(2,1)S(1)}, u32[]{:S(2)}, u32[]{:S(2)}) %collective-permute-start) | collective-permute-done | bytes 65568 | tf_op jit(solution)/shard_map/ppermute | solution.py:244
  28.9 0.0 collective-permute-start.4
  28.9 1.8 %collective-permute-done.1.refs_2_ = bf16[128,256]{1,0:T(8,128)(2,1)S(1)} collective-permute-done((bf16[128,256]{1,0:T(8,128)(2,1)S(1)}, bf16[128,256]{1,0:T(8,128)(2,1)S(1)}, u32[]{:S(2)}, u32[]{:S(2)}) %collective-permute-start.1) | collective-permute-done | bytes 65568 | tf_op jit(solution)/shard_map/ppermute | solution.py:244
  30.7 0.0 collective-permute-start.5
  30.7 0.0 collective-permute-done.2.refs_3_
  30.7 0.5 collective-permute-start.6
  31.2 0.0 collective-permute-done.15.refs_4_
  31.2 0.7 %copy-done = bf16[4,128,256]{2,1,0:T(8,128)(2,1)} copy-done((bf16[4,128,256]{2,1,0:T(8,128)(2,1)}, bf16[4,128,256]{2,1,0:T(8,128)(2,1)S(1)}, u32[]{:S(2)}) %copy-start) | copy-done | bytes 262168
  31.9 1.8 %add_pieces.1 = (bf16[128,256]{1,0:T(8,128)(2,1)}, bf16[128,256]{1,0:T(8,128)(2,1)}, bf16[128,256]{1,0:T(8,128)(2,1)}, bf16[128,256]{1,0:T(8,128)(2,1)}) custom-call(bf16[128,256]{1,0:T(8,128)(2,1)} %get-tuple-element.22.refs_0_, bf16[128,256]{1,0:T(8,128)(2,1)} %get-tuple-element.23.refs_1_, bf16[128,256]{1,0:T(8,128)(2,1)} %get-tuple-element.24.refs_2_, ...), custom_call_target="tpu_custom_call" | custom-call | tf_op jit(solution)/shard_map/add_pieces/pallas_call | solution.py:238
  33.7 1.1 %collective-permute-start.16 = (bf16[128,256]{1,0:T(8,128)(2,1)}, bf16[128,256]{1,0:T(8,128)(2,1)S(1)}, u32[]{:S(2)}, u32[]{:S(2)}) collective-permute-start(bf16[128,256]{1,0:T(8,128)(2,1)} %get-tuple-element.28), channel_id=1, source_target_pairs={{0,2},{1,3},{2,0},{3,1},{4,6},{5,7},{6,4},{7,5},{8,10},{9,11},{10,... | collective-permute-start | bytes 196616 | tf_op jit(solution)/shard_map/ppermute | solution.py:244
  34.8 0.0 collective-permute-done.3.refs_4_
  34.8 1.5 %collective-permute-start.17 = (bf16[128,256]{1,0:T(8,128)(2,1)}, bf16[128,256]{1,0:T(8,128)(2,1)S(1)}, u32[]{:S(2)}, u32[]{:S(2)}) collective-permute-start(bf16[128,256]{1,0:T(8,128)(2,1)} %get-tuple-element.29), channel_id=1, source_target_pairs={{0,4},{1,5},{2,6},{3,7},{4,0},{5,1},{6,2},{7,3},{8,12},{9,13},{10,... | collective-permute-start | bytes 196616 | tf_op jit(solution)/shard_map/ppermute | solution.py:244
  36.3 0.0 collective-permute-done.4.refs_5_
  36.3 1.0 %collective-permute-start.18 = (bf16[128,256]{1,0:T(8,128)(2,1)}, bf16[128,256]{1,0:T(8,128)(2,1)S(1)}, u32[]{:S(2)}, u32[]{:S(2)}) collective-permute-start(bf16[128,256]{1,0:T(8,128)(2,1)} %get-tuple-element.30), channel_id=1, source_target_pairs={{0,6},{1,7},{2,4},{3,5},{4,2},{5,3},{6,0},{7,1},{8,14},{9,15},{10,... | collective-permute-start | bytes 196616 | tf_op jit(solution)/shard_map/ppermute | solution.py:244
  37.3 0.0 collective-permute-done.5.refs_6_
  37.3 0.0 collective-permute-done.6.refs_7_
  37.3 0.0 copy-start.14
  37.3 0.0 copy-done.5
  37.3 0.0 copy-done.8
  37.3 0.6 copy-done.11
  37.9 0.0 copy-done.14
  37.9 5.1 %attend_forward.1 = bf16[128,1024]{1,0:T(8,128)(2,1)} custom-call(bf16[128,256]{1,0:T(8,128)(2,1)} %get-tuple-element.17.refs_0_, bf16[128,256]{1,0:T(8,128)(2,1)} %copy-done.2, bf16[128,256]{1,0:T(8,128)(2,1)} %copy-done.3, bf16[128,256]{1,0:T(8,128)(2,1)} %copy-done.4, bf16[128,256]{1,0:T(8,128)(2,1)} %copy-done.5, bf16[128,256]{1,0:T(8,128)(2,1)} %copy-done.8, ...), custom_call_target="tpu_custom_call" | custom-call | tf_op jit(solution)/shard_map/attend_forward/pallas_call | solution.py:238
  43.1 1.1 %collective-permute-start.7 = (bf16[128,1024]{1,0:T(8,128)(2,1)}, bf16[128,1024]{1,0:T(8,128)(2,1)S(1)}, u32[]{:S(2)}, u32[]{:S(2)}) collective-permute-start(bf16[128,1024]{1,0:T(8,128)(2,1)} %attend_forward.1), channel_id=1, source_target_pairs={{24,0},{0,8},{8,16},{16,24},{25,1},{1,9},{9,17},{17,25},{26,2},{2,... | collective-permute-start | bytes 786440 | tf_op jit(solution)/shard_map/ppermute | solution.py:335
  44.1 2.6 %query_back.1.refs_4_ = f32[128,1024]{1,0:T(8,128)} custom-call(bf16[128,512]{1,0:T(8,128)(2,1)} %get-tuple-element.31.dq_ref, bf16[1024,512]{1,0:T(8,128)(2,1)} %bitcast.12), custom_call_target="tpu_custom_call" | custom-call | tf_op jit(solution)/shard_map/query_back/pallas_call | solution.py:238
  46.7 0.0 collective-permute-done.16.refs_1_
  46.7 0.0 collective-permute-done.17.refs_2_
  46.7 0.0 collective-permute-done.18.refs_3_
  46.7 0.6 copy-done.12
  47.3 0.0 copy-done.15
  47.4 0.0 copy-done.17
  47.4 2.6 %input_back.1 = bf16[128,1024]{1,0:T(8,128)(2,1)} custom-call(bf16[128,256]{1,0:T(8,128)(2,1)} %get-tuple-element.27.refs_0_, bf16[128,256]{1,0:T(8,128)(2,1)} %copy-done.12, bf16[128,256]{1,0:T(8,128)(2,1)} %copy-done.15, bf16[128,256]{1,0:T(8,128)(2,1)} %copy-done.17, f32[128,1024]{1,0:T(8,128)} %query_back.1.refs_4_, bf16[128,1024]{1,0:T(8,128)(2,1)} %bitcast.17, ...), custom_call_target="tpu_custom_call" | custom-call | tf_op jit(solution)/shard_map/input_back/pallas_call | solution.py:238
  50.0 2.7 %collective-permute-start.19 = (bf16[128,1024]{1,0:T(8,128)(2,1)}, bf16[128,1024]{1,0:T(8,128)(2,1)S(1)}, u32[]{:S(2)}, u32[]{:S(2)}) collective-permute-start(bf16[128,1024]{1,0:T(8,128)(2,1)} %input_back.1), channel_id=1, source_target_pairs={{8,0},{16,8},{24,16},{0,24},{9,1},{17,9},{25,17},{1,25},{10,2},{18... | collective-permute-start | bytes 786440 | tf_op jit(solution)/shard_map/ppermute | solution.py:343
  52.8 0.0 collective-permute-done.7
  52.8 5.4 %collective-permute-done.19 = bf16[128,1024]{1,0:T(8,128)(2,1)S(1)} collective-permute-done((bf16[128,1024]{1,0:T(8,128)(2,1)}, bf16[128,1024]{1,0:T(8,128)(2,1)S(1)}, u32[]{:S(2)}, u32[]{:S(2)}) %collective-permute-start.19) | collective-permute-done | bytes 262176 | tf_op jit(solution)/shard_map/ppermute | solution.py:343
  58.1 0.7 %copy.14 = bf16[1,128,1024]{2,1,0:T(8,128)(2,1)} copy(bf16[1,128,1024]{2,1,0:T(8,128)(2,1)S(1)} %bitcast.28) | data formatting | bytes 524288
  58.8 0.7 %copy.15 = bf16[1,128,1024]{2,1,0:T(8,128)(2,1)} copy(bf16[1,128,1024]{2,1,0:T(8,128)(2,1)S(1)} %bitcast.29) | data formatting | bytes 524288
  (23 shorter events, 0.0 us)
Async XLA Ops:
  2.8 5.6 %collective-permute-start.8 = (bf16[128,256]{1,0:T(8,128)(2,1)}, bf16[128,256]{1,0:T(8,128)(2,1)S(1)}, u32[]{:S(2)}, u32[]{:S(2)}) collective-permute-start(bf16[128,256]{1,0:T(8,128)(2,1)} %project_kv.1.refs_0_), channel_id=1, source_target_pairs={{0,2},{1,3},{2,0},{3,1},{4,6},{5,7},{6,4},{7,5},{8,10},{9,11},{10,... | collective-permute-start | bytes 196616 | tf_op jit(solution)/shard_map/ppermute | solution.py:244
  5.7 4.5 %collective-permute-start.9 = (bf16[128,256]{1,0:T(8,128)(2,1)}, bf16[128,256]{1,0:T(8,128)(2,1)S(1)}, u32[]{:S(2)}, u32[]{:S(2)}) collective-permute-start(bf16[128,256]{1,0:T(8,128)(2,1)} %project_kv.1.refs_0_), channel_id=1, source_target_pairs={{0,4},{1,5},{2,6},{3,7},{4,0},{5,1},{6,2},{7,3},{8,12},{9,13},{10,... | collective-permute-start | bytes 196616 | tf_op jit(solution)/shard_map/ppermute | solution.py:244
  7.3 5.4 %collective-permute-start.10 = (bf16[128,256]{1,0:T(8,128)(2,1)}, bf16[128,256]{1,0:T(8,128)(2,1)S(1)}, u32[]{:S(2)}, u32[]{:S(2)}) collective-permute-start(bf16[128,256]{1,0:T(8,128)(2,1)} %project_kv.1.refs_0_), channel_id=1, source_target_pairs={{0,6},{1,7},{2,4},{3,5},{4,2},{5,3},{6,0},{7,1},{8,14},{9,15},{10,... | collective-permute-start | bytes 196616 | tf_op jit(solution)/shard_map/ppermute | solution.py:244
  7.3 9.3 %collective-permute-start.11 = (bf16[128,256]{1,0:T(8,128)(2,1)}, bf16[128,256]{1,0:T(8,128)(2,1)S(1)}, u32[]{:S(2)}, u32[]{:S(2)}) collective-permute-start(bf16[128,256]{1,0:T(8,128)(2,1)} %project_kv.1.refs_0_), channel_id=1, source_target_pairs={{0,1},{1,0},{2,3},{3,2},{4,5},{5,4},{6,7},{7,6},{8,9},{9,8},{10,11... | collective-permute-start | bytes 196616 | tf_op jit(solution)/shard_map/ppermute | solution.py:244
  8.4 8.2 %copy-start.6 = (bf16[128,256]{1,0:T(8,128)(2,1)}, bf16[128,256]{1,0:T(8,128)(2,1)S(1)}, u32[]{:S(2)}) copy-start(bf16[128,256]{1,0:T(8,128)(2,1)S(1)} %collective-permute-done.8.refs_1_) | copy-start | bytes 196612
  8.4 8.2 %collective-permute-start.12 = (bf16[128,256]{1,0:T(8,128)(2,1)S(1)}, bf16[128,256]{1,0:T(8,128)(2,1)S(1)}, u32[]{:S(2)}, u32[]{:S(2)}) collective-permute-start(bf16[128,256]{1,0:T(8,128)(2,1)S(1)} %collective-permute-done.8.refs_1_), channel_id=1, source_target_pairs={{0,1},{1,0},{2,3},{3,2},{4,5},{5,4},{6,7},{7,6},{8,9},{9,8},{10,11... | collective-permute-start | bytes 196616 | tf_op jit(solution)/shard_map/ppermute | solution.py:244
  10.2 6.4 %copy-start.7 = (bf16[128,256]{1,0:T(8,128)(2,1)}, bf16[128,256]{1,0:T(8,128)(2,1)S(1)}, u32[]{:S(2)}) copy-start(bf16[128,256]{1,0:T(8,128)(2,1)S(1)} %collective-permute-done.9.refs_2_) | copy-start | bytes 196612
  10.2 6.4 %collective-permute-start.13 = (bf16[128,256]{1,0:T(8,128)(2,1)S(1)}, bf16[128,256]{1,0:T(8,128)(2,1)S(1)}, u32[]{:S(2)}, u32[]{:S(2)}) collective-permute-start(bf16[128,256]{1,0:T(8,128)(2,1)S(1)} %collective-permute-done.9.refs_2_), channel_id=1, source_target_pairs={{0,1},{1,0},{2,3},{3,2},{4,5},{5,4},{6,7},{7,6},{8,9},{9,8},{10,11... | collective-permute-start | bytes 196616 | tf_op jit(solution)/shard_map/ppermute | solution.py:244
  12.6 4.0 %copy-start.9 = (bf16[128,256]{1,0:T(8,128)(2,1)}, bf16[128,256]{1,0:T(8,128)(2,1)S(1)}, u32[]{:S(2)}) copy-start(bf16[128,256]{1,0:T(8,128)(2,1)S(1)} %collective-permute-done.10.refs_3_) | copy-start | bytes 196612
  12.6 4.0 %collective-permute-start.14 = (bf16[128,256]{1,0:T(8,128)(2,1)S(1)}, bf16[128,256]{1,0:T(8,128)(2,1)S(1)}, u32[]{:S(2)}, u32[]{:S(2)}) collective-permute-start(bf16[128,256]{1,0:T(8,128)(2,1)S(1)} %collective-permute-done.10.refs_3_), channel_id=1, source_target_pairs={{0,1},{1,0},{2,3},{3,2},{4,5},{5,4},{6,7},{7,6},{8,9},{9,8},{10,11... | collective-permute-start | bytes 196616 | tf_op jit(solution)/shard_map/ppermute | solution.py:244
  16.6 0.6 %copy-start.10 = (bf16[128,256]{1,0:T(8,128)(2,1)}, bf16[128,256]{1,0:T(8,128)(2,1)S(1)}, u32[]{:S(2)}) copy-start(bf16[128,256]{1,0:T(8,128)(2,1)S(1)} %collective-permute-done.11.refs_4_) | copy-start | bytes 196612
  16.6 0.6 %copy-start.13 = (bf16[128,256]{1,0:T(8,128)(2,1)}, bf16[128,256]{1,0:T(8,128)(2,1)S(1)}, u32[]{:S(2)}) copy-start(bf16[128,256]{1,0:T(8,128)(2,1)S(1)} %collective-permute-done.12.refs_5_) | copy-start | bytes 196612
  16.6 0.6 %copy-start.16 = (bf16[128,256]{1,0:T(8,128)(2,1)}, bf16[128,256]{1,0:T(8,128)(2,1)S(1)}, u32[]{:S(2)}) copy-start(bf16[128,256]{1,0:T(8,128)(2,1)S(1)} %collective-permute-done.13.refs_6_) | copy-start | bytes 196612
  16.7 0.6 %copy-start.18 = (bf16[128,256]{1,0:T(8,128)(2,1)}, bf16[128,256]{1,0:T(8,128)(2,1)S(1)}, u32[]{:S(2)}) copy-start(bf16[128,256]{1,0:T(8,128)(2,1)S(1)} %collective-permute-done.14.refs_7_) | copy-start | bytes 196612
  17.3 7.2 %copy-start.1 = (bf16[128,256]{1,0:T(8,128)(2,1)S(1)}, bf16[128,256]{1,0:T(8,128)(2,1)}, u32[]{:S(2)}) copy-start(bf16[128,256]{1,0:T(8,128)(2,1)} %get-tuple-element.17.refs_0_) | copy-start | bytes 196612
  24.0 7.2 %collective-permute-start.15 = (bf16[4,128,256]{2,1,0:T(8,128)(2,1)}, bf16[4,128,256]{2,1,0:T(8,128)(2,1)S(1)}, u32[]{:S(2)}, u32[]{:S(2)}) collective-permute-start(bf16[4,128,256]{2,1,0:T(8,128)(2,1)} %get-tuple-element.26), channel_id=1, source_target_pairs={{0,1},{1,0},{2,3},{3,2},{4,5},{5,4},{6,7},{7,6},{8,9},{9,8},{10,11... | collective-permute-start | bytes 786440 | tf_op jit(solution)/shard_map/ppermute | solution.py:244
  24.5 4.4 %collective-permute-start = (bf16[128,256]{1,0:T(8,128)(2,1)S(1)}, bf16[128,256]{1,0:T(8,128)(2,1)S(1)}, u32[]{:S(2)}, u32[]{:S(2)}) collective-permute-start(bf16[128,256]{1,0:T(8,128)(2,1)S(1)} %copy-done.1), channel_id=1, source_target_pairs={{0,2},{1,3},{2,0},{3,1},{4,6},{5,7},{6,4},{7,5},{8,10},{9,11},{10,... | collective-permute-start | bytes 196616 | tf_op jit(solution)/shard_map/ppermute | solution.py:244
  25.0 5.7 %collective-permute-start.1 = (bf16[128,256]{1,0:T(8,128)(2,1)S(1)}, bf16[128,256]{1,0:T(8,128)(2,1)S(1)}, u32[]{:S(2)}, u32[]{:S(2)}) collective-permute-start(bf16[128,256]{1,0:T(8,128)(2,1)S(1)} %copy-done.1), channel_id=1, source_target_pairs={{0,4},{1,5},{2,6},{3,7},{4,0},{5,1},{6,2},{7,3},{8,12},{9,13},{10,... | collective-permute-start | bytes 196616 | tf_op jit(solution)/shard_map/ppermute | solution.py:244
  25.4 5.3 %collective-permute-start.2 = (bf16[128,256]{1,0:T(8,128)(2,1)S(1)}, bf16[128,256]{1,0:T(8,128)(2,1)S(1)}, u32[]{:S(2)}, u32[]{:S(2)}) collective-permute-start(bf16[128,256]{1,0:T(8,128)(2,1)S(1)} %copy-done.1), channel_id=1, source_target_pairs={{0,6},{1,7},{2,4},{3,5},{4,2},{5,3},{6,0},{7,1},{8,14},{9,15},{10,... | collective-permute-start | bytes 196616 | tf_op jit(solution)/shard_map/ppermute | solution.py:244
  27.9 6.8 %collective-permute-start.3 = (bf16[128,256]{1,0:T(8,128)(2,1)S(1)}, bf16[128,256]{1,0:T(8,128)(2,1)S(1)}, u32[]{:S(2)}, u32[]{:S(2)}) collective-permute-start(bf16[128,256]{1,0:T(8,128)(2,1)S(1)} %copy-done.1), channel_id=1, source_target_pairs={{0,1},{1,0},{2,3},{3,2},{4,5},{5,4},{6,7},{7,6},{8,9},{9,8},{10,11... | collective-permute-start | bytes 196616 | tf_op jit(solution)/shard_map/ppermute | solution.py:244
  28.9 4.8 %copy-start.2 = (bf16[128,256]{1,0:T(8,128)(2,1)}, bf16[128,256]{1,0:T(8,128)(2,1)S(1)}, u32[]{:S(2)}) copy-start(bf16[128,256]{1,0:T(8,128)(2,1)S(1)} %collective-permute-done.refs_1_) | copy-start | bytes 196612
  28.9 7.4 %collective-permute-start.4 = (bf16[128,256]{1,0:T(8,128)(2,1)S(1)}, bf16[128,256]{1,0:T(8,128)(2,1)S(1)}, u32[]{:S(2)}, u32[]{:S(2)}) collective-permute-start(bf16[128,256]{1,0:T(8,128)(2,1)S(1)} %collective-permute-done.refs_1_), channel_id=1, source_target_pairs={{0,1},{1,0},{2,3},{3,2},{4,5},{5,4},{6,7},{7,6},{8,9},{9,8},{10,11... | collective-permute-start | bytes 196616 | tf_op jit(solution)/shard_map/ppermute | solution.py:244
  30.7 3.1 %copy-start.3 = (bf16[128,256]{1,0:T(8,128)(2,1)}, bf16[128,256]{1,0:T(8,128)(2,1)S(1)}, u32[]{:S(2)}) copy-start(bf16[128,256]{1,0:T(8,128)(2,1)S(1)} %collective-permute-done.1.refs_2_) | copy-start | bytes 196612
  30.7 6.6 %collective-permute-start.5 = (bf16[128,256]{1,0:T(8,128)(2,1)S(1)}, bf16[128,256]{1,0:T(8,128)(2,1)S(1)}, u32[]{:S(2)}, u32[]{:S(2)}) collective-permute-start(bf16[128,256]{1,0:T(8,128)(2,1)S(1)} %collective-permute-done.1.refs_2_), channel_id=1, source_target_pairs={{0,1},{1,0},{2,3},{3,2},{4,5},{5,4},{6,7},{7,6},{8,9},{9,8},{10,11... | collective-permute-start | bytes 196616 | tf_op jit(solution)/shard_map/ppermute | solution.py:244
  30.7 3.0 %copy-start.4 = (bf16[128,256]{1,0:T(8,128)(2,1)}, bf16[128,256]{1,0:T(8,128)(2,1)S(1)}, u32[]{:S(2)}) copy-start(bf16[128,256]{1,0:T(8,128)(2,1)S(1)} %collective-permute-done.2.refs_3_) | copy-start | bytes 196612
  30.7 6.6 %collective-permute-start.6 = (bf16[128,256]{1,0:T(8,128)(2,1)S(1)}, bf16[128,256]{1,0:T(8,128)(2,1)S(1)}, u32[]{:S(2)}, u32[]{:S(2)}) collective-permute-start(bf16[128,256]{1,0:T(8,128)(2,1)S(1)} %collective-permute-done.2.refs_3_), channel_id=1, source_target_pairs={{0,1},{1,0},{2,3},{3,2},{4,5},{5,4},{6,7},{7,6},{8,9},{9,8},{10,11... | collective-permute-start | bytes 196616 | tf_op jit(solution)/shard_map/ppermute | solution.py:244
  31.2 0.7 %copy-start = (bf16[4,128,256]{2,1,0:T(8,128)(2,1)}, bf16[4,128,256]{2,1,0:T(8,128)(2,1)S(1)}, u32[]{:S(2)}) copy-start(bf16[4,128,256]{2,1,0:T(8,128)(2,1)S(1)} %collective-permute-done.15.refs_4_) | copy-start | bytes 786436
  33.7 13.0 %collective-permute-start.16 = (bf16[128,256]{1,0:T(8,128)(2,1)}, bf16[128,256]{1,0:T(8,128)(2,1)S(1)}, u32[]{:S(2)}, u32[]{:S(2)}) collective-permute-start(bf16[128,256]{1,0:T(8,128)(2,1)} %get-tuple-element.28), channel_id=1, source_target_pairs={{0,2},{1,3},{2,0},{3,1},{4,6},{5,7},{6,4},{7,5},{8,10},{9,11},{10,... | collective-permute-start | bytes 196616 | tf_op jit(solution)/shard_map/ppermute | solution.py:244
  34.8 2.5 %copy-start.5 = (bf16[128,256]{1,0:T(8,128)(2,1)}, bf16[128,256]{1,0:T(8,128)(2,1)S(1)}, u32[]{:S(2)}) copy-start(bf16[128,256]{1,0:T(8,128)(2,1)S(1)} %collective-permute-done.3.refs_4_) | copy-start | bytes 196612
  34.8 11.9 %collective-permute-start.17 = (bf16[128,256]{1,0:T(8,128)(2,1)}, bf16[128,256]{1,0:T(8,128)(2,1)S(1)}, u32[]{:S(2)}, u32[]{:S(2)}) collective-permute-start(bf16[128,256]{1,0:T(8,128)(2,1)} %get-tuple-element.29), channel_id=1, source_target_pairs={{0,4},{1,5},{2,6},{3,7},{4,0},{5,1},{6,2},{7,3},{8,12},{9,13},{10,... | collective-permute-start | bytes 196616 | tf_op jit(solution)/shard_map/ppermute | solution.py:244
  36.3 1.0 %copy-start.8 = (bf16[128,256]{1,0:T(8,128)(2,1)}, bf16[128,256]{1,0:T(8,128)(2,1)S(1)}, u32[]{:S(2)}) copy-start(bf16[128,256]{1,0:T(8,128)(2,1)S(1)} %collective-permute-done.4.refs_5_) | copy-start | bytes 196612
  36.3 10.4 %collective-permute-start.18 = (bf16[128,256]{1,0:T(8,128)(2,1)}, bf16[128,256]{1,0:T(8,128)(2,1)S(1)}, u32[]{:S(2)}, u32[]{:S(2)}) collective-permute-start(bf16[128,256]{1,0:T(8,128)(2,1)} %get-tuple-element.30), channel_id=1, source_target_pairs={{0,6},{1,7},{2,4},{3,5},{4,2},{5,3},{6,0},{7,1},{8,14},{9,15},{10,... | collective-permute-start | bytes 196616 | tf_op jit(solution)/shard_map/ppermute | solution.py:244
  37.3 0.6 %copy-start.11 = (bf16[128,256]{1,0:T(8,128)(2,1)}, bf16[128,256]{1,0:T(8,128)(2,1)S(1)}, u32[]{:S(2)}) copy-start(bf16[128,256]{1,0:T(8,128)(2,1)S(1)} %collective-permute-done.5.refs_6_) | copy-start | bytes 196612
  37.3 0.6 %copy-start.14 = (bf16[128,256]{1,0:T(8,128)(2,1)}, bf16[128,256]{1,0:T(8,128)(2,1)S(1)}, u32[]{:S(2)}) copy-start(bf16[128,256]{1,0:T(8,128)(2,1)S(1)} %collective-permute-done.6.refs_7_) | copy-start | bytes 196612
  43.1 9.7 %collective-permute-start.7 = (bf16[128,1024]{1,0:T(8,128)(2,1)}, bf16[128,1024]{1,0:T(8,128)(2,1)S(1)}, u32[]{:S(2)}, u32[]{:S(2)}) collective-permute-start(bf16[128,1024]{1,0:T(8,128)(2,1)} %attend_forward.1), channel_id=1, source_target_pairs={{24,0},{0,8},{8,16},{16,24},{25,1},{1,9},{9,17},{17,25},{26,2},{2,... | collective-permute-start | bytes 786440 | tf_op jit(solution)/shard_map/ppermute | solution.py:335
  46.7 0.6 %copy-start.12 = (bf16[128,256]{1,0:T(8,128)(2,1)}, bf16[128,256]{1,0:T(8,128)(2,1)S(1)}, u32[]{:S(2)}) copy-start(bf16[128,256]{1,0:T(8,128)(2,1)S(1)} %collective-permute-done.16.refs_1_) | copy-start | bytes 196612
  46.7 0.6 %copy-start.15 = (bf16[128,256]{1,0:T(8,128)(2,1)}, bf16[128,256]{1,0:T(8,128)(2,1)S(1)}, u32[]{:S(2)}) copy-start(bf16[128,256]{1,0:T(8,128)(2,1)S(1)} %collective-permute-done.17.refs_2_) | copy-start | bytes 196612
  46.7 0.6 %copy-start.17 = (bf16[128,256]{1,0:T(8,128)(2,1)}, bf16[128,256]{1,0:T(8,128)(2,1)S(1)}, u32[]{:S(2)}) copy-start(bf16[128,256]{1,0:T(8,128)(2,1)S(1)} %collective-permute-done.18.refs_3_) | copy-start | bytes 196612
  50.0 8.1 %collective-permute-start.19 = (bf16[128,1024]{1,0:T(8,128)(2,1)}, bf16[128,1024]{1,0:T(8,128)(2,1)S(1)}, u32[]{:S(2)}, u32[]{:S(2)}) collective-permute-start(bf16[128,1024]{1,0:T(8,128)(2,1)} %input_back.1), channel_id=1, source_target_pairs={{8,0},{16,8},{24,16},{0,24},{9,1},{17,9},{25,17},{1,25},{10,2},{18... | collective-permute-start | bytes 786440 | tf_op jit(solution)/shard_map/ppermute | solution.py:343

commit v2 on v1

--- a/solution.py
+++ b/solution.py
@@ -8,6 +8,7 @@
 from jax.experimental.pallas import tpu as pltpu
 from jax.sharding import PartitionSpec as P
 
+
 HEADS = 8
 KV_HEADS = 2
 HEAD_DIM = 64
@@ -17,6 +18,7 @@
 
 NORM_EPSILON = 1e-05
 MASKED_SCORE = -1e30
+
 F32 = jnp.float32
 BF16 = jnp.bfloat16
 
@@ -42,10 +44,28 @@
     return (widened * inverse * gain).astype(BF16), inverse, widened
 
 
-def project_kv(x_ref, gain_ref, wk_ref, wv_ref, kv_ref):
-    normed, _, _ = rms(x_ref[...], gain_ref[...])
-    kv_ref[:, :KV_COLS] = dot(normed, wk_ref[...]).astype(BF16)
-    kv_ref[:, KV_COLS:] = dot(normed, wv_ref[...]).astype(BF16)
+def project_kv(gain_ref, xf_hbm, xb_hbm, wk_hbm, wv_hbm, kv_ref, xf_ref, xb_ref, wk_ref, wv_ref, sems):
+    copies = [
+        pltpu.make_async_copy(source, target, sems.at[place])
+        for place, (source, target) in enumerate(
+            ((xf_hbm, xf_ref), (wk_hbm, wk_ref), (wv_hbm, wv_ref), (xb_hbm, xb_ref))
+        )
+    ]
+    for copy in copies:
+        copy.start()
+    gain = gain_ref[...]
+    rows = xf_ref.shape[0]
+    copies[0].wait()
+    normed_f, _, _ = rms(xf_ref[...], gain)
+    copies[3].wait()
+    normed_b, _, _ = rms(xb_ref[...], gain)
+    normed = jnp.concatenate([normed_f, normed_b], axis=0)
+    copies[1].wait()
+    copies[2].wait()
+    for place, weight_ref in enumerate((wk_ref, wv_ref)):
+        both = dot(normed, weight_ref[...]).astype(BF16)
+        kv_ref[:, place * KV_COLS : (place + 1) * KV_COLS] = both[:rows]
+        kv_ref[:, (2 + place) * KV_COLS : (3 + place) * KV_COLS] = both[rows:]
 
 
 def spread_heads(flat, out_ref, scale):
@@ -68,29 +88,28 @@
     counts_ref,
     xf_ref,
     xb_ref,
-    cot_ref,
     gain_ref,
-    wq_ref,
-    wk_ref,
-    wv_ref,
-    wo_ref,
     frames_ref,
-    kvf_ref,
+    cot_hbm,
+    wq_hbm,
+    wo_hbm,
     qf_ref,
     qb_ref,
     dout_ref,
     bias_ref,
+    cot_ref,
+    wq_ref,
+    wo_ref,
+    sems,
 ):
+    copies = [
+        pltpu.make_async_copy(source, target, sems.at[place])
+        for place, (source, target) in enumerate(((wq_hbm, wq_ref), (cot_hbm, cot_ref), (wo_hbm, wo_ref)))
+    ]
+    for copy in copies:
+        copy.start()
     gain = gain_ref[...]
     rows = xf_ref.shape[0]
-    normed_f, _, _ = rms(xf_ref[...], gain)
-    kvf_ref[:, :KV_COLS] = dot(normed_f, wk_ref[...]).astype(BF16)
-    kvf_ref[:, KV_COLS:] = dot(normed_f, wv_ref[...]).astype(BF16)
-    scale = 1.0 / math.sqrt(HEAD_DIM)
-    spread_heads(dot(normed_f, wq_ref[...]), qf_ref, scale)
-    normed_b, _, _ = rms(xb_ref[...], gain)
-    spread_heads(dot(normed_b, wq_ref[...]), qb_ref, scale)
-    spread_heads(dot(cot_ref[...], wo_ref[...], NT), dout_ref, 1.0)
     me = me_ref[0]
     row = lax.broadcasted_iota(jnp.int32, (rows, rows), 0)
     query_frames = jnp.broadcast_to(frames_ref[pl.ds(me, 1), :], (rows, rows))
@@ -100,6 +119,16 @@
         key_frames = jnp.transpose(own.astype(F32)).astype(jnp.int32)
         visible = (key_frames <= query_frames) & (row < counts_ref[source])
         bias_ref[place * rows : (place + 1) * rows, :] = jnp.where(visible, 0.0, MASKED_SCORE)
+    normed_f, _, _ = rms(xf_ref[...], gain)
+    normed_b, _, _ = rms(xb_ref[...], gain)
+    scale = 1.0 / math.sqrt(HEAD_DIM)
+    copies[0].wait()
+    queries = dot(jnp.concatenate([normed_f, normed_b], axis=0), wq_ref[...])
+    spread_heads(queries[:rows], qf_ref, scale)
+    spread_heads(queries[rows:], qb_ref, scale)
+    copies[1].wait()
+    copies[2].wait()
+    spread_heads(dot(cot_ref[...], wo_ref[...], NT), dout_ref, 1.0)
 
 
 def scores_of(keys_ref, q_rows, bias_ref, s_ref, chunk):
@@ -125,7 +154,7 @@
     total = rows * count
     chunk = 2 * rows
     for place, piece in enumerate(pieces):
-        kv_ref[place * rows : (place + 1) * rows, :] = piece[...]
+        kv_ref[place * rows : (place + 1) * rows, :] = piece[:, 2 * KV_COLS :]
     keys_t = jnp.transpose(kv_ref[:, :KV_COLS])
     scale = 1.0 / math.sqrt(HEAD_DIM)
     wide = 2 * rows
@@ -185,7 +214,7 @@
     total = rows * count
     chunk = 2 * rows
     for place, piece in enumerate(pieces):
-        kv_ref[place * rows : (place + 1) * rows, :] = piece[...]
+        kv_ref[place * rows : (place + 1) * rows, :] = piece[:, : 2 * KV_COLS]
     values_t = jnp.transpose(kv_ref[:, KV_COLS:])
     wide = 2 * rows
     for pair in range(PAIRS):
@@ -205,8 +234,11 @@
     out_ref[...] = (x_ref[...].astype(F32) + dot(attended, wo_ref[...])).astype(BF16)
 
 
-def query_back(dq_ref, wq_ref, out_ref):
+def query_back(dq_ref, wq_ref, next_ref, out_ref, next_hbm, sem):
+    copy = pltpu.make_async_copy(next_ref, next_hbm, sem)
+    copy.start()
     out_ref[...] = dot(dq_ref[...], wq_ref[...], NT)
+    copy.wait()
 
 
 def add_pieces(count, *refs):
@@ -232,29 +264,59 @@
     out_ref[...] = grad.astype(BF16)
 
 
-def call(kernel, outs, args, scratch=(), smem=0, name=None):
-    specs = [pl.BlockSpec(memory_space=pltpu.SMEM)] * smem + vmem(len(args) - smem)
-    out_specs = vmem(len(outs)) if isinstance(outs, (list, tuple)) else vmem(1)[0]
-    return pl.pallas_call(
-        kernel, out_shape=outs, in_specs=specs, out_specs=out_specs, scratch_shapes=list(scratch), name=name
+def local(array):
+    return pltpu.with_memory_space_constraint(array, pltpu.VMEM)
+
+
+def size_of(item):
+    return math.prod(item.shape) * jnp.dtype(item.dtype).itemsize
+
+
+def call(kernel, outs, args, scratch=(), sems=None, smem=0, hbm=0, out_hbm=0):
+    many = isinstance(outs, (list, tuple))
+    outs = list(outs) if many else [outs]
+    inside, kept = len(args) - hbm, len(outs) - out_hbm
+    args = list(args[:smem]) + [local(arg) for arg in args[smem:inside]] + [
+        pltpu.with_memory_space_constraint(arg, pltpu.HBM) for arg in args[inside:]
+    ]
+    room = sum(size_of(item) for item in scratch) + (8 << 20)
+    scratch = list(scratch) + ([] if sems is None else [pltpu.SemaphoreType.DMA(sems)])
+    results = pl.pallas_call(
+        kernel,
+        out_shape=[pltpu.VMEM(out.shape, out.dtype) for out in outs[:kept]] + outs[kept:],
+        in_specs=[pl.BlockSpec(memory_space=pltpu.SMEM)] * smem
+        + vmem(inside - smem)
+        + [pl.BlockSpec(memory_space=pltpu.HBM)] * hbm,
+        out_specs=vmem(kept) + [pl.BlockSpec(memory_space=pltpu.HBM)] * out_hbm,
+        scratch_shapes=scratch,
+        compiler_params=pltpu.CompilerParams(vmem_limit_bytes=room),
     )(*args)
+    return results if many else results[0]
 
 
 def swap(block, step, size):
     return lax.ppermute(block, "seq", [(i, i ^ step) for i in range(size)])
 
 
-def gather_pieces(block, size):
-    if size > 8 or size % 2:
-        everything = lax.all_gather(block, "seq", axis=0)
-        me = lax.axis_index("seq")
-        return [lax.dynamic_index_in_dim(everything, me ^ step, 0, False) for step in order_of(size)]
-    near = [block] + [swap(block, step, size) for step in range(2, size, 2)]
-    return near + [swap(piece, 1, size) for piece in near]
-
-
 def order_of(size):
     return list(range(0, size, 2)) + list(range(1, size, 2))
+
+
+def by_permutes(size):
+    return size in (2, 4, 8)
+
+
+def gather_near(block, size):
+    if not by_permutes(size):
+        return lax.all_gather(block, "seq", axis=0)
+    return [block] + [swap(block, step, size) for step in range(2, size, 2)]
+
+
+def gather_far(near, size):
+    if not by_permutes(size):
+        me = lax.axis_index("seq")
+        return [lax.dynamic_index_in_dim(near, me ^ step, 0, False) for step in order_of(size)]
+    return near + [swap(piece, 1, size) for piece in near]
 
 
 def on_device(
@@ -270,9 +332,9 @@
     frame_index,
     valid_counts,
 ):
-    xf, xb, cot = forward_input[0], stored_input[0], output_cotangent[0]
-    wq, wk, wv, wo = query_weight[0], key_weight[0], value_weight[0], output_weight[0]
-    rows, width = xf.shape
+    xf_hbm, xb_hbm, cot_hbm = forward_input[0], stored_input[0], output_cotangent[0]
+    wq_hbm, wk_hbm, wv_hbm, wo_hbm = query_weight[0], key_weight[0], value_weight[0], output_weight[0]
+    rows, width = xf_hbm.shape
     total = rows * size
     sections = lax.axis_size("section")
     order = order_of(size)
@@ -280,22 +342,44 @@
     kv_shape = shape((rows, 2 * KV_COLS), BF16)
     spread = shape((HEADS * rows, KV_COLS), BF16)
     wide = 2 * rows
-
-    kvb = call(project_kv, kv_shape, (xb, norm_gain, wk, wv), name="project_kv")
-    pieces_b = gather_pieces(kvb, size)
+    gain = local(norm_gain)
+    frames = frame_index.reshape(size, rows)
     me = lax.axis_index("seq").astype(jnp.int32).reshape(1)
-    kvf, qf, qb, dout, bias = call(
+
+    kv, xf, xb, wk, wv = call(
+        project_kv,
+        (shape((rows, 4 * KV_COLS), BF16),) + tuple(shape(item.shape, BF16) for item in (xf_hbm, xb_hbm, wk_hbm, wv_hbm)),
+        (gain, xf_hbm, xb_hbm, wk_hbm, wv_hbm),
+        sems=(4,),
+        hbm=4,
+    )
+    near = gather_near(kv, size)
+    qf, qb, dout, bias, cot, wq, wo = call(
         partial(prepare, order),
-        (kv_shape, spread, spread, spread, shape((total, rows), F32)),
-        (me, valid_counts, xf, xb, cot, norm_gain, wq, wk, wv, wo, frame_index.reshape(size, rows)),
+        (spread, spread, spread, shape((total, rows), F32))
+        + tuple(shape(item.shape, BF16) for item in (cot_hbm, wq_hbm, wo_hbm)),
+        (me, valid_counts, xf, xb, gain, frames, cot_hbm, wq_hbm, wo_hbm),
+        sems=(3,),
         smem=2,
-        name="prepare",
-    )
-    pieces_f = gather_pieces(kvf, size)
+        hbm=3,
+    )
+    pieces = gather_far(near, size)
+    layer_out = call(
+        partial(attend_forward, size),
+        shape((rows, width), BF16),
+        (*pieces, qf, bias, xf, wo),
+        scratch=(
+            pltpu.VMEM((total, 2 * KV_COLS), BF16),
+            pltpu.VMEM((total, wide), F32),
+            pltpu.VMEM((total, wide), BF16),
+            pltpu.VMEM((HEADS * HEAD_DIM, rows), F32),
+        ),
+    )
+    shifted = lax.ppermute(layer_out, "section", [((i - 1) % sections, i) for i in range(sections)])
     *grads, dq = call(
         partial(attend_backward, size),
         (kv_shape,) * half + (shape((half, rows, 2 * KV_COLS), BF16), shape((rows, HEADS * HEAD_DIM), BF16)),
-        (*pieces_b, qb, dout, bias),
+        (*pieces, qb, dout, bias),
         scratch=(
             pltpu.VMEM((total, 2 * KV_COLS), BF16),
             pltpu.VMEM((total, wide), F32),
@@ -307,46 +391,35 @@
             pltpu.VMEM((HEADS * rows, KV_COLS), BF16),
             pltpu.VMEM((HEADS * rows, KV_COLS), BF16),
         ),
-        name="attend_backward",
     )
     even, odd = grads[:half], grads[half]
-    if size > 8 or size % 2:
-        index = lax.axis_index("seq")
+    if by_permutes(size):
+        other = swap(odd, 1, size)
+        sums = call(partial(add_pieces, half), (kv_shape,) * half, (*even, other))
+        received = [sums[0]] + [swap(sums[i], 2 * i, size) for i in range(1, half)]
+    else:
         both = jnp.stack(list(even) + [odd[i] for i in range(half)]).astype(F32)
-        places = jnp.argsort(jnp.array(order, jnp.int32) ^ index)
+        places = jnp.argsort(jnp.array(order, jnp.int32) ^ lax.axis_index("seq"))
         summed = lax.psum_scatter(both[places], "seq", scatter_dimension=0, tiled=True)
         received = [summed[0].astype(BF16)]
-    else:
-        other = swap(odd, 1, size)
-        sums = call(partial(add_pieces, half), (kv_shape,) * half, (*even, other), name="add_pieces")
-        received = [sums[0]] + [swap(sums[i], 2 * i, size) for i in range(1, half)]
-    layer_out = call(
-        partial(attend_forward, size),
-        shape((rows, width), BF16),
-        (*pieces_f, qf, bias, xf, wo),
-        scratch=(
-            pltpu.VMEM((total, 2 * KV_COLS), BF16),
-            pltpu.VMEM((total, wide), F32),
-            pltpu.VMEM((total, wide), BF16),
-            pltpu.VMEM((HEADS * HEAD_DIM, rows), F32),
-        ),
-        name="attend_forward",
-    )
-    forward_next = lax.ppermute(layer_out, "section", [((i - 1) % sections, i) for i in range(sections)])
-    base = call(query_back, shape((rows, width), F32), (dq, wq), name="query_back")
+    base, forward_next = call(
+        query_back, (shape((rows, width), F32), shape((rows, width), BF16)), (dq, wq, shifted), sems=(), out_hbm=1
+    )
     input_grad = call(
-        partial(input_back, len(received)),
-        shape((rows, width), BF16),
-        (*received, base, xb, cot, norm_gain, wk, wv),
-        name="input_back",
+        partial(input_back, len(received)), shape((rows, width), BF16), (*received, base, xb, cot, gain, wk, wv)
     )
     backward_next = lax.ppermute(input_grad, "section", [((i + 1) % sections, i) for i in range(sections)])
     return (forward_next[None], backward_next[None])
 
 
+def placed(size, *arrays):
+    return on_device(size, *arrays)
+
+
 def solution(mesh):
+    size = mesh.shape["seq"]
     return jax.shard_map(
-        partial(on_device, mesh.shape["seq"]),
+        partial(placed, size),
         mesh=mesh,
         in_specs=(
             P("section", "seq", None),

time: 59.8 us -> 46.1 us (0.77)
  Pallas kernels: 24.9 us -> 13.4 us
  starting transfers between devices: 16.3 us -> 12.2 us
  waiting for transfers between devices: 13.5 us -> 17.4 us
  local copies, waits for them, and re-layouts: 4.03 us -> 2.07 us
    pallas_call x7, Pallas kernels: 24.9 us -> 13.4 us  [call(): pl.pallas_call(kernel, out_shape=[pltpu.VMEM(out.shape, out.dtype) for ou...]
    ppermute x1, waiting for transfers between devices: 0.01 us -> 5.33 us  [on_device(): lax.ppermute(layer_out, 'section', [((i - 1) % sections, i) for i in rang...]
    ppermute x18 -> x11, starting transfers between devices: 12.5 us -> 8.76 us  [swap(): return lax.ppermute(block, 'seq', [(i, i ^ step) for i in range(size)])]
    ppermute x18 -> x11, waiting for transfers between devices: 8.1 us -> 5.92 us  [swap(): return lax.ppermute(block, 'seq', [(i, i ^ step) for i in range(size)])]
    unnamed x40 -> x7, local copies, waits for them, and re-layouts: 4.03 us -> 2.07 us
    ppermute x1, starting transfers between devices: 2.75 us -> 1.79 us  [on_device(): lax.ppermute(input_grad, 'section', [((i + 1) % sections, i) for i in ran...]
    ppermute x1, waiting for transfers between devices: 5.36 us -> 6.13 us  [on_device(): lax.ppermute(input_grad, 'section', [((i + 1) % sections, i) for i in ran...]
  transfers between devices with their start and end apart: 20 -> 13, of which waited for: 6 -> 5; matrix products, arithmetic and copies ran while one was open for 0% -> 0% of each run, Pallas kernels for 27% -> 14%
where the time goes in v2:
time: 46.1 us; the launch traced here: 45.8 us
  waiting for transfers between devices  17.4 us (38%)
  Pallas kernels  13.4 us (29%)
  starting transfers between devices  12.2 us (26%)
  local copies, waits for them, and re-layouts  2.07 us (4%)
  between operations  0.75 us (2%)
    pallas_call x7, Pallas kernels, call(): pl.pallas_call(kernel, out_shape=[pltpu.VMEM(out.shape, out.dtype) for ou...  13.4 us
    ppermute x11, starting transfers between devices, swap(): return lax.ppermute(block, 'seq', [(i, i ^ step) for i in range(size)])  8.76 us
    ppermute x1, waiting for transfers between devices, on_device(): lax.ppermute(input_grad, 'section', [((i + 1) % sections, i) for i in ran...  6.13 us
    ppermute x11, waiting for transfers between devices, swap(): return lax.ppermute(block, 'seq', [(i, i ^ step) for i in range(size)])  5.92 us
    ppermute x1, waiting for transfers between devices, on_device(): lax.ppermute(layer_out, 'section', [((i - 1) % sections, i) for i in rang...  5.33 us
    unnamed x7, local copies, waits for them, and re-layouts  2.07 us
    ppermute x1, starting transfers between devices, on_device(): lax.ppermute(input_grad, 'section', [((i + 1) % sections, i) for i in ran...  1.79 us
    ppermute x1, starting transfers between devices, on_device(): lax.ppermute(layer_out, 'section', [((i - 1) % sections, i) for i in rang...  1.62 us
  transfers between devices with their start and end apart: 13, of which 5 were waited for; matrix products, arithmetic and copies ran while one was open for 0% of the time, Pallas kernels for 14%

profile of v2, /device:TPU:0, one launch (start us, length us, event | category | flops | bytes accessed | tf_op | source)
XLA Modules:
  0.0 45.8 jit_solution(829570301480113683)
XLA Ops:
  0.6 0.0 copy-start
  0.6 0.7 %copy-done = f32[1,1024]{1,0:T(1,128)S(1)} copy-done((f32[1,1024]{1,0:T(1,128)S(1)}, f32[1,1024]{1,0:T(1,128)}, u32[]{:S(2)}) %copy-start) | copy-done | bytes 4120
  1.3 1.8 %shard_map.113 = (bf16[128,512]{1,0:T(8,128)(2,1)S(1)}, bf16[128,1024]{1,0:T(8,128)(2,1)S(1)}, bf16[128,1024]{1,0:T(8,128)(2,1)S(1)}, bf16[1024,128]{1,0:T(8,128)(2,1)S(1)}, bf16[1024,128]{1,0:T(8,128)(2,1)S(1)}) custom-call(f32[1,1024]{1,0:T(1,128)S(1)} %copy-done, bf16[128,1024]{1,0:T(8,128)(2,1)} %bitcast.15, bf16[128,1024]{1,0:T(8,128)(2,1)} %bitcast.16, ...), custom_call_target="tpu_custom_call" | custom-call | tf_op jit(solution)/shard_map/pallas_call | solution.py:284
  3.1 4.0 %collective-permute-start.2 = (bf16[128,512]{1,0:T(8,128)(2,1)S(1)}, bf16[128,512]{1,0:T(8,128)(2,1)S(1)}, u32[]{:S(2)}, u32[]{:S(2)}) collective-permute-start(bf16[128,512]{1,0:T(8,128)(2,1)S(1)} %get-tuple-element.26.refs_0_), channel_id=1, source_target_pairs={{0,6},{1,7},{2,4},{3,5},{4,2},{5,3},{6,0},{7,1},{8,14},{9,15},{10,... | collective-permute-start | bytes 393224 | tf_op jit(solution)/shard_map/ppermute | solution.py:298
  7.1 0.5 %collective-permute-start.1 = (bf16[128,512]{1,0:T(8,128)(2,1)S(1)}, bf16[128,512]{1,0:T(8,128)(2,1)S(1)}, u32[]{:S(2)}, u32[]{:S(2)}) collective-permute-start(bf16[128,512]{1,0:T(8,128)(2,1)S(1)} %get-tuple-element.26.refs_0_), channel_id=1, source_target_pairs={{0,4},{1,5},{2,6},{3,7},{4,0},{5,1},{6,2},{7,3},{8,12},{9,13},{10,... | collective-permute-start | bytes 393224 | tf_op jit(solution)/shard_map/ppermute | solution.py:298
  7.6 0.1 collective-permute-start
  7.8 0.0 collective-permute-start.3
  7.8 3.2 %collective-permute-done.2.refs_3_ = bf16[128,512]{1,0:T(8,128)(2,1)S(1)} collective-permute-done((bf16[128,512]{1,0:T(8,128)(2,1)S(1)}, bf16[128,512]{1,0:T(8,128)(2,1)S(1)}, u32[]{:S(2)}, u32[]{:S(2)}) %collective-permute-start.2) | collective-permute-done | bytes 131104 | tf_op jit(solution)/shard_map/ppermute | solution.py:298
  11.0 0.0 collective-permute-start.6
  11.0 2.4 %collective-permute-done.1.refs_2_ = bf16[128,512]{1,0:T(8,128)(2,1)S(1)} collective-permute-done((bf16[128,512]{1,0:T(8,128)(2,1)S(1)}, bf16[128,512]{1,0:T(8,128)(2,1)S(1)}, u32[]{:S(2)}, u32[]{:S(2)}) %collective-permute-start.1) | collective-permute-done | bytes 131104 | tf_op jit(solution)/shard_map/ppermute | solution.py:298
  13.4 0.0 collective-permute-start.5
  13.4 0.2 collective-permute-done.refs_1_
  13.7 0.3 collective-permute-start.4
  13.9 0.0 copy-start.1
  13.9 0.0 copy-start.2
  13.9 0.7 %copy-done.1 = s32[1024]{0:T(1024)S(1)} copy-done((s32[1024]{0:T(1024)S(1)}, s32[1024]{0:T(1024)}, u32[]{:S(2)}) %copy-start.1) | copy-done | bytes 4120
  14.6 0.0 copy-done.2
  14.6 3.1 %shard_map.114 = (bf16[1024,128]{1,0:T(8,128)(2,1)S(1)}, bf16[1024,128]{1,0:T(8,128)(2,1)S(1)}, bf16[1024,128]{1,0:T(8,128)(2,1)S(1)}, f32[1024,128]{1,0:T(8,128...) custom-call(s32[1]{0:T(128)} %bitcast.4.me_ref, ...), custom_call_target="tpu_custom_call" | custom-call | tf_op jit(solution)/shard_map/pallas_call | solution.py:284
  17.8 0.0 collective-permute-done.3.refs_4_
  17.8 0.0 collective-permute-done.6.refs_7_
  17.8 0.0 collective-permute-done.5.refs_6_
  17.8 0.0 collective-permute-done.4.refs_5_
  17.8 4.6 %shard_map.115 = (bf16[128,256]{1,0:T(8,128)(2,1)S(1)}, bf16[128,256]{1,0:T(8,128)(2,1)S(1)}, bf16[128,256]{1,0:T(8,128)(2,1)S(1)}, bf16[128,256]{1,0:T(8,128)(2...) custom-call(bf16[128,512]{1,0:T(8,128)(2,1)S(1)} %get-tuple-element.26.refs_0_, ...), custom_call_target="tpu_custom_call" | custom-call | tf_op jit(solution)/shard_map/pallas_call | solution.py:284
  22.4 0.3 collective-permute-start.8
  22.7 2.7 %shard_map.116 = bf16[128,1024]{1,0:T(8,128)(2,1)S(1)} custom-call(bf16[128,512]{1,0:T(8,128)(2,1)S(1)} %get-tuple-element.26.refs_0_, bf16[128,512]{1,0:T(8,128)(2,1)S(1)} %collective-permute-done.refs_1_, bf16[128,512]{1,0:T(8,128)(2,1)S(1)} %collective-permute-done.1.refs_2_, bf16[128,512]{1,0:T(8,128)(2,1)S(1)} %collective-permute-done.2.refs_3_, ...), custom_call_target="tpu_custom_call" | custom-call | tf_op jit(solution)/shard_map/pallas_call | solution.py:284
  25.4 1.6 %collective-permute-start.7 = (bf16[128,1024]{1,0:T(8,128)(2,1)S(1)}, bf16[128,1024]{1,0:T(8,128)(2,1)S(1)}, u32[]{:S(2)}, u32[]{:S(2)}) collective-permute-start(bf16[128,1024]{1,0:T(8,128)(2,1)S(1)} %shard_map.116), channel_id=1, source_target_pairs={{24,0},{0,8},{8,16},{16,24},{25,1},{1,9},{9,17},{17,25},{26,2},{2,... | collective-permute-start | bytes 786440 | tf_op jit(solution)/shard_map/ppermute | solution.py:378
  27.0 0.0 collective-permute-done.8.refs_4_
  27.0 0.1 shard_map.118
  27.1 1.6 %collective-permute-start.9 = (bf16[128,256]{1,0:T(8,128)(2,1)S(1)}, bf16[128,256]{1,0:T(8,128)(2,1)S(1)}, u32[]{:S(2)}, u32[]{:S(2)}) collective-permute-start(bf16[128,256]{1,0:T(8,128)(2,1)S(1)} %get-tuple-element.43), channel_id=1, source_target_pairs={{0,2},{1,3},{2,0},{3,1},{4,6},{5,7},{6,4},{7,5},{8,10},{9,11},{10,... | collective-permute-start | bytes 196616 | tf_op jit(solution)/shard_map/ppermute | solution.py:298
  28.7 0.7 %collective-permute-start.10 = (bf16[128,256]{1,0:T(8,128)(2,1)S(1)}, bf16[128,256]{1,0:T(8,128)(2,1)S(1)}, u32[]{:S(2)}, u32[]{:S(2)}) collective-permute-start(bf16[128,256]{1,0:T(8,128)(2,1)S(1)} %get-tuple-element.44), channel_id=1, source_target_pairs={{0,4},{1,5},{2,6},{3,7},{4,0},{5,1},{6,2},{7,3},{8,12},{9,13},{10,... | collective-permute-start | bytes 196616 | tf_op jit(solution)/shard_map/ppermute | solution.py:298
  29.4 1.2 %collective-permute-start.11 = (bf16[128,256]{1,0:T(8,128)(2,1)S(1)}, bf16[128,256]{1,0:T(8,128)(2,1)S(1)}, u32[]{:S(2)}, u32[]{:S(2)}) collective-permute-start(bf16[128,256]{1,0:T(8,128)(2,1)S(1)} %get-tuple-element.45), channel_id=1, source_target_pairs={{0,6},{1,7},{2,4},{3,5},{4,2},{5,3},{6,0},{7,1},{8,14},{9,15},{10,... | collective-permute-start | bytes 196616 | tf_op jit(solution)/shard_map/ppermute | solution.py:298
  30.6 5.3 %collective-permute-done.7.next_ref = bf16[128,1024]{1,0:T(8,128)(2,1)S(1)} collective-permute-done((bf16[128,1024]{1,0:T(8,128)(2,1)S(1)}, bf16[128,1024]{1,0:T(8,128)(2,1)S(1)}, u32[]{:S(2)}, u32[]{:S(2)}) %collective-permute-start.7) | collective-permute-done | bytes 262176 | tf_op jit(solution)/shard_map/ppermute | solution.py:378
  36.0 0.7 %shard_map.117 = (f32[128,1024]{1,0:T(8,128)S(1)}, bf16[128,1024]{1,0:T(8,128)(2,1)}) custom-call(bf16[128,512]{1,0:T(8,128)(2,1)S(1)} %get-tuple-element.32.dq_ref, bf16[1024,512]{1,0:T(8,128)(2,1)S(1)} %get-tuple-element.33.wq_ref, bf16[128,1024]{1,0:T(8,128)(2,1)S(1)} %collective-permute-done.7.next_ref), custom_call_target="tpu_custom_call" | custom-call | tf_op jit(solution)/shard_map/pallas_call | solution.py:284
  36.7 0.0 collective-permute-done.9.refs_1_
  36.7 0.0 collective-permute-done.10.refs_2_
  36.7 0.0 collective-permute-done.11.refs_3_
  36.7 0.5 %shard_map.119 = bf16[128,1024]{1,0:T(8,128)(2,1)S(1)} custom-call(bf16[128,256]{1,0:T(8,128)(2,1)S(1)} %get-tuple-element.42.refs_0_, bf16[128,256]{1,0:T(8,128)(2,1)S(1)} %collective-permute-done.9.refs_1_, bf16[128,256]{1,0:T(8,128)(2,1)S(1)} %collective-permute-done.10.refs_2_, bf16[128,256]{1,0:T(8,128)(2,1)S(1)} %collective-permute-done.11.refs_3_, ...), custom_call_target="tpu_custom_call" | custom-call | tf_op jit(solution)/shard_map/pallas_call | solution.py:284
  37.2 1.8 %collective-permute-start.12 = (bf16[128,1024]{1,0:T(8,128)(2,1)S(1)}, bf16[128,1024]{1,0:T(8,128)(2,1)S(1)}, u32[]{:S(2)}, u32[]{:S(2)}) collective-permute-start(bf16[128,1024]{1,0:T(8,128)(2,1)S(1)} %shard_map.119), channel_id=1, source_target_pairs={{8,0},{16,8},{24,16},{0,24},{9,1},{17,9},{25,17},{1,25},{10,2},{18... | collective-permute-start | bytes 786440 | tf_op jit(solution)/shard_map/ppermute | solution.py:411
  39.0 6.1 %collective-permute-done.12 = bf16[128,1024]{1,0:T(8,128)(2,1)S(1)} collective-permute-done((bf16[128,1024]{1,0:T(8,128)(2,1)S(1)}, bf16[128,1024]{1,0:T(8,128)(2,1)S(1)}, u32[]{:S(2)}, u32[]{:S(2)}) %collective-permute-start.12) | collective-permute-done | bytes 262176 | tf_op jit(solution)/shard_map/ppermute | solution.py:411
  45.1 0.7 %copy.13 = bf16[1,128,1024]{2,1,0:T(8,128)(2,1)} copy(bf16[1,128,1024]{2,1,0:T(8,128)(2,1)S(1)} %bitcast.14) | data formatting | bytes 524288
Async XLA Ops:
  0.6 0.7 %copy-start = (f32[1,1024]{1,0:T(1,128)S(1)}, f32[1,1024]{1,0:T(1,128)}, u32[]{:S(2)}) copy-start(f32[1,1024]{1,0:T(1,128)} %refs_7_.1) | copy-start | bytes 12292
  3.1 7.9 %collective-permute-start.2 = (bf16[128,512]{1,0:T(8,128)(2,1)S(1)}, bf16[128,512]{1,0:T(8,128)(2,1)S(1)}, u32[]{:S(2)}, u32[]{:S(2)}) collective-permute-start(bf16[128,512]{1,0:T(8,128)(2,1)S(1)} %get-tuple-element.26.refs_0_), channel_id=1, source_target_pairs={{0,6},{1,7},{2,4},{3,5},{4,2},{5,3},{6,0},{7,1},{8,14},{9,15},{10,... | collective-permute-start | bytes 393224 | tf_op jit(solution)/shard_map/ppermute | solution.py:298
  7.1 6.3 %collective-permute-start.1 = (bf16[128,512]{1,0:T(8,128)(2,1)S(1)}, bf16[128,512]{1,0:T(8,128)(2,1)S(1)}, u32[]{:S(2)}, u32[]{:S(2)}) collective-permute-start(bf16[128,512]{1,0:T(8,128)(2,1)S(1)} %get-tuple-element.26.refs_0_), channel_id=1, source_target_pairs={{0,4},{1,5},{2,6},{3,7},{4,0},{5,1},{6,2},{7,3},{8,12},{9,13},{10,... | collective-permute-start | bytes 393224 | tf_op jit(solution)/shard_map/ppermute | solution.py:298
  7.6 6.0 %collective-permute-start = (bf16[128,512]{1,0:T(8,128)(2,1)S(1)}, bf16[128,512]{1,0:T(8,128)(2,1)S(1)}, u32[]{:S(2)}, u32[]{:S(2)}) collective-permute-start(bf16[128,512]{1,0:T(8,128)(2,1)S(1)} %get-tuple-element.26.refs_0_), channel_id=1, source_target_pairs={{0,2},{1,3},{2,0},{3,1},{4,6},{5,7},{6,4},{7,5},{8,10},{9,11},{10,... | collective-permute-start | bytes 393224 | tf_op jit(solution)/shard_map/ppermute | solution.py:298
  7.8 10.0 %collective-permute-start.3 = (bf16[128,512]{1,0:T(8,128)(2,1)S(1)}, bf16[128,512]{1,0:T(8,128)(2,1)S(1)}, u32[]{:S(2)}, u32[]{:S(2)}) collective-permute-start(bf16[128,512]{1,0:T(8,128)(2,1)S(1)} %get-tuple-element.26.refs_0_), channel_id=1, source_target_pairs={{0,1},{1,0},{2,3},{3,2},{4,5},{5,4},{6,7},{7,6},{8,9},{9,8},{10,11... | collective-permute-start | bytes 393224 | tf_op jit(solution)/shard_map/ppermute | solution.py:298
  11.0 6.8 %collective-permute-start.6 = (bf16[128,512]{1,0:T(8,128)(2,1)S(1)}, bf16[128,512]{1,0:T(8,128)(2,1)S(1)}, u32[]{:S(2)}, u32[]{:S(2)}) collective-permute-start(bf16[128,512]{1,0:T(8,128)(2,1)S(1)} %collective-permute-done.2.refs_3_), channel_id=1, source_target_pairs={{0,1},{1,0},{2,3},{3,2},{4,5},{5,4},{6,7},{7,6},{8,9},{9,8},{10,11... | collective-permute-start | bytes 393224 | tf_op jit(solution)/shard_map/ppermute | solution.py:298
  13.4 4.3 %collective-permute-start.5 = (bf16[128,512]{1,0:T(8,128)(2,1)S(1)}, bf16[128,512]{1,0:T(8,128)(2,1)S(1)}, u32[]{:S(2)}, u32[]{:S(2)}) collective-permute-start(bf16[128,512]{1,0:T(8,128)(2,1)S(1)} %collective-permute-done.1.refs_2_), channel_id=1, source_target_pairs={{0,1},{1,0},{2,3},{3,2},{4,5},{5,4},{6,7},{7,6},{8,9},{9,8},{10,11... | collective-permute-start | bytes 393224 | tf_op jit(solution)/shard_map/ppermute | solution.py:298
  13.7 4.1 %collective-permute-start.4 = (bf16[128,512]{1,0:T(8,128)(2,1)S(1)}, bf16[128,512]{1,0:T(8,128)(2,1)S(1)}, u32[]{:S(2)}, u32[]{:S(2)}) collective-permute-start(bf16[128,512]{1,0:T(8,128)(2,1)S(1)} %collective-permute-done.refs_1_), channel_id=1, source_target_pairs={{0,1},{1,0},{2,3},{3,2},{4,5},{5,4},{6,7},{7,6},{8,9},{9,8},{10,11... | collective-permute-start | bytes 393224 | tf_op jit(solution)/shard_map/ppermute | solution.py:298
  13.9 0.7 %copy-start.1 = (s32[1024]{0:T(1024)S(1)}, s32[1024]{0:T(1024)}, u32[]{:S(2)}) copy-start(s32[1024]{0:T(1024)} %param.18) | copy-start | bytes 12292
  13.9 0.7 %copy-start.2 = (s32[8]{0:T(128)S(1)}, s32[8]{0:T(128)}, u32[]{:S(2)}) copy-start(s32[8]{0:T(128)} %counts_ref.1) | copy-start | bytes 100
  22.4 4.6 %collective-permute-start.8 = (bf16[4,128,256]{2,1,0:T(8,128)(2,1)S(1)}, bf16[4,128,256]{2,1,0:T(8,128)(2,1)S(1)}, u32[]{:S(2)}, u32[]{:S(2)}) collective-permute-start(bf16[4,128,256]{2,1,0:T(8,128)(2,1)S(1)} %get-tuple-element.41), channel_id=1, source_target_pairs={{0,1},{1,0},{2,3},{3,2},{4,5},{5,4},{6,7},{7,6},{8,9},{9,8},{10,11... | collective-permute-start | bytes 786440 | tf_op jit(solution)/shard_map/ppermute | solution.py:298
  25.4 10.6 %collective-permute-start.7 = (bf16[128,1024]{1,0:T(8,128)(2,1)S(1)}, bf16[128,1024]{1,0:T(8,128)(2,1)S(1)}, u32[]{:S(2)}, u32[]{:S(2)}) collective-permute-start(bf16[128,1024]{1,0:T(8,128)(2,1)S(1)} %shard_map.116), channel_id=1, source_target_pairs={{24,0},{0,8},{8,16},{16,24},{25,1},{1,9},{9,17},{17,25},{26,2},{2,... | collective-permute-start | bytes 786440 | tf_op jit(solution)/shard_map/ppermute | solution.py:378
  27.1 9.6 %collective-permute-start.9 = (bf16[128,256]{1,0:T(8,128)(2,1)S(1)}, bf16[128,256]{1,0:T(8,128)(2,1)S(1)}, u32[]{:S(2)}, u32[]{:S(2)}) collective-permute-start(bf16[128,256]{1,0:T(8,128)(2,1)S(1)} %get-tuple-element.43), channel_id=1, source_target_pairs={{0,2},{1,3},{2,0},{3,1},{4,6},{5,7},{6,4},{7,5},{8,10},{9,11},{10,... | collective-permute-start | bytes 196616 | tf_op jit(solution)/shard_map/ppermute | solution.py:298
  28.7 8.0 %collective-permute-start.10 = (bf16[128,256]{1,0:T(8,128)(2,1)S(1)}, bf16[128,256]{1,0:T(8,128)(2,1)S(1)}, u32[]{:S(2)}, u32[]{:S(2)}) collective-permute-start(bf16[128,256]{1,0:T(8,128)(2,1)S(1)} %get-tuple-element.44), channel_id=1, source_target_pairs={{0,4},{1,5},{2,6},{3,7},{4,0},{5,1},{6,2},{7,3},{8,12},{9,13},{10,... | collective-permute-start | bytes 196616 | tf_op jit(solution)/shard_map/ppermute | solution.py:298
  29.4 7.3 %collective-permute-start.11 = (bf16[128,256]{1,0:T(8,128)(2,1)S(1)}, bf16[128,256]{1,0:T(8,128)(2,1)S(1)}, u32[]{:S(2)}, u32[]{:S(2)}) collective-permute-start(bf16[128,256]{1,0:T(8,128)(2,1)S(1)} %get-tuple-element.45), channel_id=1, source_target_pairs={{0,6},{1,7},{2,4},{3,5},{4,2},{5,3},{6,0},{7,1},{8,14},{9,15},{10,... | collective-permute-start | bytes 196616 | tf_op jit(solution)/shard_map/ppermute | solution.py:298
  37.2 7.9 %collective-permute-start.12 = (bf16[128,1024]{1,0:T(8,128)(2,1)S(1)}, bf16[128,1024]{1,0:T(8,128)(2,1)S(1)}, u32[]{:S(2)}, u32[]{:S(2)}) collective-permute-start(bf16[128,1024]{1,0:T(8,128)(2,1)S(1)} %shard_map.119), channel_id=1, source_target_pairs={{8,0},{16,8},{24,16},{0,24},{9,1},{17,9},{25,17},{1,25},{10,2},{18... | collective-permute-start | bytes 786440 | tf_op jit(solution)/shard_map/ppermute | solution.py:411

commit v3 on v2

v3 whole, which is shorter than its diff:
```python
from functools import partial
import math

import jax
import jax.numpy as jnp
from jax import lax
from jax.experimental import pallas as pl
from jax.experimental.pallas import tpu as pltpu
from jax.sharding import PartitionSpec as P


HEADS = 8
KV_HEADS = 2
HEAD_DIM = 64
GROUP = HEADS // KV_HEADS
KV_COLS = KV_HEADS * HEAD_DIM
PAIRS = HEADS // 2

NORM_EPSILON = 1e-05
MASKED_SCORE = -1e30

F32 = jnp.float32
BF16 = jnp.bfloat16

NN = (((1,), (0,)), ((), ()))
NT = (((1,), (1,)), ((), ()))


def dot(a, b, dims=NN):
    return lax.dot_general(a, b, dims, preferred_element_type=F32)


def vmem(count):
    return [pl.BlockSpec(memory_space=pltpu.VMEM)] * count


def shape(dims, dtype):
    return jax.ShapeDtypeStruct(dims, dtype)


def rms(inputs, gain):
    widened = inputs.astype(F32)
    inverse = lax.rsqrt(jnp.mean(widened * widened, axis=-1, keepdims=True) + NORM_EPSILON)
    return (widened * inverse * gain).astype(BF16), inverse, widened


def project_kv(gain_hbm, xf_hbm, xb_hbm, wk_hbm, wv_hbm, kv_ref, gain_ref, xf_ref, xb_ref, wkv_ref, sems):
    copies = [
        pltpu.make_async_copy(source, target, sems.at[place])
        for place, (source, target) in enumerate(
            (
                (xf_hbm, xf_ref),
                (gain_hbm, gain_ref),
                (xb_hbm, xb_ref),
                (wk_hbm, wkv_ref.at[:, :KV_COLS]),
                (wv_hbm, wkv_ref.at[:, KV_COLS:]),
            )
        )
    ]
    for copy in copies:
        copy.start()
    rows = xf_ref.shape[0]
    copies[0].wait()
    copies[1].wait()
    gain = gain_ref[...]
    normed_f, _, _ = rms(xf_ref[...], gain)
    copies[2].wait()
    normed_b, _, _ = rms(xb_ref[...], gain)
    normed = jnp.concatenate([normed_f, normed_b], axis=0)
    copies[3].wait()
    copies[4].wait()
    both = dot(normed, wkv_ref[...]).astype(BF16)
    kv_ref[:, : 2 * KV_COLS] = both[:rows]
    kv_ref[:, 2 * KV_COLS :] = both[rows:]


def spread_heads(flat, out_ref, scale):
    rows = flat.shape[0]
    flat = flat.astype(BF16).astype(F32) * scale
    lane = lax.broadcasted_iota(jnp.int32, (rows, KV_COLS), 1)
    for head in range(HEADS):
        tile = head // 2
        block = flat[:, tile * KV_COLS : (tile + 1) * KV_COLS]
        group = head // GROUP
        if head % 2 != group:
            block = pltpu.roll(block, HEAD_DIM, 1)
        block = jnp.where((lane // HEAD_DIM) == group, block, 0.0)
        out_ref[head * rows : (head + 1) * rows, :] = block.astype(BF16)


def prepare(
    order,
    me_ref,
    xf_ref,
    xb_ref,
    gain_ref,
    frames_hbm,
    counts_hbm,
    cot_hbm,
    wq_hbm,
    wo_hbm,
    qf_ref,
    qb_ref,
    dout_ref,
    bias_ref,
    cot_ref,
    wq_ref,
    wo_ref,
    frames_ref,
    counts_ref,
    sems,
):
    copies = [
        pltpu.make_async_copy(source, target, sems.at[place])
        for place, (source, target) in enumerate(
            (
                (wq_hbm, wq_ref),
                (frames_hbm, frames_ref),
                (counts_hbm, counts_ref),
                (cot_hbm, cot_ref),
                (wo_hbm, wo_ref),
            )
        )
    ]
    for copy in copies:
        copy.start()
    gain = gain_ref[...]
    rows = xf_ref.shape[0]
    normed_f, _, _ = rms(xf_ref[...], gain)
    normed_b, _, _ = rms(xb_ref[...], gain)
    copies[1].wait()
    copies[2].wait()
    me = me_ref[0]
    row = lax.broadcasted_iota(jnp.int32, (rows, rows), 0)
    query_frames = jnp.broadcast_to(frames_ref[pl.ds(me, 1), :], (rows, rows))
    for place, step in enumerate(order):
        source = jnp.bitwise_xor(me, step)
        own = jnp.broadcast_to(frames_ref[pl.ds(source, 1), :], (rows, rows))
        key_frames = jnp.transpose(own.astype(F32)).astype(jnp.int32)
        visible = (key_frames <= query_frames) & (row < counts_ref[source])
        bias_ref[place * rows : (place + 1) * rows, :] = jnp.where(visible, 0.0, MASKED_SCORE)
    scale = 1.0 / math.sqrt(HEAD_DIM)
    copies[0].wait()
    queries = dot(jnp.concatenate([normed_f, normed_b], axis=0), wq_ref[...])
    spread_heads(queries[:rows], qf_ref, scale)
    spread_heads(queries[rows:], qb_ref, scale)
    copies[3].wait()
    copies[4].wait()
    spread_heads(dot(cot_ref[...], wo_ref[...], NT), dout_ref, 1.0)


def score_block(keys, q_rows, bias_ref, s_ref, slot, lines, top):
    block = dot(keys[lines], q_rows, NT)
    bias = bias_ref[lines, :]
    block = block + jnp.concatenate([bias, bias], axis=1)
    s_ref[slot, lines, :] = block
    part = jnp.max(block, axis=0, keepdims=True)
    return part if top is None else jnp.maximum(top, part)


def plus(left, right):
    return right if left is None else left + right


def attend_backward(count, *refs):
    pieces = refs[:count]
    q_ref, dout_ref, bias_ref = refs[count : count + 3]
    half = count // 2
    even_refs = refs[count + 3 : count + 3 + half]
    odd_ref, dq_ref = refs[count + 3 + half : count + 5 + half]
    kv_ref, s_ref, dp_ref, e_ref, acc_ref, dqt_ref = refs[count + 5 + half :]
    rows = pieces[0].shape[0]
    total = rows * count
    chunk = min(4 * rows, total)
    for place, piece in enumerate(pieces):
        kv_ref[place * rows : (place + 1) * rows, :] = piece[:, 2 * KV_COLS :]
    keys = kv_ref[:, :KV_COLS]
    values = kv_ref[:, KV_COLS:]
    keys_t = jnp.transpose(keys)
    scale = 1.0 / math.sqrt(HEAD_DIM)
    wide = 2 * rows
    tops, stats, scaled = {}, {}, {}
    for step in range(-1, PAIRS + 1):
        ahead, now, behind = step + 1, step, step - 1
        top = row_sum = mixed = query_grad = None
        for first in range(0, total, chunk):
            lines = slice(first, first + chunk)
            if ahead < PAIRS:
                q_rows = q_ref[ahead * wide : (ahead + 1) * wide, :]
                top = score_block(keys, q_rows, bias_ref, s_ref, ahead % 2, lines, top)
            if 0 <= now < PAIRS:
                slot = now % 2
                weights = jnp.exp(s_ref[slot, lines, :] - tops[now])
                prob_grad = dot(values[lines], dout_ref[now * wide : (now + 1) * wide, :], NT)
                row_sum = plus(row_sum, jnp.sum(weights, axis=0, keepdims=True))
                mixed = plus(mixed, jnp.sum(weights * prob_grad, axis=0, keepdims=True))
                dp_ref[slot, lines, :] = prob_grad
                e_ref[slot, lines, :] = weights.astype(BF16)
            if behind >= 0:
                slot = behind % 2
                weights = e_ref[slot, lines, :]
                score_grad = weights * (dp_ref[slot, lines, :] - stats[behind][1]).astype(BF16)
                group = (2 * behind) // GROUP
                own = slice(group * HEAD_DIM, (group + 1) * HEAD_DIM)
                query_grad = plus(query_grad, dot(keys_t[own, lines], score_grad))
                key_grad = dot(score_grad, scaled[behind][0])
                value_grad = dot(weights, scaled[behind][1])
                if behind:
                    key_grad = key_grad + acc_ref[lines, :KV_COLS]
                    value_grad = value_grad + acc_ref[lines, KV_COLS:]
                if behind < PAIRS - 1:
                    acc_ref[lines, :KV_COLS] = key_grad
                    acc_ref[lines, KV_COLS:] = value_grad
                else:
                    for place in range(first // rows, (first + chunk) // rows):
                        target = even_refs[place] if place < half else odd_ref.at[place - half]
                        inner = slice(place * rows - first, (place + 1) * rows - first)
                        target[:, :KV_COLS] = key_grad[inner].astype(BF16)
                        target[:, KV_COLS:] = value_grad[inner].astype(BF16)
        if ahead < PAIRS:
            tops[ahead] = top
        if 0 <= now < PAIRS:
            inverse_sum = 1.0 / row_sum
            stats[now] = (inverse_sum, mixed * inverse_sum)
            cols = slice(now * wide, (now + 1) * wide)
            factor = jnp.transpose(jnp.broadcast_to(inverse_sum, (KV_COLS, wide)))
            scaled[now] = (
                (q_ref[cols, :].astype(F32) * factor).astype(BF16),
                (dout_ref[cols, :].astype(F32) * factor).astype(BF16),
            )
        if behind >= 0:
            part = query_grad * (stats[behind][0] * scale)
            dqt_ref[2 * behind * HEAD_DIM : (2 * behind + 1) * HEAD_DIM, :] = part[:, :rows]
            dqt_ref[(2 * behind + 1) * HEAD_DIM : (2 * behind + 2) * HEAD_DIM, :] = part[:, rows:]
    dq_ref[...] = jnp.transpose(dqt_ref[...]).astype(BF16)


def attend_forward(count, *refs):
    pieces = refs[:count]
    q_ref, bias_ref, x_ref, wo_ref, out_ref = refs[count : count + 5]
    kv_ref, s_ref, at_ref = refs[count + 5 :]
    rows = pieces[0].shape[0]
    total = rows * count
    chunk = min(4 * rows, total)
    for place, piece in enumerate(pieces):
        kv_ref[place * rows : (place + 1) * rows, :] = piece[:, : 2 * KV_COLS]
    keys = kv_ref[:, :KV_COLS]
    values_t = jnp.transpose(kv_ref[:, KV_COLS:])
    ones = jnp.ones((16, total), BF16)
    extended = [
        jnp.concatenate([values_t[group * HEAD_DIM : (group + 1) * HEAD_DIM], ones], axis=0)
        for group in range(KV_HEADS)
    ]
    wide = 2 * rows
    tops = {}
    for now in range(-1, PAIRS):
        ahead = now + 1
        top = mixed = None
        for first in range(0, total, chunk):
            lines = slice(first, first + chunk)
            if ahead < PAIRS:
                q_rows = q_ref[ahead * wide : (ahead + 1) * wide, :]
                top = score_block(keys, q_rows, bias_ref, s_ref, ahead % 2, lines, top)
            if now >= 0:
                weights = jnp.exp(s_ref[now % 2, lines, :] - tops[now])
                mixed = plus(mixed, dot(extended[(2 * now) // GROUP][:, lines], weights.astype(BF16)))
        if ahead < PAIRS:
            tops[ahead] = top
        if now >= 0:
            part = mixed[:HEAD_DIM] * (1.0 / mixed[HEAD_DIM : HEAD_DIM + 1])
            at_ref[2 * now * HEAD_DIM : (2 * now + 1) * HEAD_DIM, :] = part[:, :rows]
            at_ref[(2 * now + 1) * HEAD_DIM : (2 * now + 2) * HEAD_DIM, :] = part[:, rows:]
    attended = jnp.transpose(at_ref[...]).astype(BF16)
    out_ref[...] = (x_ref[...].astype(F32) + dot(attended, wo_ref[...])).astype(BF16)


def query_back(dq_ref, wq_ref, next_ref, out_ref, next_hbm, sem):
    copy = pltpu.make_async_copy(next_ref, next_hbm, sem)
    copy.start()
    out_ref[...] = dot(dq_ref[...], wq_ref[...], NT)
    copy.wait()


def add_pieces(count, *refs):
    for place in range(count):
        left = refs[place][...].astype(F32)
        refs[count + 1 + place][...] = (left + refs[count][place].astype(F32)).astype(BF16)


def input_back(count, *refs):
    pieces = refs[:count]
    base_ref, x_ref, cot_ref, gain_ref, wkv_ref, out_ref = refs[count:]
    grads = pieces[0][...].astype(F32)
    for piece in pieces[1:]:
        grads = grads + piece[...].astype(F32)
    grads = grads.astype(BF16)
    gain = gain_ref[...]
    normed_grad = base_ref[...] + dot(grads, wkv_ref[...], NT)
    _, inverse, widened = rms(x_ref[...], gain)
    scaled = normed_grad * gain
    mean = jnp.mean(widened * scaled, axis=-1, keepdims=True)
    grad = cot_ref[...].astype(F32) + inverse * scaled - widened * (inverse * inverse * inverse * mean)
    out_ref[...] = grad.astype(BF16)


def local(array):
    return pltpu.with_memory_space_constraint(array, pltpu.VMEM)


def size_of(item):
    return math.prod(item.shape) * jnp.dtype(item.dtype).itemsize


def call(kernel, outs, args, scratch=(), sems=None, smem=0, hbm=0, out_hbm=0):
    many = isinstance(outs, (list, tuple))
    outs = list(outs) if many else [outs]
    inside, kept = len(args) - hbm, len(outs) - out_hbm
    args = list(args[:smem]) + [local(arg) for arg in args[smem:inside]] + [
        pltpu.with_memory_space_constraint(arg, pltpu.HBM) for arg in args[inside:]
    ]
    room = sum(size_of(item) for item in scratch) + (8 << 20)
    scratch = list(scratch) + ([] if sems is None else [pltpu.SemaphoreType.DMA(sems)])
    results = pl.pallas_call(
        kernel,
        out_shape=[pltpu.VMEM(out.shape, out.dtype) for out in outs[:kept]] + outs[kept:],
        in_specs=[pl.BlockSpec(memory_space=pltpu.SMEM)] * smem
        + vmem(inside - smem)
        + [pl.BlockSpec(memory_space=pltpu.HBM)] * hbm,
        out_specs=vmem(kept) + [pl.BlockSpec(memory_space=pltpu.HBM)] * out_hbm,
        scratch_shapes=scratch,
        compiler_params=pltpu.CompilerParams(vmem_limit_bytes=room),
    )(*args)
    return results if many else results[0]


def swap(block, step, size):
    return lax.ppermute(block, "seq", [(i, i ^ step) for i in range(size)])


def order_of(size):
    return list(range(0, size, 2)) + list(range(1, size, 2))


def by_permutes(size):
    return size in (2, 4, 8)


def gather_near(block, size):
    if not by_permutes(size):
        return lax.all_gather(block, "seq", axis=0)
    return [block] + [swap(block, step, size) for step in range(2, size, 2)]


def gather_far(near, size):
    if not by_permutes(size):
        me = lax.axis_index("seq")
        return [lax.dynamic_index_in_dim(near, me ^ step, 0, False) for step in order_of(size)]
    return near + [swap(piece, 1, size) for piece in near]


def on_device(
    size,
    forward_input,
    stored_input,
    output_cotangent,
    norm_gain,
    query_weight,
    key_weight,
    value_weight,
    output_weight,
    frame_index,
    valid_counts,
):
    xf_hbm, xb_hbm, cot_hbm = forward_input[0], stored_input[0], output_cotangent[0]
    wq_hbm, wk_hbm, wv_hbm, wo_hbm = query_weight[0], key_weight[0], value_weight[0], output_weight[0]
    rows, width = xf_hbm.shape
    total = rows * size
    sections = lax.axis_size("section")
    order = order_of(size)
    half = size // 2
    kv_shape = shape((rows, 2 * KV_COLS), BF16)
    spread = shape((HEADS * rows, KV_COLS), BF16)
    wide = 2 * rows
    frames = frame_index.reshape(size, rows)
    me = lax.axis_index("seq").astype(jnp.int32).reshape(1)

    kv, gain, xf, xb, wkv = call(
        project_kv,
        (
            shape((rows, 4 * KV_COLS), BF16),
            shape(norm_gain.shape, F32),
            shape(xf_hbm.shape, BF16),
            shape(xb_hbm.shape, BF16),
            shape((width, 2 * KV_COLS), BF16),
        ),
        (norm_gain, xf_hbm, xb_hbm, wk_hbm, wv_hbm),
        sems=(5,),
        hbm=5,
    )
    near = gather_near(kv, size)
    qf, qb, dout, bias, cot, wq, wo = call(
        partial(prepare, order),
        (spread, spread, spread, shape((total, rows), F32))
        + tuple(shape(item.shape, BF16) for item in (cot_hbm, wq_hbm, wo_hbm)),
        (me, xf, xb, gain, frames, valid_counts, cot_hbm, wq_hbm, wo_hbm),
        scratch=(pltpu.VMEM(frames.shape, jnp.int32), pltpu.SMEM(valid_counts.shape, jnp.int32)),
        sems=(5,),
        smem=1,
        hbm=5,
    )
    pieces = gather_far(near, size)
    layer_out = call(
        partial(attend_forward, size),
        shape((rows, width), BF16),
        (*pieces, qf, bias, xf, wo),
        scratch=(
            pltpu.VMEM((total, 2 * KV_COLS), BF16),
            pltpu.VMEM((2, total, wide), F32),
            pltpu.VMEM((HEADS * HEAD_DIM, rows), F32),
        ),
    )
    shifted = lax.ppermute(layer_out, "section", [((i - 1) % sections, i) for i in range(sections)])
    *grads, dq = call(
        partial(attend_backward, size),
        (kv_shape,) * half + (shape((half, rows, 2 * KV_COLS), BF16), shape((rows, HEADS * HEAD_DIM), BF16)),
        (*pieces, qb, dout, bias),
        scratch=(
            pltpu.VMEM((total, 2 * KV_COLS), BF16),
            pltpu.VMEM((2, total, wide), F32),
            pltpu.VMEM((2, total, wide), F32),
            pltpu.VMEM((2, total, wide), BF16),
            pltpu.VMEM((total, 2 * KV_COLS), F32),
            pltpu.VMEM((HEADS * HEAD_DIM, rows), F32),
        ),
    )
    even, odd = grads[:half], grads[half]
    if by_permutes(size):
        other = swap(odd, 1, size)
        sums = call(partial(add_pieces, half), (kv_shape,) * half, (*even, other))
        received = [sums[0]] + [swap(sums[i], 2 * i, size) for i in range(1, half)]
    else:
        both = jnp.stack(list(even) + [odd[i] for i in range(half)]).astype(F32)
        places = jnp.argsort(jnp.array(order, jnp.int32) ^ lax.axis_index("seq"))
        summed = lax.psum_scatter(both[places], "seq", scatter_dimension=0, tiled=True)
        received = [summed[0].astype(BF16)]
    base, forward_next = call(
        query_back, (shape((rows, width), F32), shape((rows, width), BF16)), (dq, wq, shifted), sems=(), out_hbm=1
    )
    input_grad = call(
        partial(input_back, len(received)), shape((rows, width), BF16), (*received, base, xb, cot, gain, wkv)
    )
    backward_next = lax.ppermute(input_grad, "section", [((i + 1) % sections, i) for i in range(sections)])
    return (forward_next[None], backward_next[None])


def placed(size, *arrays):
    return on_device(size, *arrays)


def solution(mesh):
    size = mesh.shape["seq"]
    return jax.shard_map(
        partial(placed, size),
        mesh=mesh,
        in_specs=(
            P("section", "seq", None),
            P("section", "seq", None),
            P("section", "seq", None),
            P("section", None),
            P("section", None, None),
            P("section", None, None),
            P("section", None, None),
            P("section", None, None),
            P(),
            P(),
        ),
        out_specs=(P("section", "seq", None), P("section", "seq", None)),
        check_vma=False,
    )
```

time: 46.1 us -> 42 us (0.911)
  Pallas kernels: 13.4 us -> 10.8 us
  local copies, waits for them, and re-layouts: 2.07 us -> 0.7 us
    pallas_call x7, Pallas kernels: 13.4 us -> 10.8 us  [call(): pl.pallas_call(kernel, out_shape=[pltpu.VMEM(out.shape, out.dtype) for ou...]
    unnamed x7 -> x1, local copies, waits for them, and re-layouts: 2.07 us -> 0.7 us
  transfers between devices with their start and end apart: 13 -> 13, of which waited for: 5 -> 5; matrix products, arithmetic and copies ran while one was open for 0% -> 0% of each run, Pallas kernels for 14% -> 12%
where the time goes in v3:
time: 42 us; the launch traced here: 41.9 us
  waiting for transfers between devices  17.4 us (41%)
  starting transfers between devices  12.2 us (29%)
  Pallas kernels  10.8 us (26%)
  between operations  0.74 us (2%)
  local copies, waits for them, and re-layouts  0.7 us (2%)
    pallas_call x7, Pallas kernels, call(): pl.pallas_call(kernel, out_shape=[pltpu.VMEM(out.shape, out.dtype) for ou...  10.8 us
    ppermute x11, starting transfers between devices, swap(): return lax.ppermute(block, 'seq', [(i, i ^ step) for i in range(size)])  8.77 us
    ppermute x1, waiting for transfers between devices, on_device(): lax.ppermute(input_grad, 'section', [((i + 1) % sections, i) for i in ran...  6.13 us
    ppermute x11, waiting for transfers between devices, swap(): return lax.ppermute(block, 'seq', [(i, i ^ step) for i in range(size)])  5.92 us
    ppermute x1, waiting for transfers between devices, on_device(): lax.ppermute(layer_out, 'section', [((i - 1) % sections, i) for i in rang...  5.33 us
    ppermute x1, starting transfers between devices, on_device(): lax.ppermute(input_grad, 'section', [((i + 1) % sections, i) for i in ran...  1.79 us
    ppermute x1, starting transfers between devices, on_device(): lax.ppermute(layer_out, 'section', [((i - 1) % sections, i) for i in rang...  1.63 us
  transfers between devices with their start and end apart: 13, of which 5 were waited for; matrix products, arithmetic and copies ran while one was open for 0% of the time, Pallas kernels for 12%

profile of v3, /device:TPU:0, one launch (start us, length us, event | category | flops | bytes accessed | tf_op | source)
XLA Modules:
  0.0 41.9 jit_solution(411383290722644110)
XLA Ops:
  0.6 1.6 %shard_map.113 = (bf16[128,512]{1,0:T(8,128)(2,1)S(1)}, f32[1,1024]{1,0:T(1,128)S(1)}, bf16[128,1024]{1,0:T(8,128)(2,1)S(1)}, bf16[128,1024]{1,0:T(8,128)(2,1)S(1)}, bf16[1024,256]{1,0:T(8,128)(2,1)S(1)}) custom-call(f32[1,1024]{1,0:T(1,128)} %gain_hbm.1, bf16[128,1024]{1,0:T(8,128)(2,1)} %bitcast.14, bf16[128,1024]{1,0:T(8,128)(2,1)} %bitcast.15, ...), custom_call_target="tpu_custom_call" | custom-call | tf_op jit(solution)/shard_map/pallas_call | solution.py:323
  2.3 4.0 %collective-permute-start.2 = (bf16[128,512]{1,0:T(8,128)(2,1)S(1)}, bf16[128,512]{1,0:T(8,128)(2,1)S(1)}, u32[]{:S(2)}, u32[]{:S(2)}) collective-permute-start(bf16[128,512]{1,0:T(8,128)(2,1)S(1)} %get-tuple-element.26.refs_0_), channel_id=1, source_target_pairs={{0,6},{1,7},{2,4},{3,5},{4,2},{5,3},{6,0},{7,1},{8,14},{9,15},{10,... | collective-permute-start | bytes 393224 | tf_op jit(solution)/shard_map/ppermute | solution.py:337
  6.2 0.5 %collective-permute-start.1 = (bf16[128,512]{1,0:T(8,128)(2,1)S(1)}, bf16[128,512]{1,0:T(8,128)(2,1)S(1)}, u32[]{:S(2)}, u32[]{:S(2)}) collective-permute-start(bf16[128,512]{1,0:T(8,128)(2,1)S(1)} %get-tuple-element.26.refs_0_), channel_id=1, source_target_pairs={{0,4},{1,5},{2,6},{3,7},{4,0},{5,1},{6,2},{7,3},{8,12},{9,13},{10,... | collective-permute-start | bytes 393224 | tf_op jit(solution)/shard_map/ppermute | solution.py:337
  6.7 0.1 collective-permute-start
  6.9 0.0 collective-permute-start.3
  6.9 3.2 %collective-permute-done.2.refs_3_ = bf16[128,512]{1,0:T(8,128)(2,1)S(1)} collective-permute-done((bf16[128,512]{1,0:T(8,128)(2,1)S(1)}, bf16[128,512]{1,0:T(8,128)(2,1)S(1)}, u32[]{:S(2)}, u32[]{:S(2)}) %collective-permute-start.2) | collective-permute-done | bytes 131104 | tf_op jit(solution)/shard_map/ppermute | solution.py:337
  10.1 0.0 collective-permute-start.6
  10.1 2.4 %collective-permute-done.1.refs_2_ = bf16[128,512]{1,0:T(8,128)(2,1)S(1)} collective-permute-done((bf16[128,512]{1,0:T(8,128)(2,1)S(1)}, bf16[128,512]{1,0:T(8,128)(2,1)S(1)}, u32[]{:S(2)}, u32[]{:S(2)}) %collective-permute-start.1) | collective-permute-done | bytes 131104 | tf_op jit(solution)/shard_map/ppermute | solution.py:337
  12.5 0.0 collective-permute-start.5
  12.5 0.2 collective-permute-done.refs_1_
  12.8 0.3 collective-permute-start.4
  13.1 2.4 %shard_map.114 = (bf16[1024,128]{1,0:T(8,128)(2,1)S(1)}, bf16[1024,128]{1,0:T(8,128)(2,1)S(1)}, bf16[1024,128]{1,0:T(8,128)(2,1)S(1)}, f32[1024,128]{1,0:T(8,128...) custom-call(s32[1]{0:T(128)} %bitcast.4.me_ref, ...), custom_call_target="tpu_custom_call" | custom-call | tf_op jit(solution)/shard_map/pallas_call | solution.py:323
  15.4 0.0 collective-permute-done.3.refs_4_
  15.4 0.0 collective-permute-done.6.refs_7_
  15.4 0.0 collective-permute-done.5.refs_6_
  15.5 0.0 collective-permute-done.4.refs_5_
  15.5 3.8 %shard_map.115 = (bf16[128,256]{1,0:T(8,128)(2,1)S(1)}, bf16[128,256]{1,0:T(8,128)(2,1)S(1)}, bf16[128,256]{1,0:T(8,128)(2,1)S(1)}, bf16[128,256]{1,0:T(8,128)(2...) custom-call(bf16[128,512]{1,0:T(8,128)(2,1)S(1)} %get-tuple-element.26.refs_0_, ...), custom_call_target="tpu_custom_call" | custom-call | tf_op jit(solution)/shard_map/pallas_call | solution.py:323
  19.2 0.3 collective-permute-start.8
  19.5 1.9 %shard_map.116 = bf16[128,1024]{1,0:T(8,128)(2,1)S(1)} custom-call(bf16[128,512]{1,0:T(8,128)(2,1)S(1)} %get-tuple-element.26.refs_0_, bf16[128,512]{1,0:T(8,128)(2,1)S(1)} %collective-permute-done.refs_1_, bf16[128,512]{1,0:T(8,128)(2,1)S(1)} %collective-permute-done.1.refs_2_, bf16[128,512]{1,0:T(8,128)(2,1)S(1)} %collective-permute-done.2.refs_3_, ...), custom_call_target="tpu_custom_call" | custom-call | tf_op jit(solution)/shard_map/pallas_call | solution.py:323
  21.4 1.6 %collective-permute-start.7 = (bf16[128,1024]{1,0:T(8,128)(2,1)S(1)}, bf16[128,1024]{1,0:T(8,128)(2,1)S(1)}, u32[]{:S(2)}, u32[]{:S(2)}) collective-permute-start(bf16[128,1024]{1,0:T(8,128)(2,1)S(1)} %shard_map.116), channel_id=1, source_target_pairs={{24,0},{0,8},{8,16},{16,24},{25,1},{1,9},{9,17},{17,25},{26,2},{2,... | collective-permute-start | bytes 786440 | tf_op jit(solution)/shard_map/ppermute | solution.py:422
  23.1 0.0 collective-permute-done.8.refs_4_
  23.1 0.1 shard_map.118
  23.1 1.6 %collective-permute-start.9 = (bf16[128,256]{1,0:T(8,128)(2,1)S(1)}, bf16[128,256]{1,0:T(8,128)(2,1)S(1)}, u32[]{:S(2)}, u32[]{:S(2)}) collective-permute-start(bf16[128,256]{1,0:T(8,128)(2,1)S(1)} %get-tuple-element.44), channel_id=1, source_target_pairs={{0,2},{1,3},{2,0},{3,1},{4,6},{5,7},{6,4},{7,5},{8,10},{9,11},{10,... | collective-permute-start | bytes 196616 | tf_op jit(solution)/shard_map/ppermute | solution.py:337
  24.7 0.7 %collective-permute-start.10 = (bf16[128,256]{1,0:T(8,128)(2,1)S(1)}, bf16[128,256]{1,0:T(8,128)(2,1)S(1)}, u32[]{:S(2)}, u32[]{:S(2)}) collective-permute-start(bf16[128,256]{1,0:T(8,128)(2,1)S(1)} %get-tuple-element.45), channel_id=1, source_target_pairs={{0,4},{1,5},{2,6},{3,7},{4,0},{5,1},{6,2},{7,3},{8,12},{9,13},{10,... | collective-permute-start | bytes 196616 | tf_op jit(solution)/shard_map/ppermute | solution.py:337
  25.5 1.2 %collective-permute-start.11 = (bf16[128,256]{1,0:T(8,128)(2,1)S(1)}, bf16[128,256]{1,0:T(8,128)(2,1)S(1)}, u32[]{:S(2)}, u32[]{:S(2)}) collective-permute-start(bf16[128,256]{1,0:T(8,128)(2,1)S(1)} %get-tuple-element.46), channel_id=1, source_target_pairs={{0,6},{1,7},{2,4},{3,5},{4,2},{5,3},{6,0},{7,1},{8,14},{9,15},{10,... | collective-permute-start | bytes 196616 | tf_op jit(solution)/shard_map/ppermute | solution.py:337
  26.7 5.3 %collective-permute-done.7.next_ref = bf16[128,1024]{1,0:T(8,128)(2,1)S(1)} collective-permute-done((bf16[128,1024]{1,0:T(8,128)(2,1)S(1)}, bf16[128,1024]{1,0:T(8,128)(2,1)S(1)}, u32[]{:S(2)}, u32[]{:S(2)}) %collective-permute-start.7) | collective-permute-done | bytes 262176 | tf_op jit(solution)/shard_map/ppermute | solution.py:422
  32.0 0.7 %shard_map.117 = (f32[128,1024]{1,0:T(8,128)S(1)}, bf16[128,1024]{1,0:T(8,128)(2,1)}) custom-call(bf16[128,512]{1,0:T(8,128)(2,1)S(1)} %get-tuple-element.33.dq_ref, bf16[1024,512]{1,0:T(8,128)(2,1)S(1)} %get-tuple-element.34.wq_ref, bf16[128,1024]{1,0:T(8,128)(2,1)S(1)} %collective-permute-done.7.next_ref), custom_call_target="tpu_custom_call" | custom-call | tf_op jit(solution)/shard_map/pallas_call | solution.py:323
  32.7 0.0 collective-permute-done.9.refs_1_
  32.8 0.0 collective-permute-done.10.refs_2_
  32.8 0.0 collective-permute-done.11.refs_3_
  32.8 0.4 %shard_map.119 = bf16[128,1024]{1,0:T(8,128)(2,1)S(1)} custom-call(bf16[128,256]{1,0:T(8,128)(2,1)S(1)} %get-tuple-element.43.refs_0_, bf16[128,256]{1,0:T(8,128)(2,1)S(1)} %collective-permute-done.9.refs_1_, bf16[128,256]{1,0:T(8,128)(2,1)S(1)} %collective-permute-done.10.refs_2_, bf16[128,256]{1,0:T(8,128)(2,1)S(1)} %collective-permute-done.11.refs_3_, ...), custom_call_target="tpu_custom_call" | custom-call | tf_op jit(solution)/shard_map/pallas_call | solution.py:323
  33.2 1.8 %collective-permute-start.12 = (bf16[128,1024]{1,0:T(8,128)(2,1)S(1)}, bf16[128,1024]{1,0:T(8,128)(2,1)S(1)}, u32[]{:S(2)}, u32[]{:S(2)}) collective-permute-start(bf16[128,1024]{1,0:T(8,128)(2,1)S(1)} %shard_map.119), channel_id=1, source_target_pairs={{8,0},{16,8},{24,16},{0,24},{9,1},{17,9},{25,17},{1,25},{10,2},{18... | collective-permute-start | bytes 786440 | tf_op jit(solution)/shard_map/ppermute | solution.py:452
  35.0 6.1 %collective-permute-done.12 = bf16[128,1024]{1,0:T(8,128)(2,1)S(1)} collective-permute-done((bf16[128,1024]{1,0:T(8,128)(2,1)S(1)}, bf16[128,1024]{1,0:T(8,128)(2,1)S(1)}, u32[]{:S(2)}, u32[]{:S(2)}) %collective-permute-start.12) | collective-permute-done | bytes 262176 | tf_op jit(solution)/shard_map/ppermute | solution.py:452
  41.2 0.7 %copy.13 = bf16[1,128,1024]{2,1,0:T(8,128)(2,1)} copy(bf16[1,128,1024]{2,1,0:T(8,128)(2,1)S(1)} %bitcast.13) | data formatting | bytes 524288
Async XLA Ops:
  2.3 7.9 %collective-permute-start.2 = (bf16[128,512]{1,0:T(8,128)(2,1)S(1)}, bf16[128,512]{1,0:T(8,128)(2,1)S(1)}, u32[]{:S(2)}, u32[]{:S(2)}) collective-permute-start(bf16[128,512]{1,0:T(8,128)(2,1)S(1)} %get-tuple-element.26.refs_0_), channel_id=1, source_target_pairs={{0,6},{1,7},{2,4},{3,5},{4,2},{5,3},{6,0},{7,1},{8,14},{9,15},{10,... | collective-permute-start | bytes 393224 | tf_op jit(solution)/shard_map/ppermute | solution.py:337
  6.2 6.3 %collective-permute-start.1 = (bf16[128,512]{1,0:T(8,128)(2,1)S(1)}, bf16[128,512]{1,0:T(8,128)(2,1)S(1)}, u32[]{:S(2)}, u32[]{:S(2)}) collective-permute-start(bf16[128,512]{1,0:T(8,128)(2,1)S(1)} %get-tuple-element.26.refs_0_), channel_id=1, source_target_pairs={{0,4},{1,5},{2,6},{3,7},{4,0},{5,1},{6,2},{7,3},{8,12},{9,13},{10,... | collective-permute-start | bytes 393224 | tf_op jit(solution)/shard_map/ppermute | solution.py:337
  6.7 6.0 %collective-permute-start = (bf16[128,512]{1,0:T(8,128)(2,1)S(1)}, bf16[128,512]{1,0:T(8,128)(2,1)S(1)}, u32[]{:S(2)}, u32[]{:S(2)}) collective-permute-start(bf16[128,512]{1,0:T(8,128)(2,1)S(1)} %get-tuple-element.26.refs_0_), channel_id=1, source_target_pairs={{0,2},{1,3},{2,0},{3,1},{4,6},{5,7},{6,4},{7,5},{8,10},{9,11},{10,... | collective-permute-start | bytes 393224 | tf_op jit(solution)/shard_map/ppermute | solution.py:337
  6.9 8.5 %collective-permute-start.3 = (bf16[128,512]{1,0:T(8,128)(2,1)S(1)}, bf16[128,512]{1,0:T(8,128)(2,1)S(1)}, u32[]{:S(2)}, u32[]{:S(2)}) collective-permute-start(bf16[128,512]{1,0:T(8,128)(2,1)S(1)} %get-tuple-element.26.refs_0_), channel_id=1, source_target_pairs={{0,1},{1,0},{2,3},{3,2},{4,5},{5,4},{6,7},{7,6},{8,9},{9,8},{10,11... | collective-permute-start | bytes 393224 | tf_op jit(solution)/shard_map/ppermute | solution.py:337
  10.1 5.3 %collective-permute-start.6 = (bf16[128,512]{1,0:T(8,128)(2,1)S(1)}, bf16[128,512]{1,0:T(8,128)(2,1)S(1)}, u32[]{:S(2)}, u32[]{:S(2)}) collective-permute-start(bf16[128,512]{1,0:T(8,128)(2,1)S(1)} %collective-permute-done.2.refs_3_), channel_id=1, source_target_pairs={{0,1},{1,0},{2,3},{3,2},{4,5},{5,4},{6,7},{7,6},{8,9},{9,8},{10,11... | collective-permute-start | bytes 393224 | tf_op jit(solution)/shard_map/ppermute | solution.py:337
  12.5 2.9 %collective-permute-start.5 = (bf16[128,512]{1,0:T(8,128)(2,1)S(1)}, bf16[128,512]{1,0:T(8,128)(2,1)S(1)}, u32[]{:S(2)}, u32[]{:S(2)}) collective-permute-start(bf16[128,512]{1,0:T(8,128)(2,1)S(1)} %collective-permute-done.1.refs_2_), channel_id=1, source_target_pairs={{0,1},{1,0},{2,3},{3,2},{4,5},{5,4},{6,7},{7,6},{8,9},{9,8},{10,11... | collective-permute-start | bytes 393224 | tf_op jit(solution)/shard_map/ppermute | solution.py:337
  12.8 2.7 %collective-permute-start.4 = (bf16[128,512]{1,0:T(8,128)(2,1)S(1)}, bf16[128,512]{1,0:T(8,128)(2,1)S(1)}, u32[]{:S(2)}, u32[]{:S(2)}) collective-permute-start(bf16[128,512]{1,0:T(8,128)(2,1)S(1)} %collective-permute-done.refs_1_), channel_id=1, source_target_pairs={{0,1},{1,0},{2,3},{3,2},{4,5},{5,4},{6,7},{7,6},{8,9},{9,8},{10,11... | collective-permute-start | bytes 393224 | tf_op jit(solution)/shard_map/ppermute | solution.py:337
  19.2 3.9 %collective-permute-start.8 = (bf16[4,128,256]{2,1,0:T(8,128)(2,1)S(1)}, bf16[4,128,256]{2,1,0:T(8,128)(2,1)S(1)}, u32[]{:S(2)}, u32[]{:S(2)}) collective-permute-start(bf16[4,128,256]{2,1,0:T(8,128)(2,1)S(1)} %get-tuple-element.42), channel_id=1, source_target_pairs={{0,1},{1,0},{2,3},{3,2},{4,5},{5,4},{6,7},{7,6},{8,9},{9,8},{10,11... | collective-permute-start | bytes 786440 | tf_op jit(solution)/shard_map/ppermute | solution.py:337
  21.4 10.6 %collective-permute-start.7 = (bf16[128,1024]{1,0:T(8,128)(2,1)S(1)}, bf16[128,1024]{1,0:T(8,128)(2,1)S(1)}, u32[]{:S(2)}, u32[]{:S(2)}) collective-permute-start(bf16[128,1024]{1,0:T(8,128)(2,1)S(1)} %shard_map.116), channel_id=1, source_target_pairs={{24,0},{0,8},{8,16},{16,24},{25,1},{1,9},{9,17},{17,25},{26,2},{2,... | collective-permute-start | bytes 786440 | tf_op jit(solution)/shard_map/ppermute | solution.py:422
  23.1 9.6 %collective-permute-start.9 = (bf16[128,256]{1,0:T(8,128)(2,1)S(1)}, bf16[128,256]{1,0:T(8,128)(2,1)S(1)}, u32[]{:S(2)}, u32[]{:S(2)}) collective-permute-start(bf16[128,256]{1,0:T(8,128)(2,1)S(1)} %get-tuple-element.44), channel_id=1, source_target_pairs={{0,2},{1,3},{2,0},{3,1},{4,6},{5,7},{6,4},{7,5},{8,10},{9,11},{10,... | collective-permute-start | bytes 196616 | tf_op jit(solution)/shard_map/ppermute | solution.py:337
  24.7 8.0 %collective-permute-start.10 = (bf16[128,256]{1,0:T(8,128)(2,1)S(1)}, bf16[128,256]{1,0:T(8,128)(2,1)S(1)}, u32[]{:S(2)}, u32[]{:S(2)}) collective-permute-start(bf16[128,256]{1,0:T(8,128)(2,1)S(1)} %get-tuple-element.45), channel_id=1, source_target_pairs={{0,4},{1,5},{2,6},{3,7},{4,0},{5,1},{6,2},{7,3},{8,12},{9,13},{10,... | collective-permute-start | bytes 196616 | tf_op jit(solution)/shard_map/ppermute | solution.py:337
  25.5 7.3 %collective-permute-start.11 = (bf16[128,256]{1,0:T(8,128)(2,1)S(1)}, bf16[128,256]{1,0:T(8,128)(2,1)S(1)}, u32[]{:S(2)}, u32[]{:S(2)}) collective-permute-start(bf16[128,256]{1,0:T(8,128)(2,1)S(1)} %get-tuple-element.46), channel_id=1, source_target_pairs={{0,6},{1,7},{2,4},{3,5},{4,2},{5,3},{6,0},{7,1},{8,14},{9,15},{10,... | collective-permute-start | bytes 196616 | tf_op jit(solution)/shard_map/ppermute | solution.py:337
  33.2 7.9 %collective-permute-start.12 = (bf16[128,1024]{1,0:T(8,128)(2,1)S(1)}, bf16[128,1024]{1,0:T(8,128)(2,1)S(1)}, u32[]{:S(2)}, u32[]{:S(2)}) collective-permute-start(bf16[128,1024]{1,0:T(8,128)(2,1)S(1)} %shard_map.119), channel_id=1, source_target_pairs={{8,0},{16,8},{24,16},{0,24},{9,1},{17,9},{25,17},{1,25},{10,2},{18... | collective-permute-start | bytes 786440 | tf_op jit(solution)/shard_map/ppermute | solution.py:452

commit v4 on v3

--- a/solution.py
+++ b/solution.py
@@ -149,124 +149,184 @@
     spread_heads(dot(cot_ref[...], wo_ref[...], NT), dout_ref, 1.0)
 
 
-def score_block(keys, q_rows, bias_ref, s_ref, slot, lines, top):
-    block = dot(keys[lines], q_rows, NT)
-    bias = bias_ref[lines, :]
-    block = block + jnp.concatenate([bias, bias], axis=1)
-    s_ref[slot, lines, :] = block
-    part = jnp.max(block, axis=0, keepdims=True)
-    return part if top is None else jnp.maximum(top, part)
-
-
 def plus(left, right):
     return right if left is None else left + right
 
 
+def twice(bias):
+    return jnp.concatenate([bias, bias], axis=1)
+
+
+def score_block(keys, q_rows, bias):
+    return dot(keys, q_rows, NT) + twice(bias)
+
+
+def with_ones(values):
+    values_t = jnp.transpose(values)
+    ones = jnp.ones((16, values.shape[0]), BF16)
+    return [
+        jnp.concatenate([values_t[group * HEAD_DIM : (group + 1) * HEAD_DIM], ones], axis=0)
+        for group in range(KV_HEADS)
+    ]
+
+
+def late_chunks(count, rows):
+    half = count // 2
+    pieces = 3 if (half - 1) % 3 == 0 else 1
+    starts = list(range(1, half, pieces)) + list(range(half, count - 1, pieces))
+    return [slice(start * rows, (start + pieces) * rows) for start in starts]
+
+
+def attend_early(far_ref, own_ref, qf_ref, qb_ref, dout_ref, bias_ref, top_ref, mix_ref, stat_ref, e_ref, dp_ref):
+    rows = own_ref.shape[0]
+    pieces = jnp.concatenate([far_ref[...], own_ref[...]], axis=0)
+    bias = jnp.concatenate([bias_ref[:rows, :], bias_ref[-rows:, :]], axis=0)
+    extended = with_ones(pieces[:, KV_COLS : 2 * KV_COLS])
+    wide = 2 * rows
+    for pair in range(PAIRS):
+        cols = slice(pair * wide, (pair + 1) * wide)
+        block = score_block(pieces[:, :KV_COLS], qf_ref[cols, :], bias)
+        top = jnp.max(block, axis=0, keepdims=True)
+        top_ref[pair : pair + 1, :] = top
+        weights = jnp.exp(block - top).astype(BF16)
+        mix_ref[pair] = dot(extended[(2 * pair) // GROUP], weights)
+        block = score_block(pieces[:, 2 * KV_COLS : 3 * KV_COLS], qb_ref[cols, :], bias)
+        top = jnp.max(block, axis=0, keepdims=True)
+        weights = jnp.exp(block - top)
+        prob_grad = dot(pieces[:, 3 * KV_COLS :], dout_ref[cols, :], NT)
+        stat_ref[0:1, cols] = top
+        stat_ref[1:2, cols] = jnp.sum(weights, axis=0, keepdims=True)
+        stat_ref[2:3, cols] = jnp.sum(weights * prob_grad, axis=0, keepdims=True)
+        e_ref[:, cols] = weights.astype(BF16)
+        dp_ref[:, cols] = prob_grad
+
+
 def attend_backward(count, *refs):
-    pieces = refs[:count]
-    q_ref, dout_ref, bias_ref = refs[count : count + 3]
+    pieces = refs[: count - 2]
+    q_ref, dout_ref, bias_ref, far_ref, own_ref, stat_ref, e1_ref, dp1_ref = refs[count - 2 : count + 6]
+    odd_ref, u_ref, e_ref, qs_ref, ds_ref, keys_ref, rs_ref = refs[count + 6 : count + 13]
+    values_ref, s_ref, dp_ref, acc_ref = refs[count + 13 :]
+    rows = own_ref.shape[0]
+    total = rows * count
     half = count // 2
-    even_refs = refs[count + 3 : count + 3 + half]
-    odd_ref, dq_ref = refs[count + 3 + half : count + 5 + half]
-    kv_ref, s_ref, dp_ref, e_ref, acc_ref, dqt_ref = refs[count + 5 + half :]
-    rows = pieces[0].shape[0]
-    total = rows * count
-    chunk = min(4 * rows, total)
-    for place, piece in enumerate(pieces):
-        kv_ref[place * rows : (place + 1) * rows, :] = piece[:, 2 * KV_COLS :]
-    keys = kv_ref[:, :KV_COLS]
-    values = kv_ref[:, KV_COLS:]
-    keys_t = jnp.transpose(keys)
+    odd = slice(0, half * rows)
+    for place, piece in enumerate((far_ref, *pieces, own_ref)):
+        lines = slice(place * rows, (place + 1) * rows)
+        keys_ref[lines, :] = piece[:, 2 * KV_COLS : 3 * KV_COLS]
+        values_ref[lines, :] = piece[:, 3 * KV_COLS :]
     scale = 1.0 / math.sqrt(HEAD_DIM)
     wide = 2 * rows
+    chunks = late_chunks(count, rows)
     tops, stats, scaled = {}, {}, {}
     for step in range(-1, PAIRS + 1):
         ahead, now, behind = step + 1, step, step - 1
-        top = row_sum = mixed = query_grad = None
-        for first in range(0, total, chunk):
-            lines = slice(first, first + chunk)
+        top = row_sum = mixed = None
+        if behind >= 0:
+            cols = slice(behind * wide, (behind + 1) * wide)
+            delta, factor = stats[behind]
+            weights = e1_ref[:, cols].astype(F32) * factor
+            score_grad = (weights * (dp1_ref[:, cols] - delta)).astype(BF16)
+            weights = weights.astype(BF16)
+            for lines, part in ((slice(0, rows), slice(0, rows)), (slice(total - rows, total), slice(rows, wide))):
+                e_ref[lines, cols] = weights[part]
+                u_ref[lines, cols] = score_grad[part]
+        for lines in chunks:
+            if 0 <= now < PAIRS:
+                cols = slice(now * wide, (now + 1) * wide)
+                weights = jnp.exp(s_ref[now % 2, lines, :] - tops[now])
+                prob_grad = dot(values_ref[lines, :], dout_ref[cols, :], NT)
+                row_sum = plus(row_sum, jnp.sum(weights, axis=0, keepdims=True))
+                mixed = plus(mixed, jnp.sum(weights * prob_grad, axis=0, keepdims=True))
+                dp_ref[now % 2, lines, :] = prob_grad
+                e_ref[lines, cols] = weights.astype(BF16)
             if ahead < PAIRS:
                 q_rows = q_ref[ahead * wide : (ahead + 1) * wide, :]
-                top = score_block(keys, q_rows, bias_ref, s_ref, ahead % 2, lines, top)
-            if 0 <= now < PAIRS:
-                slot = now % 2
-                weights = jnp.exp(s_ref[slot, lines, :] - tops[now])
-                prob_grad = dot(values[lines], dout_ref[now * wide : (now + 1) * wide, :], NT)
-                row_sum = plus(row_sum, jnp.sum(weights, axis=0, keepdims=True))
-                mixed = plus(mixed, jnp.sum(weights * prob_grad, axis=0, keepdims=True))
-                dp_ref[slot, lines, :] = prob_grad
-                e_ref[slot, lines, :] = weights.astype(BF16)
+                block = score_block(keys_ref[lines, :], q_rows, bias_ref[lines, :])
+                s_ref[ahead % 2, lines, :] = block
+                part = jnp.max(block, axis=0, keepdims=True)
+                top = part if top is None else jnp.maximum(top, part)
             if behind >= 0:
-                slot = behind % 2
-                weights = e_ref[slot, lines, :]
-                score_grad = weights * (dp_ref[slot, lines, :] - stats[behind][1]).astype(BF16)
-                group = (2 * behind) // GROUP
-                own = slice(group * HEAD_DIM, (group + 1) * HEAD_DIM)
-                query_grad = plus(query_grad, dot(keys_t[own, lines], score_grad))
-                key_grad = dot(score_grad, scaled[behind][0])
-                value_grad = dot(weights, scaled[behind][1])
-                if behind:
-                    key_grad = key_grad + acc_ref[lines, :KV_COLS]
-                    value_grad = value_grad + acc_ref[lines, KV_COLS:]
-                if behind < PAIRS - 1:
-                    acc_ref[lines, :KV_COLS] = key_grad
-                    acc_ref[lines, KV_COLS:] = value_grad
-                else:
-                    for place in range(first // rows, (first + chunk) // rows):
-                        target = even_refs[place] if place < half else odd_ref.at[place - half]
-                        inner = slice(place * rows - first, (place + 1) * rows - first)
-                        target[:, :KV_COLS] = key_grad[inner].astype(BF16)
-                        target[:, KV_COLS:] = value_grad[inner].astype(BF16)
+                cols = slice(behind * wide, (behind + 1) * wide)
+                difference = (dp_ref[behind % 2, lines, :] - stats[behind][0]).astype(BF16)
+                u_ref[lines, cols] = e_ref[lines, cols] * difference
+                if lines.stop == odd.stop:
+                    key_grad = dot(u_ref[odd, cols], scaled[behind][0])
+                    value_grad = dot(e_ref[odd, cols], scaled[behind][1])
+                    if behind:
+                        key_grad = key_grad + acc_ref[:, :KV_COLS]
+                        value_grad = value_grad + acc_ref[:, KV_COLS:]
+                    if behind < PAIRS - 1:
+                        acc_ref[:, :KV_COLS] = key_grad
+                        acc_ref[:, KV_COLS:] = value_grad
+                    else:
+                        for place in range(half):
+                            inner = slice(place * rows, (place + 1) * rows)
+                            odd_ref[place, :, :KV_COLS] = key_grad[inner].astype(BF16)
+                            odd_ref[place, :, KV_COLS:] = value_grad[inner].astype(BF16)
         if ahead < PAIRS:
-            tops[ahead] = top
+            tops[ahead] = jnp.maximum(top, stat_ref[0:1, ahead * wide : (ahead + 1) * wide])
         if 0 <= now < PAIRS:
-            inverse_sum = 1.0 / row_sum
-            stats[now] = (inverse_sum, mixed * inverse_sum)
             cols = slice(now * wide, (now + 1) * wide)
-            factor = jnp.transpose(jnp.broadcast_to(inverse_sum, (KV_COLS, wide)))
+            factor = jnp.exp(stat_ref[0:1, cols] - tops[now])
+            inverse_sum = 1.0 / (row_sum + factor * stat_ref[1:2, cols])
+            stats[now] = ((mixed + factor * stat_ref[2:3, cols]) * inverse_sum, factor)
+            rs_ref[0:1, cols] = inverse_sum * scale
+            column = jnp.transpose(jnp.broadcast_to(inverse_sum, (KV_COLS, wide)))
             scaled[now] = (
-                (q_ref[cols, :].astype(F32) * factor).astype(BF16),
-                (dout_ref[cols, :].astype(F32) * factor).astype(BF16),
+                (q_ref[cols, :].astype(F32) * column).astype(BF16),
+                (dout_ref[cols, :].astype(F32) * column).astype(BF16),
             )
-        if behind >= 0:
-            part = query_grad * (stats[behind][0] * scale)
-            dqt_ref[2 * behind * HEAD_DIM : (2 * behind + 1) * HEAD_DIM, :] = part[:, :rows]
-            dqt_ref[(2 * behind + 1) * HEAD_DIM : (2 * behind + 2) * HEAD_DIM, :] = part[:, rows:]
+            qs_ref[cols, :], ds_ref[cols, :] = scaled[now]
+
+
+def finish_backward(u_ref, e_ref, qs_ref, ds_ref, keys_ref, rs_ref, *refs):
+    even_refs, dq_ref, dqt_ref = refs[:-2], refs[-2], refs[-1]
+    rows = even_refs[0].shape[0]
+    even = slice(len(even_refs) * rows, 2 * len(even_refs) * rows)
+    wide = 2 * rows
+    key_grad = dot(u_ref[even, :], qs_ref[...]).astype(BF16)
+    value_grad = dot(e_ref[even, :], ds_ref[...]).astype(BF16)
+    for place, target in enumerate(even_refs):
+        target[:, :KV_COLS] = key_grad[place * rows : (place + 1) * rows]
+        target[:, KV_COLS:] = value_grad[place * rows : (place + 1) * rows]
+    keys_t = jnp.transpose(keys_ref[...])
+    for pair in range(PAIRS):
+        group = (2 * pair) // GROUP
+        cols = slice(pair * wide, (pair + 1) * wide)
+        part = dot(keys_t[group * HEAD_DIM : (group + 1) * HEAD_DIM], u_ref[:, cols]) * rs_ref[0:1, cols]
+        dqt_ref[2 * pair * HEAD_DIM : (2 * pair + 1) * HEAD_DIM, :] = part[:, :rows]
+        dqt_ref[(2 * pair + 1) * HEAD_DIM : (2 * pair + 2) * HEAD_DIM, :] = part[:, rows:]
     dq_ref[...] = jnp.transpose(dqt_ref[...]).astype(BF16)
 
 
 def attend_forward(count, *refs):
-    pieces = refs[:count]
-    q_ref, bias_ref, x_ref, wo_ref, out_ref = refs[count : count + 5]
+    pieces = refs[: count - 2]
+    q_ref, bias_ref, x_ref, wo_ref, top_ref, mix_ref, out_ref = refs[count - 2 : count + 5]
     kv_ref, s_ref, at_ref = refs[count + 5 :]
     rows = pieces[0].shape[0]
-    total = rows * count
-    chunk = min(4 * rows, total)
     for place, piece in enumerate(pieces):
-        kv_ref[place * rows : (place + 1) * rows, :] = piece[:, : 2 * KV_COLS]
-    keys = kv_ref[:, :KV_COLS]
-    values_t = jnp.transpose(kv_ref[:, KV_COLS:])
-    ones = jnp.ones((16, total), BF16)
-    extended = [
-        jnp.concatenate([values_t[group * HEAD_DIM : (group + 1) * HEAD_DIM], ones], axis=0)
-        for group in range(KV_HEADS)
-    ]
+        kv_ref[(place + 1) * rows : (place + 2) * rows, :] = piece[:, : 2 * KV_COLS]
+    chunks = late_chunks(count, rows)
+    extended = [with_ones(kv_ref[lines, KV_COLS:]) for lines in chunks]
     wide = 2 * rows
     tops = {}
     for now in range(-1, PAIRS):
         ahead = now + 1
         top = mixed = None
-        for first in range(0, total, chunk):
-            lines = slice(first, first + chunk)
+        for place, lines in enumerate(chunks):
             if ahead < PAIRS:
                 q_rows = q_ref[ahead * wide : (ahead + 1) * wide, :]
-                top = score_block(keys, q_rows, bias_ref, s_ref, ahead % 2, lines, top)
+                block = score_block(kv_ref[lines, :KV_COLS], q_rows, bias_ref[lines, :])
+                s_ref[ahead % 2, lines, :] = block
+                part = jnp.max(block, axis=0, keepdims=True)
+                top = part if top is None else jnp.maximum(top, part)
             if now >= 0:
-                weights = jnp.exp(s_ref[now % 2, lines, :] - tops[now])
-                mixed = plus(mixed, dot(extended[(2 * now) // GROUP][:, lines], weights.astype(BF16)))
+                weights = jnp.exp(s_ref[now % 2, lines, :] - tops[now]).astype(BF16)
+                mixed = plus(mixed, dot(extended[place][(2 * now) // GROUP], weights))
         if ahead < PAIRS:
-            tops[ahead] = top
+            tops[ahead] = jnp.maximum(top, top_ref[ahead : ahead + 1, :])
         if now >= 0:
+            mixed = mixed + mix_ref[now] * jnp.exp(top_ref[now : now + 1, :] - tops[now])
             part = mixed[:HEAD_DIM] * (1.0 / mixed[HEAD_DIM : HEAD_DIM + 1])
             at_ref[2 * now * HEAD_DIM : (2 * now + 1) * HEAD_DIM, :] = part[:, :rows]
             at_ref[(2 * now + 1) * HEAD_DIM : (2 * now + 2) * HEAD_DIM, :] = part[:, rows:]
@@ -284,7 +344,7 @@
 def add_pieces(count, *refs):
     for place in range(count):
         left = refs[place][...].astype(F32)
-        refs[count + 1 + place][...] = (left + refs[count][place].astype(F32)).astype(BF16)
+        refs[count + 1 + place][...] = (left + refs[count][(place + 1) % count].astype(F32)).astype(BF16)
 
 
 def input_back(count, *refs):
@@ -338,11 +398,11 @@
 
 
 def order_of(size):
-    return list(range(0, size, 2)) + list(range(1, size, 2))
+    return list(range(1, size, 2)) + list(range(2, size, 2)) + [0]
 
 
 def by_permutes(size):
-    return size in (2, 4, 8)
+    return size in (4, 8)
 
 
 def gather_near(block, size):
@@ -355,7 +415,8 @@
     if not by_permutes(size):
         me = lax.axis_index("seq")
         return [lax.dynamic_index_in_dim(near, me ^ step, 0, False) for step in order_of(size)]
-    return near + [swap(piece, 1, size) for piece in near]
+    far = [swap(piece, 1, size) for piece in near]
+    return far + near[1:] + near[:1]
 
 
 def on_device(
@@ -409,10 +470,21 @@
         hbm=5,
     )
     pieces = gather_far(near, size)
+    top, mix, stat, early, early_dp = call(
+        attend_early,
+        (
+            shape((PAIRS, wide), F32),
+            shape((PAIRS, HEAD_DIM + 16, wide), F32),
+            shape((8, HEADS * rows), F32),
+            shape((wide, HEADS * rows), BF16),
+            shape((wide, HEADS * rows), F32),
+        ),
+        (pieces[0], pieces[-1], qf, qb, dout, bias),
+    )
     layer_out = call(
         partial(attend_forward, size),
         shape((rows, width), BF16),
-        (*pieces, qf, bias, xf, wo),
+        (*pieces[1:-1], qf, bias, xf, wo, top, mix),
         scratch=(
             pltpu.VMEM((total, 2 * KV_COLS), BF16),
             pltpu.VMEM((2, total, wide), F32),
@@ -420,26 +492,37 @@
         ),
     )
     shifted = lax.ppermute(layer_out, "section", [((i - 1) % sections, i) for i in range(sections)])
-    *grads, dq = call(
+    odd, *later = call(
         partial(attend_backward, size),
-        (kv_shape,) * half + (shape((half, rows, 2 * KV_COLS), BF16), shape((rows, HEADS * HEAD_DIM), BF16)),
-        (*pieces, qb, dout, bias),
+        (
+            shape((half, rows, 2 * KV_COLS), BF16),
+            shape((total, HEADS * rows), BF16),
+            shape((total, HEADS * rows), BF16),
+            spread,
+            spread,
+            shape((total, KV_COLS), BF16),
+            shape((8, HEADS * rows), F32),
+        ),
+        (*pieces[1:-1], qb, dout, bias, pieces[0], pieces[-1], stat, early, early_dp),
         scratch=(
-            pltpu.VMEM((total, 2 * KV_COLS), BF16),
+            pltpu.VMEM((total, KV_COLS), BF16),
             pltpu.VMEM((2, total, wide), F32),
             pltpu.VMEM((2, total, wide), F32),
-            pltpu.VMEM((2, total, wide), BF16),
-            pltpu.VMEM((total, 2 * KV_COLS), F32),
-            pltpu.VMEM((HEADS * HEAD_DIM, rows), F32),
+            pltpu.VMEM((half * rows, 2 * KV_COLS), F32),
         ),
     )
-    even, odd = grads[:half], grads[half]
+    *even, dq = call(
+        finish_backward,
+        (kv_shape,) * half + (shape((rows, HEADS * HEAD_DIM), BF16),),
+        later,
+        scratch=(pltpu.VMEM((HEADS * HEAD_DIM, rows), F32),),
+    )
     if by_permutes(size):
         other = swap(odd, 1, size)
         sums = call(partial(add_pieces, half), (kv_shape,) * half, (*even, other))
-        received = [sums[0]] + [swap(sums[i], 2 * i, size) for i in range(1, half)]
+        received = [sums[-1]] + [swap(sums[i], 2 * i + 2, size) for i in range(half - 1)]
     else:
-        both = jnp.stack(list(even) + [odd[i] for i in range(half)]).astype(F32)
+        both = jnp.stack([odd[i] for i in range(half)] + list(even)).astype(F32)
         places = jnp.argsort(jnp.array(order, jnp.int32) ^ lax.axis_index("seq"))
         summed = lax.psum_scatter(both[places], "seq", scatter_dimension=0, tiled=True)
         received = [summed[0].astype(BF16)]

time: 42 us -> 43.1 us (1.026)
  Pallas kernels: 10.8 us -> 13.1 us
  waiting for transfers between devices: 17.4 us -> 16.3 us
    pallas_call x7 -> x9, Pallas kernels: 10.8 us -> 13.1 us  [call(): pl.pallas_call(kernel, out_shape=[pltpu.VMEM(out.shape, out.dtype) for ou...]
    ppermute x1, waiting for transfers between devices: 5.33 us -> 4.2 us  [on_device(): lax.ppermute(layer_out, 'section', [((i - 1) % sections, i) for i in rang...]
  transfers between devices with their start and end apart: 13 -> 13, of which waited for: 5 -> 5; matrix products, arithmetic and copies ran while one was open for 0% -> 0% of each run, Pallas kernels for 12% -> 18%
where the time goes in v4:
time: 43.1 us; the launch traced here: 43 us
  waiting for transfers between devices  16.3 us (38%)
  Pallas kernels  13.1 us (30%)
  starting transfers between devices  12.2 us (28%)
  between operations  0.76 us (2%)
  local copies, waits for them, and re-layouts  0.7 us (2%)
    pallas_call x9, Pallas kernels, call(): pl.pallas_call(kernel, out_shape=[pltpu.VMEM(out.shape, out.dtype) for ou...  13.1 us
    ppermute x11, starting transfers between devices, swap(): return lax.ppermute(block, 'seq', [(i, i ^ step) for i in range(size)])  8.77 us
    ppermute x1, waiting for transfers between devices, on_device(): lax.ppermute(input_grad, 'section', [((i + 1) % sections, i) for i in ran...  6.14 us
    ppermute x11, waiting for transfers between devices, swap(): return lax.ppermute(block, 'seq', [(i, i ^ step) for i in range(size)])  5.92 us
    ppermute x1, waiting for transfers between devices, on_device(): lax.ppermute(layer_out, 'section', [((i - 1) % sections, i) for i in rang...  4.2 us
    ppermute x1, starting transfers between devices, on_device(): lax.ppermute(input_grad, 'section', [((i + 1) % sections, i) for i in ran...  1.79 us
    ppermute x1, starting transfers between devices, on_device(): lax.ppermute(layer_out, 'section', [((i - 1) % sections, i) for i in rang...  1.62 us
  transfers between devices with their start and end apart: 13, of which 5 were waited for; matrix products, arithmetic and copies ran while one was open for 0% of the time, Pallas kernels for 18%

profile of v4, /device:TPU:0, one launch (start us, length us, event | category | flops | bytes accessed | tf_op | source)
XLA Modules:
  0.0 43.0 jit_solution(12219666087773827766)
XLA Ops:
  0.6 1.6 %shard_map.113 = (bf16[128,512]{1,0:T(8,128)(2,1)S(1)}, f32[1,1024]{1,0:T(1,128)S(1)}, bf16[128,1024]{1,0:T(8,128)(2,1)S(1)}, bf16[128,1024]{1,0:T(8,128)(2,1)S(1)}, bf16[1024,256]{1,0:T(8,128)(2,1)S(1)}) custom-call(f32[1,1024]{1,0:T(1,128)} %gain_hbm.1, bf16[128,1024]{1,0:T(8,128)(2,1)} %bitcast.14, bf16[128,1024]{1,0:T(8,128)(2,1)} %bitcast.15, ...), custom_call_target="tpu_custom_call" | custom-call | tf_op jit(solution)/shard_map/pallas_call | solution.py:383
  2.3 4.0 %collective-permute-start.4 = (bf16[128,512]{1,0:T(8,128)(2,1)S(1)}, bf16[128,512]{1,0:T(8,128)(2,1)S(1)}, u32[]{:S(2)}, u32[]{:S(2)}) collective-permute-start(bf16[128,512]{1,0:T(8,128)(2,1)S(1)} %get-tuple-element.37.own_ref.refs_10_), channel_id=1, source_target_pairs={{0,6},{1,7},{2,4},{3,5},{4,2},{5,3},{6,0},{7,1},{8,14},{9,15},{10,... | collective-permute-start | bytes 393224 | tf_op jit(solution)/shard_map/ppermute | solution.py:397
  6.2 0.5 %collective-permute-start.2 = (bf16[128,512]{1,0:T(8,128)(2,1)S(1)}, bf16[128,512]{1,0:T(8,128)(2,1)S(1)}, u32[]{:S(2)}, u32[]{:S(2)}) collective-permute-start(bf16[128,512]{1,0:T(8,128)(2,1)S(1)} %get-tuple-element.37.own_ref.refs_10_), channel_id=1, source_target_pairs={{0,4},{1,5},{2,6},{3,7},{4,0},{5,1},{6,2},{7,3},{8,12},{9,13},{10,... | collective-permute-start | bytes 393224 | tf_op jit(solution)/shard_map/ppermute | solution.py:397
  6.7 0.1 collective-permute-start
  6.9 0.0 collective-permute-start.6
  6.9 3.2 %collective-permute-done.4.refs_5_ = bf16[128,512]{1,0:T(8,128)(2,1)S(1)} collective-permute-done((bf16[128,512]{1,0:T(8,128)(2,1)S(1)}, bf16[128,512]{1,0:T(8,128)(2,1)S(1)}, u32[]{:S(2)}, u32[]{:S(2)}) %collective-permute-start.4) | collective-permute-done | bytes 131104 | tf_op jit(solution)/shard_map/ppermute | solution.py:397
  10.1 0.0 collective-permute-start.5
  10.1 2.4 %collective-permute-done.2.refs_4_ = bf16[128,512]{1,0:T(8,128)(2,1)S(1)} collective-permute-done((bf16[128,512]{1,0:T(8,128)(2,1)S(1)}, bf16[128,512]{1,0:T(8,128)(2,1)S(1)}, u32[]{:S(2)}, u32[]{:S(2)}) %collective-permute-start.2) | collective-permute-done | bytes 131104 | tf_op jit(solution)/shard_map/ppermute | solution.py:397
  12.5 0.0 collective-permute-start.3
  12.5 0.2 collective-permute-done.refs_3_
  12.8 0.3 collective-permute-start.1
  13.1 2.6 %shard_map.114 = (bf16[1024,128]{1,0:T(8,128)(2,1)S(1)}, bf16[1024,128]{1,0:T(8,128)(2,1)S(1)}, bf16[1024,128]{1,0:T(8,128)(2,1)S(1)}, f32[1024,128]{1,0:T(8,128...) custom-call(s32[1]{0:T(128)} %bitcast.4.me_ref, ...), custom_call_target="tpu_custom_call" | custom-call | tf_op jit(solution)/shard_map/pallas_call | solution.py:383
  15.6 0.0 collective-permute-done.6.far_ref.refs_9_
  15.6 1.7 %shard_map.115 = (f32[4,256]{1,0:T(4,128)S(1)}, f32[4,80,256]{2,1,0:T(8,128)S(1)}, f32[8,1024]{1,0:T(8,128)S(1)}, bf16[256,1024]{1,0:T(8,128)(2,1)S(1)}, f32[256,1024]{1,0:T(8,128)S(1)}) custom-call(bf16[128,512]{1,0:T(8,128)(2,1)S(1)} %collective-permute-done.6.far_ref.refs_9_, bf16[128,512]{1,0:T(8,128)(2,1)S(1)} %get-tuple-element.37.own_ref.refs_10_, ...), custom_call_target="tpu_custom_call" | custom-call | tf_op jit(solution)/shard_map/pallas_call | solution.py:383
  17.4 0.0 collective-permute-done.5.refs_2_
  17.4 0.0 collective-permute-done.3.refs_1_
  17.4 0.0 collective-permute-done.1.refs_0_
  17.4 3.2 %shard_map.116 = (bf16[4,128,256]{2,1,0:T(8,128)(2,1)S(1)}, bf16[1024,1024]{1,0:T(8,128)(2,1)S(1)}, bf16[1024,1024]{1,0:T(8,128)(2,1)S(1)}, bf16[1024,128]{1,0:T...) custom-call(bf16[128,512]{1,0:T(8,128)(2,1)S(1)} %collective-permute-done.1.re, ...), custom_call_target="tpu_custom_call" | custom-call | tf_op jit(solution)/shard_map/pallas_call | solution.py:383
  20.6 0.3 collective-permute-start.8
  20.9 1.7 %shard_map.118 = bf16[128,1024]{1,0:T(8,128)(2,1)S(1)} custom-call(bf16[128,512]{1,0:T(8,128)(2,1)S(1)} %collective-permute-done.1.refs_0_, bf16[128,512]{1,0:T(8,128)(2,1)S(1)} %collective-permute-done.3.refs_1_, bf16[128,512]{1,0:T(8,128)(2,1)S(1)} %collective-permute-done.5.refs_2_, bf16[128,512]{1,0:T(8,128)(2,1)S(1)} %collective-permute-done.refs_3_, ...), custom_call_target="tpu_custom_call" | custom-call | tf_op jit(solution)/shard_map/pallas_call | solution.py:383
  22.6 1.6 %collective-permute-start.7 = (bf16[128,1024]{1,0:T(8,128)(2,1)S(1)}, bf16[128,1024]{1,0:T(8,128)(2,1)S(1)}, u32[]{:S(2)}, u32[]{:S(2)}) collective-permute-start(bf16[128,1024]{1,0:T(8,128)(2,1)S(1)} %shard_map.118), channel_id=1, source_target_pairs={{24,0},{0,8},{8,16},{16,24},{25,1},{1,9},{9,17},{17,25},{26,2},{2,... | collective-permute-start | bytes 786440 | tf_op jit(solution)/shard_map/ppermute | solution.py:494
  24.2 1.1 %shard_map.117 = (bf16[128,256]{1,0:T(8,128)(2,1)S(1)}, bf16[128,256]{1,0:T(8,128)(2,1)S(1)}, bf16[128,256]{1,0:T(8,128)(2,1)S(1)}, bf16[128,256]{1,0:T(8,128)(2,1)S(1)}, bf16[128,512]{1,0:T(8,128)(2,1)S(1)}) custom-call(bf16[1024,1024]{1,0:T(8,128)(2,1)S(1)} %get-tuple-element.48.u_ref, bf16[1024,1024]{1,0:T(8,128)(2,1)S(1)} %get-tuple-element.49.e_ref, ...), custom_call_target="tpu_custom_call" | custom-call | tf_op jit(solution)/shard_map/pallas_call | solution.py:383
  25.3 0.0 collective-permute-done.8.refs_4_
  25.3 0.1 shard_map.120
  25.4 1.6 %collective-permute-start.9 = (bf16[128,256]{1,0:T(8,128)(2,1)S(1)}, bf16[128,256]{1,0:T(8,128)(2,1)S(1)}, u32[]{:S(2)}, u32[]{:S(2)}) collective-permute-start(bf16[128,256]{1,0:T(8,128)(2,1)S(1)} %get-tuple-element.66), channel_id=1, source_target_pairs={{0,2},{1,3},{2,0},{3,1},{4,6},{5,7},{6,4},{7,5},{8,10},{9,11},{10,... | collective-permute-start | bytes 196616 | tf_op jit(solution)/shard_map/ppermute | solution.py:397
  27.0 0.7 %collective-permute-start.10 = (bf16[128,256]{1,0:T(8,128)(2,1)S(1)}, bf16[128,256]{1,0:T(8,128)(2,1)S(1)}, u32[]{:S(2)}, u32[]{:S(2)}) collective-permute-start(bf16[128,256]{1,0:T(8,128)(2,1)S(1)} %get-tuple-element.67), channel_id=1, source_target_pairs={{0,4},{1,5},{2,6},{3,7},{4,0},{5,1},{6,2},{7,3},{8,12},{9,13},{10,... | collective-permute-start | bytes 196616 | tf_op jit(solution)/shard_map/ppermute | solution.py:397
  27.7 1.2 %collective-permute-start.11 = (bf16[128,256]{1,0:T(8,128)(2,1)S(1)}, bf16[128,256]{1,0:T(8,128)(2,1)S(1)}, u32[]{:S(2)}, u32[]{:S(2)}) collective-permute-start(bf16[128,256]{1,0:T(8,128)(2,1)S(1)} %get-tuple-element.68), channel_id=1, source_target_pairs={{0,6},{1,7},{2,4},{3,5},{4,2},{5,3},{6,0},{7,1},{8,14},{9,15},{10,... | collective-permute-start | bytes 196616 | tf_op jit(solution)/shard_map/ppermute | solution.py:397
  28.9 4.2 %collective-permute-done.7.next_ref = bf16[128,1024]{1,0:T(8,128)(2,1)S(1)} collective-permute-done((bf16[128,1024]{1,0:T(8,128)(2,1)S(1)}, bf16[128,1024]{1,0:T(8,128)(2,1)S(1)}, u32[]{:S(2)}, u32[]{:S(2)}) %collective-permute-start.7) | collective-permute-done | bytes 262176 | tf_op jit(solution)/shard_map/ppermute | solution.py:494
  33.2 0.7 %shard_map.119 = (f32[128,1024]{1,0:T(8,128)S(1)}, bf16[128,1024]{1,0:T(8,128)(2,1)}) custom-call(bf16[128,512]{1,0:T(8,128)(2,1)S(1)} %get-tuple-element.54.dq_ref, bf16[1024,512]{1,0:T(8,128)(2,1)S(1)} %get-tuple-element.55.wq_ref, bf16[128,1024]{1,0:T(8,128)(2,1)S(1)} %collective-permute-done.7.next_ref), custom_call_target="tpu_custom_call" | custom-call | tf_op jit(solution)/shard_map/pallas_call | solution.py:383
  33.9 0.0 collective-permute-done.9.refs_1_
  33.9 0.0 collective-permute-done.10.refs_2_
  33.9 0.0 collective-permute-done.11.refs_3_
  33.9 0.4 %shard_map.121 = bf16[128,1024]{1,0:T(8,128)(2,1)S(1)} custom-call(bf16[128,256]{1,0:T(8,128)(2,1)S(1)} %get-tuple-element.65.refs_0_, bf16[128,256]{1,0:T(8,128)(2,1)S(1)} %collective-permute-done.9.refs_1_, bf16[128,256]{1,0:T(8,128)(2,1)S(1)} %collective-permute-done.10.refs_2_, bf16[128,256]{1,0:T(8,128)(2,1)S(1)} %collective-permute-done.11.refs_3_, ...), custom_call_target="tpu_custom_call" | custom-call | tf_op jit(solution)/shard_map/pallas_call | solution.py:383
  34.3 1.8 %collective-permute-start.12 = (bf16[128,1024]{1,0:T(8,128)(2,1)S(1)}, bf16[128,1024]{1,0:T(8,128)(2,1)S(1)}, u32[]{:S(2)}, u32[]{:S(2)}) collective-permute-start(bf16[128,1024]{1,0:T(8,128)(2,1)S(1)} %shard_map.121), channel_id=1, source_target_pairs={{8,0},{16,8},{24,16},{0,24},{9,1},{17,9},{25,17},{1,25},{10,2},{18... | collective-permute-start | bytes 786440 | tf_op jit(solution)/shard_map/ppermute | solution.py:535
  36.1 6.1 %collective-permute-done.12 = bf16[128,1024]{1,0:T(8,128)(2,1)S(1)} collective-permute-done((bf16[128,1024]{1,0:T(8,128)(2,1)S(1)}, bf16[128,1024]{1,0:T(8,128)(2,1)S(1)}, u32[]{:S(2)}, u32[]{:S(2)}) %collective-permute-start.12) | collective-permute-done | bytes 262176 | tf_op jit(solution)/shard_map/ppermute | solution.py:535
  42.3 0.7 %copy.13 = bf16[1,128,1024]{2,1,0:T(8,128)(2,1)} copy(bf16[1,128,1024]{2,1,0:T(8,128)(2,1)S(1)} %bitcast.13) | data formatting | bytes 524288
Async XLA Ops:
  2.3 7.9 %collective-permute-start.4 = (bf16[128,512]{1,0:T(8,128)(2,1)S(1)}, bf16[128,512]{1,0:T(8,128)(2,1)S(1)}, u32[]{:S(2)}, u32[]{:S(2)}) collective-permute-start(bf16[128,512]{1,0:T(8,128)(2,1)S(1)} %get-tuple-element.37.own_ref.refs_10_), channel_id=1, source_target_pairs={{0,6},{1,7},{2,4},{3,5},{4,2},{5,3},{6,0},{7,1},{8,14},{9,15},{10,... | collective-permute-start | bytes 393224 | tf_op jit(solution)/shard_map/ppermute | solution.py:397
  6.2 6.3 %collective-permute-start.2 = (bf16[128,512]{1,0:T(8,128)(2,1)S(1)}, bf16[128,512]{1,0:T(8,128)(2,1)S(1)}, u32[]{:S(2)}, u32[]{:S(2)}) collective-permute-start(bf16[128,512]{1,0:T(8,128)(2,1)S(1)} %get-tuple-element.37.own_ref.refs_10_), channel_id=1, source_target_pairs={{0,4},{1,5},{2,6},{3,7},{4,0},{5,1},{6,2},{7,3},{8,12},{9,13},{10,... | collective-permute-start | bytes 393224 | tf_op jit(solution)/shard_map/ppermute | solution.py:397
  6.7 6.0 %collective-permute-start = (bf16[128,512]{1,0:T(8,128)(2,1)S(1)}, bf16[128,512]{1,0:T(8,128)(2,1)S(1)}, u32[]{:S(2)}, u32[]{:S(2)}) collective-permute-start(bf16[128,512]{1,0:T(8,128)(2,1)S(1)} %get-tuple-element.37.own_ref.refs_10_), channel_id=1, source_target_pairs={{0,2},{1,3},{2,0},{3,1},{4,6},{5,7},{6,4},{7,5},{8,10},{9,11},{10,... | collective-permute-start | bytes 393224 | tf_op jit(solution)/shard_map/ppermute | solution.py:397
  6.9 8.8 %collective-permute-start.6 = (bf16[128,512]{1,0:T(8,128)(2,1)S(1)}, bf16[128,512]{1,0:T(8,128)(2,1)S(1)}, u32[]{:S(2)}, u32[]{:S(2)}) collective-permute-start(bf16[128,512]{1,0:T(8,128)(2,1)S(1)} %get-tuple-element.37.own_ref.refs_10_), channel_id=1, source_target_pairs={{0,1},{1,0},{2,3},{3,2},{4,5},{5,4},{6,7},{7,6},{8,9},{9,8},{10,11... | collective-permute-start | bytes 393224 | tf_op jit(solution)/shard_map/ppermute | solution.py:397
  10.1 7.2 %collective-permute-start.5 = (bf16[128,512]{1,0:T(8,128)(2,1)S(1)}, bf16[128,512]{1,0:T(8,128)(2,1)S(1)}, u32[]{:S(2)}, u32[]{:S(2)}) collective-permute-start(bf16[128,512]{1,0:T(8,128)(2,1)S(1)} %collective-permute-done.4.refs_5_), channel_id=1, source_target_pairs={{0,1},{1,0},{2,3},{3,2},{4,5},{5,4},{6,7},{7,6},{8,9},{9,8},{10,11... | collective-permute-start | bytes 393224 | tf_op jit(solution)/shard_map/ppermute | solution.py:397
  12.5 4.8 %collective-permute-start.3 = (bf16[128,512]{1,0:T(8,128)(2,1)S(1)}, bf16[128,512]{1,0:T(8,128)(2,1)S(1)}, u32[]{:S(2)}, u32[]{:S(2)}) collective-permute-start(bf16[128,512]{1,0:T(8,128)(2,1)S(1)} %collective-permute-done.2.refs_4_), channel_id=1, source_target_pairs={{0,1},{1,0},{2,3},{3,2},{4,5},{5,4},{6,7},{7,6},{8,9},{9,8},{10,11... | collective-permute-start | bytes 393224 | tf_op jit(solution)/shard_map/ppermute | solution.py:397
  12.8 4.6 %collective-permute-start.1 = (bf16[128,512]{1,0:T(8,128)(2,1)S(1)}, bf16[128,512]{1,0:T(8,128)(2,1)S(1)}, u32[]{:S(2)}, u32[]{:S(2)}) collective-permute-start(bf16[128,512]{1,0:T(8,128)(2,1)S(1)} %collective-permute-done.refs_3_), channel_id=1, source_target_pairs={{0,1},{1,0},{2,3},{3,2},{4,5},{5,4},{6,7},{7,6},{8,9},{9,8},{10,11... | collective-permute-start | bytes 393224 | tf_op jit(solution)/shard_map/ppermute | solution.py:397
  20.6 4.7 %collective-permute-start.8 = (bf16[4,128,256]{2,1,0:T(8,128)(2,1)S(1)}, bf16[4,128,256]{2,1,0:T(8,128)(2,1)S(1)}, u32[]{:S(2)}, u32[]{:S(2)}) collective-permute-start(bf16[4,128,256]{2,1,0:T(8,128)(2,1)S(1)} %get-tuple-element.64), channel_id=1, source_target_pairs={{0,1},{1,0},{2,3},{3,2},{4,5},{5,4},{6,7},{7,6},{8,9},{9,8},{10,11... | collective-permute-start | bytes 786440 | tf_op jit(solution)/shard_map/ppermute | solution.py:397
  22.6 10.6 %collective-permute-start.7 = (bf16[128,1024]{1,0:T(8,128)(2,1)S(1)}, bf16[128,1024]{1,0:T(8,128)(2,1)S(1)}, u32[]{:S(2)}, u32[]{:S(2)}) collective-permute-start(bf16[128,1024]{1,0:T(8,128)(2,1)S(1)} %shard_map.118), channel_id=1, source_target_pairs={{24,0},{0,8},{8,16},{16,24},{25,1},{1,9},{9,17},{17,25},{26,2},{2,... | collective-permute-start | bytes 786440 | tf_op jit(solution)/shard_map/ppermute | solution.py:494
  25.4 8.5 %collective-permute-start.9 = (bf16[128,256]{1,0:T(8,128)(2,1)S(1)}, bf16[128,256]{1,0:T(8,128)(2,1)S(1)}, u32[]{:S(2)}, u32[]{:S(2)}) collective-permute-start(bf16[128,256]{1,0:T(8,128)(2,1)S(1)} %get-tuple-element.66), channel_id=1, source_target_pairs={{0,2},{1,3},{2,0},{3,1},{4,6},{5,7},{6,4},{7,5},{8,10},{9,11},{10,... | collective-permute-start | bytes 196616 | tf_op jit(solution)/shard_map/ppermute | solution.py:397
  27.0 6.9 %collective-permute-start.10 = (bf16[128,256]{1,0:T(8,128)(2,1)S(1)}, bf16[128,256]{1,0:T(8,128)(2,1)S(1)}, u32[]{:S(2)}, u32[]{:S(2)}) collective-permute-start(bf16[128,256]{1,0:T(8,128)(2,1)S(1)} %get-tuple-element.67), channel_id=1, source_target_pairs={{0,4},{1,5},{2,6},{3,7},{4,0},{5,1},{6,2},{7,3},{8,12},{9,13},{10,... | collective-permute-start | bytes 196616 | tf_op jit(solution)/shard_map/ppermute | solution.py:397
  27.7 6.1 %collective-permute-start.11 = (bf16[128,256]{1,0:T(8,128)(2,1)S(1)}, bf16[128,256]{1,0:T(8,128)(2,1)S(1)}, u32[]{:S(2)}, u32[]{:S(2)}) collective-permute-start(bf16[128,256]{1,0:T(8,128)(2,1)S(1)} %get-tuple-element.68), channel_id=1, source_target_pairs={{0,6},{1,7},{2,4},{3,5},{4,2},{5,3},{6,0},{7,1},{8,14},{9,15},{10,... | collective-permute-start | bytes 196616 | tf_op jit(solution)/shard_map/ppermute | solution.py:397
  34.3 7.9 %collective-permute-start.12 = (bf16[128,1024]{1,0:T(8,128)(2,1)S(1)}, bf16[128,1024]{1,0:T(8,128)(2,1)S(1)}, u32[]{:S(2)}, u32[]{:S(2)}) collective-permute-start(bf16[128,1024]{1,0:T(8,128)(2,1)S(1)} %shard_map.121), channel_id=1, source_target_pairs={{8,0},{16,8},{24,16},{0,24},{9,1},{17,9},{25,17},{1,25},{10,2},{18... | collective-permute-start | bytes 786440 | tf_op jit(solution)/shard_map/ppermute | solution.py:535

commit v5 on v4

--- a/solution.py
+++ b/solution.py
@@ -172,45 +172,57 @@
 
 def late_chunks(count, rows):
     half = count // 2
-    pieces = 3 if (half - 1) % 3 == 0 else 1
-    starts = list(range(1, half, pieces)) + list(range(half, count - 1, pieces))
-    return [slice(start * rows, (start + pieces) * rows) for start in starts]
-
-
-def attend_early(far_ref, own_ref, qf_ref, qb_ref, dout_ref, bias_ref, top_ref, mix_ref, stat_ref, e_ref, dp_ref):
+    odd = 3 if (half - 1) % 3 == 0 else 1
+    even = 2 if half % 2 == 0 else 1
+    blocks = [(start, odd) for start in range(1, half, odd)]
+    blocks += [(start, even) for start in range(half, count - 2, even)]
+    return [slice(start * rows, (start + pieces) * rows) for start, pieces in blocks]
+
+
+def attend_early(
+    far_ref, near_ref, own_ref, qf_ref, qb_ref, dout_ref, bias_ref, top_ref, mix_ref, stat_ref, e_ref, dp_ref
+):
     rows = own_ref.shape[0]
-    pieces = jnp.concatenate([far_ref[...], own_ref[...]], axis=0)
-    bias = jnp.concatenate([bias_ref[:rows, :], bias_ref[-rows:, :]], axis=0)
+    pieces = jnp.concatenate([far_ref[...], near_ref[...], own_ref[...]], axis=0)
+    bias = jnp.concatenate([bias_ref[:rows, :], bias_ref[-2 * rows :, :]], axis=0)
     extended = with_ones(pieces[:, KV_COLS : 2 * KV_COLS])
     wide = 2 * rows
-    for pair in range(PAIRS):
-        cols = slice(pair * wide, (pair + 1) * wide)
-        block = score_block(pieces[:, :KV_COLS], qf_ref[cols, :], bias)
-        top = jnp.max(block, axis=0, keepdims=True)
-        top_ref[pair : pair + 1, :] = top
-        weights = jnp.exp(block - top).astype(BF16)
-        mix_ref[pair] = dot(extended[(2 * pair) // GROUP], weights)
-        block = score_block(pieces[:, 2 * KV_COLS : 3 * KV_COLS], qb_ref[cols, :], bias)
-        top = jnp.max(block, axis=0, keepdims=True)
-        weights = jnp.exp(block - top)
-        prob_grad = dot(pieces[:, 3 * KV_COLS :], dout_ref[cols, :], NT)
-        stat_ref[0:1, cols] = top
-        stat_ref[1:2, cols] = jnp.sum(weights, axis=0, keepdims=True)
-        stat_ref[2:3, cols] = jnp.sum(weights * prob_grad, axis=0, keepdims=True)
-        e_ref[:, cols] = weights.astype(BF16)
-        dp_ref[:, cols] = prob_grad
+    blocks = {}
+    for now in range(-1, PAIRS):
+        ahead = now + 1
+        if ahead < PAIRS:
+            cols = slice(ahead * wide, (ahead + 1) * wide)
+            prob_grad = dot(pieces[:, 3 * KV_COLS :], dout_ref[cols, :], NT)
+            dp_ref[:, cols] = prob_grad
+            blocks[ahead] = (
+                score_block(pieces[:, :KV_COLS], qf_ref[cols, :], bias),
+                score_block(pieces[:, 2 * KV_COLS : 3 * KV_COLS], qb_ref[cols, :], bias),
+                prob_grad,
+            )
+        if now >= 0:
+            cols = slice(now * wide, (now + 1) * wide)
+            forward, backward, prob_grad = blocks[now]
+            top = jnp.max(forward, axis=0, keepdims=True)
+            top_ref[now : now + 1, :] = top
+            mix_ref[now] = dot(extended[(2 * now) // GROUP], jnp.exp(forward - top).astype(BF16))
+            top = jnp.max(backward, axis=0, keepdims=True)
+            weights = jnp.exp(backward - top)
+            stat_ref[0:1, cols] = top
+            stat_ref[1:2, cols] = jnp.sum(weights, axis=0, keepdims=True)
+            stat_ref[2:3, cols] = jnp.sum(weights * prob_grad, axis=0, keepdims=True)
+            e_ref[:, cols] = weights.astype(BF16)
 
 
 def attend_backward(count, *refs):
-    pieces = refs[: count - 2]
-    q_ref, dout_ref, bias_ref, far_ref, own_ref, stat_ref, e1_ref, dp1_ref = refs[count - 2 : count + 6]
+    pieces = refs[: count - 3]
+    q_ref, dout_ref, bias_ref, far_ref, near_ref, own_ref, stat_ref, e1_ref, dp1_ref = refs[count - 3 : count + 6]
     odd_ref, u_ref, e_ref, qs_ref, ds_ref, keys_ref, rs_ref = refs[count + 6 : count + 13]
     values_ref, s_ref, dp_ref, acc_ref = refs[count + 13 :]
     rows = own_ref.shape[0]
     total = rows * count
     half = count // 2
     odd = slice(0, half * rows)
-    for place, piece in enumerate((far_ref, *pieces, own_ref)):
+    for place, piece in enumerate((far_ref, *pieces, near_ref, own_ref)):
         lines = slice(place * rows, (place + 1) * rows)
         keys_ref[lines, :] = piece[:, 2 * KV_COLS : 3 * KV_COLS]
         values_ref[lines, :] = piece[:, 3 * KV_COLS :]
@@ -221,15 +233,6 @@
     for step in range(-1, PAIRS + 1):
         ahead, now, behind = step + 1, step, step - 1
         top = row_sum = mixed = None
-        if behind >= 0:
-            cols = slice(behind * wide, (behind + 1) * wide)
-            delta, factor = stats[behind]
-            weights = e1_ref[:, cols].astype(F32) * factor
-            score_grad = (weights * (dp1_ref[:, cols] - delta)).astype(BF16)
-            weights = weights.astype(BF16)
-            for lines, part in ((slice(0, rows), slice(0, rows)), (slice(total - rows, total), slice(rows, wide))):
-                e_ref[lines, cols] = weights[part]
-                u_ref[lines, cols] = score_grad[part]
         for lines in chunks:
             if 0 <= now < PAIRS:
                 cols = slice(now * wide, (now + 1) * wide)
@@ -249,22 +252,31 @@
                 cols = slice(behind * wide, (behind + 1) * wide)
                 difference = (dp_ref[behind % 2, lines, :] - stats[behind][0]).astype(BF16)
                 u_ref[lines, cols] = e_ref[lines, cols] * difference
-                if lines.stop == odd.stop:
-                    key_grad = dot(u_ref[odd, cols], scaled[behind][0])
-                    value_grad = dot(e_ref[odd, cols], scaled[behind][1])
-                    if behind:
-                        key_grad = key_grad + acc_ref[:, :KV_COLS]
-                        value_grad = value_grad + acc_ref[:, KV_COLS:]
-                    if behind < PAIRS - 1:
-                        acc_ref[:, :KV_COLS] = key_grad
-                        acc_ref[:, KV_COLS:] = value_grad
-                    else:
-                        for place in range(half):
-                            inner = slice(place * rows, (place + 1) * rows)
-                            odd_ref[place, :, :KV_COLS] = key_grad[inner].astype(BF16)
-                            odd_ref[place, :, KV_COLS:] = value_grad[inner].astype(BF16)
         if ahead < PAIRS:
             tops[ahead] = jnp.maximum(top, stat_ref[0:1, ahead * wide : (ahead + 1) * wide])
+        if behind >= 0:
+            cols = slice(behind * wide, (behind + 1) * wide)
+            delta, factor = stats[behind]
+            weights = e1_ref[:, cols].astype(F32) * factor
+            score_grad = (weights * (dp1_ref[:, cols] - delta)).astype(BF16)
+            weights = weights.astype(BF16)
+            e_ref[:rows, cols] = weights[:rows]
+            u_ref[:rows, cols] = score_grad[:rows]
+            e_ref[total - 2 * rows :, cols] = weights[rows:]
+            u_ref[total - 2 * rows :, cols] = score_grad[rows:]
+            key_grad = dot(u_ref[odd, cols], scaled[behind][0])
+            value_grad = dot(e_ref[odd, cols], scaled[behind][1])
+            if behind:
+                key_grad = key_grad + acc_ref[:, :KV_COLS]
+                value_grad = value_grad + acc_ref[:, KV_COLS:]
+            if behind < PAIRS - 1:
+                acc_ref[:, :KV_COLS] = key_grad
+                acc_ref[:, KV_COLS:] = value_grad
+            else:
+                for place in range(half):
+                    inner = slice(place * rows, (place + 1) * rows)
+                    odd_ref[place, :, :KV_COLS] = key_grad[inner].astype(BF16)
+                    odd_ref[place, :, KV_COLS:] = value_grad[inner].astype(BF16)
         if 0 <= now < PAIRS:
             cols = slice(now * wide, (now + 1) * wide)
             factor = jnp.exp(stat_ref[0:1, cols] - tops[now])
@@ -300,9 +312,9 @@
 
 
 def attend_forward(count, *refs):
-    pieces = refs[: count - 2]
-    q_ref, bias_ref, x_ref, wo_ref, top_ref, mix_ref, out_ref = refs[count - 2 : count + 5]
-    kv_ref, s_ref, at_ref = refs[count + 5 :]
+    pieces = refs[: count - 3]
+    q_ref, bias_ref, x_ref, wo_ref, top_ref, mix_ref, out_ref = refs[count - 3 : count + 4]
+    kv_ref, s_ref, at_ref = refs[count + 4 :]
     rows = pieces[0].shape[0]
     for place, piece in enumerate(pieces):
         kv_ref[(place + 1) * rows : (place + 2) * rows, :] = piece[:, : 2 * KV_COLS]
@@ -341,10 +353,11 @@
     copy.wait()
 
 
-def add_pieces(count, *refs):
-    for place in range(count):
+def add_pieces(steps, *refs):
+    count = len(steps)
+    for place, step in enumerate(steps):
         left = refs[place][...].astype(F32)
-        refs[count + 1 + place][...] = (left + refs[count][(place + 1) % count].astype(F32)).astype(BF16)
+        refs[count + 1 + place][...] = (left + refs[count][step // 2].astype(F32)).astype(BF16)
 
 
 def input_back(count, *refs):
@@ -398,11 +411,11 @@
 
 
 def order_of(size):
-    return list(range(1, size, 2)) + list(range(2, size, 2)) + [0]
+    return list(range(1, size, 2)) + list(range(4, size, 2)) + [2, 0]
 
 
 def by_permutes(size):
-    return size in (4, 8)
+    return size == 8
 
 
 def gather_near(block, size):
@@ -416,7 +429,7 @@
         me = lax.axis_index("seq")
         return [lax.dynamic_index_in_dim(near, me ^ step, 0, False) for step in order_of(size)]
     far = [swap(piece, 1, size) for piece in near]
-    return far + near[1:] + near[:1]
+    return far + near[2:] + near[1:2] + near[:1]
 
 
 def on_device(
@@ -476,15 +489,15 @@
             shape((PAIRS, wide), F32),
             shape((PAIRS, HEAD_DIM + 16, wide), F32),
             shape((8, HEADS * rows), F32),
-            shape((wide, HEADS * rows), BF16),
-            shape((wide, HEADS * rows), F32),
+            shape((3 * rows, HEADS * rows), BF16),
+            shape((3 * rows, HEADS * rows), F32),
         ),
-        (pieces[0], pieces[-1], qf, qb, dout, bias),
+        (pieces[0], *pieces[-2:], qf, qb, dout, bias),
     )
     layer_out = call(
         partial(attend_forward, size),
         shape((rows, width), BF16),
-        (*pieces[1:-1], qf, bias, xf, wo, top, mix),
+        (*pieces[1:-2], qf, bias, xf, wo, top, mix),
         scratch=(
             pltpu.VMEM((total, 2 * KV_COLS), BF16),
             pltpu.VMEM((2, total, wide), F32),
@@ -503,7 +516,7 @@
             shape((total, KV_COLS), BF16),
             shape((8, HEADS * rows), F32),
         ),
-        (*pieces[1:-1], qb, dout, bias, pieces[0], pieces[-1], stat, early, early_dp),
+        (*pieces[1:-2], qb, dout, bias, pieces[0], *pieces[-2:], stat, early, early_dp),
         scratch=(
             pltpu.VMEM((total, KV_COLS), BF16),
             pltpu.VMEM((2, total, wide), F32),
@@ -519,8 +532,9 @@
     )
     if by_permutes(size):
         other = swap(odd, 1, size)
-        sums = call(partial(add_pieces, half), (kv_shape,) * half, (*even, other))
-        received = [sums[-1]] + [swap(sums[i], 2 * i + 2, size) for i in range(half - 1)]
+        steps = order[half:]
+        sums = call(partial(add_pieces, steps), (kv_shape,) * half, (*even, other))
+        received = [sums[-1]] + [swap(sums[steps.index(step)], step, size) for step in sorted(steps)[1:]]
     else:
         both = jnp.stack([odd[i] for i in range(half)] + list(even)).astype(F32)
         places = jnp.argsort(jnp.array(order, jnp.int32) ^ lax.axis_index("seq"))

time: 43.1 us -> 42.4 us (0.984)
  Pallas kernels: 13.1 us -> 12.4 us
    pallas_call x9, Pallas kernels: 13.1 us -> 12.4 us  [call(): pl.pallas_call(kernel, out_shape=[pltpu.VMEM(out.shape, out.dtype) for ou...]
  transfers between devices with their start and end apart: 13 -> 13, of which waited for: 5 -> 5; matrix products, arithmetic and copies ran while one was open for 0% -> 0% of each run, Pallas kernels for 18% -> 17%
where the time goes in v5:
time: 42.4 us; the launch traced here: 42.3 us
  waiting for transfers between devices  16.2 us (38%)
  Pallas kernels  12.4 us (29%)
  starting transfers between devices  12.2 us (29%)
  between operations  0.77 us (2%)
  local copies, waits for them, and re-layouts  0.7 us (2%)
    pallas_call x9, Pallas kernels, call(): pl.pallas_call(kernel, out_shape=[pltpu.VMEM(out.shape, out.dtype) for ou...  12.4 us
    ppermute x11, starting transfers between devices, swap(): return lax.ppermute(block, 'seq', [(i, i ^ step) for i in range(size)])  8.77 us
    ppermute x1, waiting for transfers between devices, on_device(): lax.ppermute(input_grad, 'section', [((i + 1) % sections, i) for i in ran...  6.11 us
    ppermute x11, waiting for transfers between devices, swap(): return lax.ppermute(block, 'seq', [(i, i ^ step) for i in range(size)])  5.92 us
    ppermute x1, waiting for transfers between devices, on_device(): lax.ppermute(layer_out, 'section', [((i - 1) % sections, i) for i in rang...  4.19 us
    ppermute x1, starting transfers between devices, on_device(): lax.ppermute(input_grad, 'section', [((i + 1) % sections, i) for i in ran...  1.79 us
    ppermute x1, starting transfers between devices, on_device(): lax.ppermute(layer_out, 'section', [((i - 1) % sections, i) for i in rang...  1.61 us
  transfers between devices with their start and end apart: 13, of which 5 were waited for; matrix products, arithmetic and copies ran while one was open for 0% of the time, Pallas kernels for 17%

profile of v5, /device:TPU:0, one launch (start us, length us, event | category | flops | bytes accessed | tf_op | source)
XLA Modules:
  0.0 42.3 jit_solution(10092873640997850735)
XLA Ops:
  0.6 1.6 %shard_map.113 = (bf16[128,512]{1,0:T(8,128)(2,1)S(1)}, f32[1,1024]{1,0:T(1,128)S(1)}, bf16[128,1024]{1,0:T(8,128)(2,1)S(1)}, bf16[128,1024]{1,0:T(8,128)(2,1)S(1)}, bf16[1024,256]{1,0:T(8,128)(2,1)S(1)}) custom-call(f32[1,1024]{1,0:T(1,128)} %gain_hbm.1, bf16[128,1024]{1,0:T(8,128)(2,1)} %bitcast.14, bf16[128,1024]{1,0:T(8,128)(2,1)} %bitcast.15, ...), custom_call_target="tpu_custom_call" | custom-call | tf_op jit(solution)/shard_map/pallas_call | solution.py:396
  2.3 4.0 %collective-permute-start.4 = (bf16[128,512]{1,0:T(8,128)(2,1)S(1)}, bf16[128,512]{1,0:T(8,128)(2,1)S(1)}, u32[]{:S(2)}, u32[]{:S(2)}) collective-permute-start(bf16[128,512]{1,0:T(8,128)(2,1)S(1)} %get-tuple-element.37.own_ref.refs_10_), channel_id=1, source_target_pairs={{0,6},{1,7},{2,4},{3,5},{4,2},{5,3},{6,0},{7,1},{8,14},{9,15},{10,... | collective-permute-start | bytes 393224 | tf_op jit(solution)/shard_map/ppermute | solution.py:410
  6.2 0.5 %collective-permute-start.2 = (bf16[128,512]{1,0:T(8,128)(2,1)S(1)}, bf16[128,512]{1,0:T(8,128)(2,1)S(1)}, u32[]{:S(2)}, u32[]{:S(2)}) collective-permute-start(bf16[128,512]{1,0:T(8,128)(2,1)S(1)} %get-tuple-element.37.own_ref.refs_10_), channel_id=1, source_target_pairs={{0,4},{1,5},{2,6},{3,7},{4,0},{5,1},{6,2},{7,3},{8,12},{9,13},{10,... | collective-permute-start | bytes 393224 | tf_op jit(solution)/shard_map/ppermute | solution.py:410
  6.7 0.1 collective-permute-start
  6.9 0.0 collective-permute-start.6
  6.9 3.2 %collective-permute-done.4.refs_4_ = bf16[128,512]{1,0:T(8,128)(2,1)S(1)} collective-permute-done((bf16[128,512]{1,0:T(8,128)(2,1)S(1)}, bf16[128,512]{1,0:T(8,128)(2,1)S(1)}, u32[]{:S(2)}, u32[]{:S(2)}) %collective-permute-start.4) | collective-permute-done | bytes 131104 | tf_op jit(solution)/shard_map/ppermute | solution.py:410
  10.1 0.0 collective-permute-start.5
  10.1 2.4 %collective-permute-done.2.refs_3_ = bf16[128,512]{1,0:T(8,128)(2,1)S(1)} collective-permute-done((bf16[128,512]{1,0:T(8,128)(2,1)S(1)}, bf16[128,512]{1,0:T(8,128)(2,1)S(1)}, u32[]{:S(2)}, u32[]{:S(2)}) %collective-permute-start.2) | collective-permute-done | bytes 131104 | tf_op jit(solution)/shard_map/ppermute | solution.py:410
  12.5 0.0 collective-permute-start.3
  12.5 0.2 collective-permute-done.near_ref.refs_9_
  12.8 0.3 collective-permute-start.1
  13.1 2.6 %shard_map.114 = (bf16[1024,128]{1,0:T(8,128)(2,1)S(1)}, bf16[1024,128]{1,0:T(8,128)(2,1)S(1)}, bf16[1024,128]{1,0:T(8,128)(2,1)S(1)}, f32[1024,128]{1,0:T(8,128...) custom-call(s32[1]{0:T(128)} %bitcast.4.me_ref, ...), custom_call_target="tpu_custom_call" | custom-call | tf_op jit(solution)/shard_map/pallas_call | solution.py:396
  15.6 0.0 collective-permute-done.6.far_ref.refs_8_
  15.6 1.4 %shard_map.115 = (f32[4,256]{1,0:T(4,128)S(1)}, f32[4,80,256]{2,1,0:T(8,128)S(1)}, f32[8,1024]{1,0:T(8,128)S(1)}, bf16[384,1024]{1,0:T(8,128)(2,1)S(1)}, f32[384,1024]{1,0:T(8,128)S(1)}) custom-call(bf16[128,512]{1,0:T(8,128)(2,1)S(1)} %collective-permute-done.6.far_ref.refs_8_, bf16[128,512]{1,0:T(8,128)(2,1)S(1)} %collective-permute-done.near_ref.refs_9_, ...), custom_call_target="tpu_custom_call" | custom-call | tf_op jit(solution)/shard_map/pallas_call | solution.py:396
  17.1 0.0 collective-permute-done.5.refs_2_
  17.1 0.0 collective-permute-done.3.refs_1_
  17.1 0.0 collective-permute-done.1.refs_0_
  17.1 3.0 %shard_map.116 = (bf16[4,128,256]{2,1,0:T(8,128)(2,1)S(1)}, bf16[1024,1024]{1,0:T(8,128)(2,1)S(1)}, bf16[1024,1024]{1,0:T(8,128)(2,1)S(1)}, bf16[1024,128]{1,0:T...) custom-call(bf16[128,512]{1,0:T(8,128)(2,1)S(1)} %collective-permute-done.1.re, ...), custom_call_target="tpu_custom_call" | custom-call | tf_op jit(solution)/shard_map/pallas_call | solution.py:396
  20.1 0.3 collective-permute-start.8
  20.4 1.5 %shard_map.118 = bf16[128,1024]{1,0:T(8,128)(2,1)S(1)} custom-call(bf16[128,512]{1,0:T(8,128)(2,1)S(1)} %collective-permute-done.1.refs_0_, bf16[128,512]{1,0:T(8,128)(2,1)S(1)} %collective-permute-done.3.refs_1_, bf16[128,512]{1,0:T(8,128)(2,1)S(1)} %collective-permute-done.5.refs_2_, bf16[128,512]{1,0:T(8,128)(2,1)S(1)} %collective-permute-done.2.refs_3_, ...), custom_call_target="tpu_custom_call" | custom-call | tf_op jit(solution)/shard_map/pallas_call | solution.py:396
  21.9 1.6 %collective-permute-start.7 = (bf16[128,1024]{1,0:T(8,128)(2,1)S(1)}, bf16[128,1024]{1,0:T(8,128)(2,1)S(1)}, u32[]{:S(2)}, u32[]{:S(2)}) collective-permute-start(bf16[128,1024]{1,0:T(8,128)(2,1)S(1)} %shard_map.118), channel_id=1, source_target_pairs={{24,0},{0,8},{8,16},{16,24},{25,1},{1,9},{9,17},{17,25},{26,2},{2,... | collective-permute-start | bytes 786440 | tf_op jit(solution)/shard_map/ppermute | solution.py:507
  23.5 1.1 %shard_map.117 = (bf16[128,256]{1,0:T(8,128)(2,1)S(1)}, bf16[128,256]{1,0:T(8,128)(2,1)S(1)}, bf16[128,256]{1,0:T(8,128)(2,1)S(1)}, bf16[128,256]{1,0:T(8,128)(2,1)S(1)}, bf16[128,512]{1,0:T(8,128)(2,1)S(1)}) custom-call(bf16[1024,1024]{1,0:T(8,128)(2,1)S(1)} %get-tuple-element.48.u_ref, bf16[1024,1024]{1,0:T(8,128)(2,1)S(1)} %get-tuple-element.49.e_ref, ...), custom_call_target="tpu_custom_call" | custom-call | tf_op jit(solution)/shard_map/pallas_call | solution.py:396
  24.6 0.0 collective-permute-done.8.refs_4_
  24.6 0.1 shard_map.120
  24.7 1.6 %collective-permute-start.9 = (bf16[128,256]{1,0:T(8,128)(2,1)S(1)}, bf16[128,256]{1,0:T(8,128)(2,1)S(1)}, u32[]{:S(2)}, u32[]{:S(2)}) collective-permute-start(bf16[128,256]{1,0:T(8,128)(2,1)S(1)} %get-tuple-element.66), channel_id=1, source_target_pairs={{0,2},{1,3},{2,0},{3,1},{4,6},{5,7},{6,4},{7,5},{8,10},{9,11},{10,... | collective-permute-start | bytes 196616 | tf_op jit(solution)/shard_map/ppermute | solution.py:410
  26.3 0.7 %collective-permute-start.10 = (bf16[128,256]{1,0:T(8,128)(2,1)S(1)}, bf16[128,256]{1,0:T(8,128)(2,1)S(1)}, u32[]{:S(2)}, u32[]{:S(2)}) collective-permute-start(bf16[128,256]{1,0:T(8,128)(2,1)S(1)} %get-tuple-element.67), channel_id=1, source_target_pairs={{0,4},{1,5},{2,6},{3,7},{4,0},{5,1},{6,2},{7,3},{8,12},{9,13},{10,... | collective-permute-start | bytes 196616 | tf_op jit(solution)/shard_map/ppermute | solution.py:410
  27.1 1.2 %collective-permute-start.11 = (bf16[128,256]{1,0:T(8,128)(2,1)S(1)}, bf16[128,256]{1,0:T(8,128)(2,1)S(1)}, u32[]{:S(2)}, u32[]{:S(2)}) collective-permute-start(bf16[128,256]{1,0:T(8,128)(2,1)S(1)} %get-tuple-element.68), channel_id=1, source_target_pairs={{0,6},{1,7},{2,4},{3,5},{4,2},{5,3},{6,0},{7,1},{8,14},{9,15},{10,... | collective-permute-start | bytes 196616 | tf_op jit(solution)/shard_map/ppermute | solution.py:410
  28.3 4.2 %collective-permute-done.7.next_ref = bf16[128,1024]{1,0:T(8,128)(2,1)S(1)} collective-permute-done((bf16[128,1024]{1,0:T(8,128)(2,1)S(1)}, bf16[128,1024]{1,0:T(8,128)(2,1)S(1)}, u32[]{:S(2)}, u32[]{:S(2)}) %collective-permute-start.7) | collective-permute-done | bytes 262176 | tf_op jit(solution)/shard_map/ppermute | solution.py:507
  32.4 0.7 %shard_map.119 = (f32[128,1024]{1,0:T(8,128)S(1)}, bf16[128,1024]{1,0:T(8,128)(2,1)}) custom-call(bf16[128,512]{1,0:T(8,128)(2,1)S(1)} %get-tuple-element.54.dq_ref, bf16[1024,512]{1,0:T(8,128)(2,1)S(1)} %get-tuple-element.55.wq_ref, bf16[128,1024]{1,0:T(8,128)(2,1)S(1)} %collective-permute-done.7.next_ref), custom_call_target="tpu_custom_call" | custom-call | tf_op jit(solution)/shard_map/pallas_call | solution.py:396
  33.2 0.0 collective-permute-done.9.refs_1_
  33.2 0.0 collective-permute-done.10.refs_2_
  33.2 0.0 collective-permute-done.11.refs_3_
  33.2 0.4 %shard_map.121 = bf16[128,1024]{1,0:T(8,128)(2,1)S(1)} custom-call(bf16[128,256]{1,0:T(8,128)(2,1)S(1)} %get-tuple-element.65.refs_0_, bf16[128,256]{1,0:T(8,128)(2,1)S(1)} %collective-permute-done.9.refs_1_, bf16[128,256]{1,0:T(8,128)(2,1)S(1)} %collective-permute-done.10.refs_2_, bf16[128,256]{1,0:T(8,128)(2,1)S(1)} %collective-permute-done.11.refs_3_, ...), custom_call_target="tpu_custom_call" | custom-call | tf_op jit(solution)/shard_map/pallas_call | solution.py:396
  33.6 1.8 %collective-permute-start.12 = (bf16[128,1024]{1,0:T(8,128)(2,1)S(1)}, bf16[128,1024]{1,0:T(8,128)(2,1)S(1)}, u32[]{:S(2)}, u32[]{:S(2)}) collective-permute-start(bf16[128,1024]{1,0:T(8,128)(2,1)S(1)} %shard_map.121), channel_id=1, source_target_pairs={{8,0},{16,8},{24,16},{0,24},{9,1},{17,9},{25,17},{1,25},{10,2},{18... | collective-permute-start | bytes 786440 | tf_op jit(solution)/shard_map/ppermute | solution.py:549
  35.4 6.1 %collective-permute-done.12 = bf16[128,1024]{1,0:T(8,128)(2,1)S(1)} collective-permute-done((bf16[128,1024]{1,0:T(8,128)(2,1)S(1)}, bf16[128,1024]{1,0:T(8,128)(2,1)S(1)}, u32[]{:S(2)}, u32[]{:S(2)}) %collective-permute-start.12) | collective-permute-done | bytes 262176 | tf_op jit(solution)/shard_map/ppermute | solution.py:549
  41.5 0.7 %copy.13 = bf16[1,128,1024]{2,1,0:T(8,128)(2,1)} copy(bf16[1,128,1024]{2,1,0:T(8,128)(2,1)S(1)} %bitcast.13) | data formatting | bytes 524288
Async XLA Ops:
  2.3 7.9 %collective-permute-start.4 = (bf16[128,512]{1,0:T(8,128)(2,1)S(1)}, bf16[128,512]{1,0:T(8,128)(2,1)S(1)}, u32[]{:S(2)}, u32[]{:S(2)}) collective-permute-start(bf16[128,512]{1,0:T(8,128)(2,1)S(1)} %get-tuple-element.37.own_ref.refs_10_), channel_id=1, source_target_pairs={{0,6},{1,7},{2,4},{3,5},{4,2},{5,3},{6,0},{7,1},{8,14},{9,15},{10,... | collective-permute-start | bytes 393224 | tf_op jit(solution)/shard_map/ppermute | solution.py:410
  6.2 6.3 %collective-permute-start.2 = (bf16[128,512]{1,0:T(8,128)(2,1)S(1)}, bf16[128,512]{1,0:T(8,128)(2,1)S(1)}, u32[]{:S(2)}, u32[]{:S(2)}) collective-permute-start(bf16[128,512]{1,0:T(8,128)(2,1)S(1)} %get-tuple-element.37.own_ref.refs_10_), channel_id=1, source_target_pairs={{0,4},{1,5},{2,6},{3,7},{4,0},{5,1},{6,2},{7,3},{8,12},{9,13},{10,... | collective-permute-start | bytes 393224 | tf_op jit(solution)/shard_map/ppermute | solution.py:410
  6.7 6.0 %collective-permute-start = (bf16[128,512]{1,0:T(8,128)(2,1)S(1)}, bf16[128,512]{1,0:T(8,128)(2,1)S(1)}, u32[]{:S(2)}, u32[]{:S(2)}) collective-permute-start(bf16[128,512]{1,0:T(8,128)(2,1)S(1)} %get-tuple-element.37.own_ref.refs_10_), channel_id=1, source_target_pairs={{0,2},{1,3},{2,0},{3,1},{4,6},{5,7},{6,4},{7,5},{8,10},{9,11},{10,... | collective-permute-start | bytes 393224 | tf_op jit(solution)/shard_map/ppermute | solution.py:410
  6.9 8.8 %collective-permute-start.6 = (bf16[128,512]{1,0:T(8,128)(2,1)S(1)}, bf16[128,512]{1,0:T(8,128)(2,1)S(1)}, u32[]{:S(2)}, u32[]{:S(2)}) collective-permute-start(bf16[128,512]{1,0:T(8,128)(2,1)S(1)} %get-tuple-element.37.own_ref.refs_10_), channel_id=1, source_target_pairs={{0,1},{1,0},{2,3},{3,2},{4,5},{5,4},{6,7},{7,6},{8,9},{9,8},{10,11... | collective-permute-start | bytes 393224 | tf_op jit(solution)/shard_map/ppermute | solution.py:410
  10.1 6.9 %collective-permute-start.5 = (bf16[128,512]{1,0:T(8,128)(2,1)S(1)}, bf16[128,512]{1,0:T(8,128)(2,1)S(1)}, u32[]{:S(2)}, u32[]{:S(2)}) collective-permute-start(bf16[128,512]{1,0:T(8,128)(2,1)S(1)} %collective-permute-done.4.refs_4_), channel_id=1, source_target_pairs={{0,1},{1,0},{2,3},{3,2},{4,5},{5,4},{6,7},{7,6},{8,9},{9,8},{10,11... | collective-permute-start | bytes 393224 | tf_op jit(solution)/shard_map/ppermute | solution.py:410
  12.5 4.5 %collective-permute-start.3 = (bf16[128,512]{1,0:T(8,128)(2,1)S(1)}, bf16[128,512]{1,0:T(8,128)(2,1)S(1)}, u32[]{:S(2)}, u32[]{:S(2)}) collective-permute-start(bf16[128,512]{1,0:T(8,128)(2,1)S(1)} %collective-permute-done.2.refs_3_), channel_id=1, source_target_pairs={{0,1},{1,0},{2,3},{3,2},{4,5},{5,4},{6,7},{7,6},{8,9},{9,8},{10,11... | collective-permute-start | bytes 393224 | tf_op jit(solution)/shard_map/ppermute | solution.py:410
  12.8 4.3 %collective-permute-start.1 = (bf16[128,512]{1,0:T(8,128)(2,1)S(1)}, bf16[128,512]{1,0:T(8,128)(2,1)S(1)}, u32[]{:S(2)}, u32[]{:S(2)}) collective-permute-start(bf16[128,512]{1,0:T(8,128)(2,1)S(1)} %collective-permute-done.near_ref.refs_9_), channel_id=1, source_target_pairs={{0,1},{1,0},{2,3},{3,2},{4,5},{5,4},{6,7},{7,6},{8,9},{9,8},{10,11... | collective-permute-start | bytes 393224 | tf_op jit(solution)/shard_map/ppermute | solution.py:410
  20.1 4.6 %collective-permute-start.8 = (bf16[4,128,256]{2,1,0:T(8,128)(2,1)S(1)}, bf16[4,128,256]{2,1,0:T(8,128)(2,1)S(1)}, u32[]{:S(2)}, u32[]{:S(2)}) collective-permute-start(bf16[4,128,256]{2,1,0:T(8,128)(2,1)S(1)} %get-tuple-element.64), channel_id=1, source_target_pairs={{0,1},{1,0},{2,3},{3,2},{4,5},{5,4},{6,7},{7,6},{8,9},{9,8},{10,11... | collective-permute-start | bytes 786440 | tf_op jit(solution)/shard_map/ppermute | solution.py:410
  21.9 10.6 %collective-permute-start.7 = (bf16[128,1024]{1,0:T(8,128)(2,1)S(1)}, bf16[128,1024]{1,0:T(8,128)(2,1)S(1)}, u32[]{:S(2)}, u32[]{:S(2)}) collective-permute-start(bf16[128,1024]{1,0:T(8,128)(2,1)S(1)} %shard_map.118), channel_id=1, source_target_pairs={{24,0},{0,8},{8,16},{16,24},{25,1},{1,9},{9,17},{17,25},{26,2},{2,... | collective-permute-start | bytes 786440 | tf_op jit(solution)/shard_map/ppermute | solution.py:507
  24.7 8.5 %collective-permute-start.9 = (bf16[128,256]{1,0:T(8,128)(2,1)S(1)}, bf16[128,256]{1,0:T(8,128)(2,1)S(1)}, u32[]{:S(2)}, u32[]{:S(2)}) collective-permute-start(bf16[128,256]{1,0:T(8,128)(2,1)S(1)} %get-tuple-element.66), channel_id=1, source_target_pairs={{0,2},{1,3},{2,0},{3,1},{4,6},{5,7},{6,4},{7,5},{8,10},{9,11},{10,... | collective-permute-start | bytes 196616 | tf_op jit(solution)/shard_map/ppermute | solution.py:410
  26.3 6.9 %collective-permute-start.10 = (bf16[128,256]{1,0:T(8,128)(2,1)S(1)}, bf16[128,256]{1,0:T(8,128)(2,1)S(1)}, u32[]{:S(2)}, u32[]{:S(2)}) collective-permute-start(bf16[128,256]{1,0:T(8,128)(2,1)S(1)} %get-tuple-element.67), channel_id=1, source_target_pairs={{0,4},{1,5},{2,6},{3,7},{4,0},{5,1},{6,2},{7,3},{8,12},{9,13},{10,... | collective-permute-start | bytes 196616 | tf_op jit(solution)/shard_map/ppermute | solution.py:410
  27.1 6.1 %collective-permute-start.11 = (bf16[128,256]{1,0:T(8,128)(2,1)S(1)}, bf16[128,256]{1,0:T(8,128)(2,1)S(1)}, u32[]{:S(2)}, u32[]{:S(2)}) collective-permute-start(bf16[128,256]{1,0:T(8,128)(2,1)S(1)} %get-tuple-element.68), channel_id=1, source_target_pairs={{0,6},{1,7},{2,4},{3,5},{4,2},{5,3},{6,0},{7,1},{8,14},{9,15},{10,... | collective-permute-start | bytes 196616 | tf_op jit(solution)/shard_map/ppermute | solution.py:410
  33.6 7.9 %collective-permute-start.12 = (bf16[128,1024]{1,0:T(8,128)(2,1)S(1)}, bf16[128,1024]{1,0:T(8,128)(2,1)S(1)}, u32[]{:S(2)}, u32[]{:S(2)}) collective-permute-start(bf16[128,1024]{1,0:T(8,128)(2,1)S(1)} %shard_map.121), channel_id=1, source_target_pairs={{8,0},{16,8},{24,16},{0,24},{9,1},{17,9},{25,17},{1,25},{10,2},{18... | collective-permute-start | bytes 786440 | tf_op jit(solution)/shard_map/ppermute | solution.py:549

commit v6 on v5

--- a/solution.py
+++ b/solution.py
@@ -213,63 +213,74 @@
             e_ref[:, cols] = weights.astype(BF16)
 
 
-def attend_backward(count, *refs):
-    pieces = refs[: count - 3]
-    q_ref, dout_ref, bias_ref, far_ref, near_ref, own_ref, stat_ref, e1_ref, dp1_ref = refs[count - 3 : count + 6]
-    odd_ref, u_ref, e_ref, qs_ref, ds_ref, keys_ref, rs_ref = refs[count + 6 : count + 13]
-    values_ref, s_ref, dp_ref, acc_ref = refs[count + 13 :]
+def attend_late(count, *refs):
+    late = count - 3
+    pieces = refs[:late]
+    qf_ref, x_ref, wo_ref, top_ref, mix_ref, qb_ref, dout_ref, bias_ref = refs[late : late + 8]
+    far_ref, near_ref, own_ref, stat_ref, e1_ref, dp1_ref = refs[late + 8 : late + 14]
+    out_ref, odd_ref, u_ref, e_ref, qs_ref, ds_ref, keys_ref, rs_ref = refs[late + 14 : late + 22]
+    kv_ref, values_ref, s_ref, dp_ref, acc_ref, at_ref = refs[late + 22 :]
     rows = own_ref.shape[0]
     total = rows * count
     half = count // 2
     odd = slice(0, half * rows)
+    wide = 2 * rows
+    scale = 1.0 / math.sqrt(HEAD_DIM)
+    chunks = late_chunks(count, rows)
     for place, piece in enumerate((far_ref, *pieces, near_ref, own_ref)):
         lines = slice(place * rows, (place + 1) * rows)
+        kv_ref[lines, :] = piece[:, : 2 * KV_COLS]
         keys_ref[lines, :] = piece[:, 2 * KV_COLS : 3 * KV_COLS]
         values_ref[lines, :] = piece[:, 3 * KV_COLS :]
-    scale = 1.0 / math.sqrt(HEAD_DIM)
-    wide = 2 * rows
-    chunks = late_chunks(count, rows)
+    extended = [with_ones(kv_ref[lines, KV_COLS:]) for lines in chunks]
     tops, stats, scaled = {}, {}, {}
-    for step in range(-1, PAIRS + 1):
+    for step in range(-1, 2 * PAIRS + 1):
         ahead, now, behind = step + 1, step, step - 1
+        pair = now % PAIRS
+        cols = slice(pair * wide, (pair + 1) * wide)
+        old = slice((behind % PAIRS) * wide, (behind % PAIRS + 1) * wide)
+        new = slice((ahead % PAIRS) * wide, (ahead % PAIRS + 1) * wide)
         top = row_sum = mixed = None
-        for lines in chunks:
+        for place, lines in enumerate(chunks):
             if 0 <= now < PAIRS:
-                cols = slice(now * wide, (now + 1) * wide)
+                weights = jnp.exp(s_ref[now % 2, lines, :] - tops[now]).astype(BF16)
+                mixed = plus(mixed, dot(extended[place][(2 * pair) // GROUP], weights))
+            elif PAIRS <= now < 2 * PAIRS:
                 weights = jnp.exp(s_ref[now % 2, lines, :] - tops[now])
                 prob_grad = dot(values_ref[lines, :], dout_ref[cols, :], NT)
                 row_sum = plus(row_sum, jnp.sum(weights, axis=0, keepdims=True))
                 mixed = plus(mixed, jnp.sum(weights * prob_grad, axis=0, keepdims=True))
                 dp_ref[now % 2, lines, :] = prob_grad
                 e_ref[lines, cols] = weights.astype(BF16)
-            if ahead < PAIRS:
-                q_rows = q_ref[ahead * wide : (ahead + 1) * wide, :]
-                block = score_block(keys_ref[lines, :], q_rows, bias_ref[lines, :])
+            if ahead < 2 * PAIRS:
+                keys = kv_ref[lines, :KV_COLS] if ahead < PAIRS else keys_ref[lines, :]
+                q_rows = qf_ref[new, :] if ahead < PAIRS else qb_ref[new, :]
+                block = score_block(keys, q_rows, bias_ref[lines, :])
                 s_ref[ahead % 2, lines, :] = block
                 part = jnp.max(block, axis=0, keepdims=True)
                 top = part if top is None else jnp.maximum(top, part)
-            if behind >= 0:
-                cols = slice(behind * wide, (behind + 1) * wide)
+            if behind >= PAIRS:
                 difference = (dp_ref[behind % 2, lines, :] - stats[behind][0]).astype(BF16)
-                u_ref[lines, cols] = e_ref[lines, cols] * difference
+                u_ref[lines, old] = e_ref[lines, old] * difference
         if ahead < PAIRS:
-            tops[ahead] = jnp.maximum(top, stat_ref[0:1, ahead * wide : (ahead + 1) * wide])
-        if behind >= 0:
-            cols = slice(behind * wide, (behind + 1) * wide)
+            tops[ahead] = jnp.maximum(top, top_ref[ahead : ahead + 1, :])
+        elif ahead < 2 * PAIRS:
+            tops[ahead] = jnp.maximum(top, stat_ref[0:1, new])
+        if behind >= PAIRS:
             delta, factor = stats[behind]
-            weights = e1_ref[:, cols].astype(F32) * factor
-            score_grad = (weights * (dp1_ref[:, cols] - delta)).astype(BF16)
+            weights = e1_ref[:, old].astype(F32) * factor
+            score_grad = (weights * (dp1_ref[:, old] - delta)).astype(BF16)
             weights = weights.astype(BF16)
-            e_ref[:rows, cols] = weights[:rows]
-            u_ref[:rows, cols] = score_grad[:rows]
-            e_ref[total - 2 * rows :, cols] = weights[rows:]
-            u_ref[total - 2 * rows :, cols] = score_grad[rows:]
-            key_grad = dot(u_ref[odd, cols], scaled[behind][0])
-            value_grad = dot(e_ref[odd, cols], scaled[behind][1])
-            if behind:
+            e_ref[:rows, old] = weights[:rows]
+            u_ref[:rows, old] = score_grad[:rows]
+            e_ref[total - 2 * rows :, old] = weights[rows:]
+            u_ref[total - 2 * rows :, old] = score_grad[rows:]
+            key_grad = dot(u_ref[odd, old], scaled[behind][0])
+            value_grad = dot(e_ref[odd, old], scaled[behind][1])
+            if behind > PAIRS:
                 key_grad = key_grad + acc_ref[:, :KV_COLS]
                 value_grad = value_grad + acc_ref[:, KV_COLS:]
-            if behind < PAIRS - 1:
+            if behind < 2 * PAIRS - 1:
                 acc_ref[:, :KV_COLS] = key_grad
                 acc_ref[:, KV_COLS:] = value_grad
             else:
@@ -278,29 +289,39 @@
                     odd_ref[place, :, :KV_COLS] = key_grad[inner].astype(BF16)
                     odd_ref[place, :, KV_COLS:] = value_grad[inner].astype(BF16)
         if 0 <= now < PAIRS:
-            cols = slice(now * wide, (now + 1) * wide)
+            mixed = mixed + mix_ref[pair] * jnp.exp(top_ref[pair : pair + 1, :] - tops[now])
+            part = mixed[:HEAD_DIM] * (1.0 / mixed[HEAD_DIM : HEAD_DIM + 1])
+            at_ref[2 * pair * HEAD_DIM : (2 * pair + 1) * HEAD_DIM, :] = part[:, :rows]
+            at_ref[(2 * pair + 1) * HEAD_DIM : (2 * pair + 2) * HEAD_DIM, :] = part[:, rows:]
+        elif PAIRS <= now < 2 * PAIRS:
             factor = jnp.exp(stat_ref[0:1, cols] - tops[now])
             inverse_sum = 1.0 / (row_sum + factor * stat_ref[1:2, cols])
             stats[now] = ((mixed + factor * stat_ref[2:3, cols]) * inverse_sum, factor)
             rs_ref[0:1, cols] = inverse_sum * scale
             column = jnp.transpose(jnp.broadcast_to(inverse_sum, (KV_COLS, wide)))
             scaled[now] = (
-                (q_ref[cols, :].astype(F32) * column).astype(BF16),
+                (qb_ref[cols, :].astype(F32) * column).astype(BF16),
                 (dout_ref[cols, :].astype(F32) * column).astype(BF16),
             )
             qs_ref[cols, :], ds_ref[cols, :] = scaled[now]
-
-
-def finish_backward(u_ref, e_ref, qs_ref, ds_ref, keys_ref, rs_ref, *refs):
-    even_refs, dq_ref, dqt_ref = refs[:-2], refs[-2], refs[-1]
+        if now == PAIRS:
+            attended = jnp.transpose(at_ref[...]).astype(BF16)
+            out_ref[...] = (x_ref[...].astype(F32) + dot(attended, wo_ref[...])).astype(BF16)
+
+
+def finish_backward(u_ref, e_ref, qs_ref, ds_ref, *even_refs):
     rows = even_refs[0].shape[0]
     even = slice(len(even_refs) * rows, 2 * len(even_refs) * rows)
-    wide = 2 * rows
     key_grad = dot(u_ref[even, :], qs_ref[...]).astype(BF16)
     value_grad = dot(e_ref[even, :], ds_ref[...]).astype(BF16)
     for place, target in enumerate(even_refs):
         target[:, :KV_COLS] = key_grad[place * rows : (place + 1) * rows]
         target[:, KV_COLS:] = value_grad[place * rows : (place + 1) * rows]
+
+
+def query_back(u_ref, keys_ref, rs_ref, wq_ref, out_ref, dqt_ref):
+    rows = out_ref.shape[0]
+    wide = 2 * rows
     keys_t = jnp.transpose(keys_ref[...])
     for pair in range(PAIRS):
         group = (2 * pair) // GROUP
@@ -308,48 +329,13 @@
         part = dot(keys_t[group * HEAD_DIM : (group + 1) * HEAD_DIM], u_ref[:, cols]) * rs_ref[0:1, cols]
         dqt_ref[2 * pair * HEAD_DIM : (2 * pair + 1) * HEAD_DIM, :] = part[:, :rows]
         dqt_ref[(2 * pair + 1) * HEAD_DIM : (2 * pair + 2) * HEAD_DIM, :] = part[:, rows:]
-    dq_ref[...] = jnp.transpose(dqt_ref[...]).astype(BF16)
-
-
-def attend_forward(count, *refs):
-    pieces = refs[: count - 3]
-    q_ref, bias_ref, x_ref, wo_ref, top_ref, mix_ref, out_ref = refs[count - 3 : count + 4]
-    kv_ref, s_ref, at_ref = refs[count + 4 :]
-    rows = pieces[0].shape[0]
-    for place, piece in enumerate(pieces):
-        kv_ref[(place + 1) * rows : (place + 2) * rows, :] = piece[:, : 2 * KV_COLS]
-    chunks = late_chunks(count, rows)
-    extended = [with_ones(kv_ref[lines, KV_COLS:]) for lines in chunks]
-    wide = 2 * rows
-    tops = {}
-    for now in range(-1, PAIRS):
-        ahead = now + 1
-        top = mixed = None
-        for place, lines in enumerate(chunks):
-            if ahead < PAIRS:
-                q_rows = q_ref[ahead * wide : (ahead + 1) * wide, :]
-                block = score_block(kv_ref[lines, :KV_COLS], q_rows, bias_ref[lines, :])
-                s_ref[ahead % 2, lines, :] = block
-                part = jnp.max(block, axis=0, keepdims=True)
-                top = part if top is None else jnp.maximum(top, part)
-            if now >= 0:
-                weights = jnp.exp(s_ref[now % 2, lines, :] - tops[now]).astype(BF16)
-                mixed = plus(mixed, dot(extended[place][(2 * now) // GROUP], weights))
-        if ahead < PAIRS:
-            tops[ahead] = jnp.maximum(top, top_ref[ahead : ahead + 1, :])
-        if now >= 0:
-            mixed = mixed + mix_ref[now] * jnp.exp(top_ref[now : now + 1, :] - tops[now])
-            part = mixed[:HEAD_DIM] * (1.0 / mixed[HEAD_DIM : HEAD_DIM + 1])
-            at_ref[2 * now * HEAD_DIM : (2 * now + 1) * HEAD_DIM, :] = part[:, :rows]
-            at_ref[(2 * now + 1) * HEAD_DIM : (2 * now + 2) * HEAD_DIM, :] = part[:, rows:]
-    attended = jnp.transpose(at_ref[...]).astype(BF16)
-    out_ref[...] = (x_ref[...].astype(F32) + dot(attended, wo_ref[...])).astype(BF16)
-
-
-def query_back(dq_ref, wq_ref, next_ref, out_ref, next_hbm, sem):
-    copy = pltpu.make_async_copy(next_ref, next_hbm, sem)
+    query_grad = jnp.transpose(dqt_ref[...]).astype(BF16)
+    out_ref[...] = dot(query_grad, wq_ref[...], NT)
+
+
+def deliver(in_ref, out_hbm, sem):
+    copy = pltpu.make_async_copy(in_ref, out_hbm, sem)
     copy.start()
-    out_ref[...] = dot(dq_ref[...], wq_ref[...], NT)
     copy.wait()
 
 
@@ -494,20 +480,10 @@
         ),
         (pieces[0], *pieces[-2:], qf, qb, dout, bias),
     )
-    layer_out = call(
-        partial(attend_forward, size),
-        shape((rows, width), BF16),
-        (*pieces[1:-2], qf, bias, xf, wo, top, mix),
-        scratch=(
-            pltpu.VMEM((total, 2 * KV_COLS), BF16),
-            pltpu.VMEM((2, total, wide), F32),
-            pltpu.VMEM((HEADS * HEAD_DIM, rows), F32),
-        ),
-    )
-    shifted = lax.ppermute(layer_out, "section", [((i - 1) % sections, i) for i in range(sections)])
-    odd, *later = call(
-        partial(attend_backward, size),
+    layer_out, odd, u, e, qs, ds, keys, rs = call(
+        partial(attend_late, size),
         (
+            shape((rows, width), BF16),
             shape((half, rows, 2 * KV_COLS), BF16),
             shape((total, HEADS * rows), BF16),
             shape((total, HEADS * rows), BF16),
@@ -516,20 +492,22 @@
             shape((total, KV_COLS), BF16),
             shape((8, HEADS * rows), F32),
         ),
-        (*pieces[1:-2], qb, dout, bias, pieces[0], *pieces[-2:], stat, early, early_dp),
+        (
+            *pieces[1:-2],
+            *(qf, xf, wo, top, mix, qb, dout, bias),
+            *(pieces[0], *pieces[-2:], stat, early, early_dp),
+        ),
         scratch=(
+            pltpu.VMEM((total, 2 * KV_COLS), BF16),
             pltpu.VMEM((total, KV_COLS), BF16),
             pltpu.VMEM((2, total, wide), F32),
             pltpu.VMEM((2, total, wide), F32),
             pltpu.VMEM((half * rows, 2 * KV_COLS), F32),
+            pltpu.VMEM((HEADS * HEAD_DIM, rows), F32),
         ),
     )
-    *even, dq = call(
-        finish_backward,
-        (kv_shape,) * half + (shape((rows, HEADS * HEAD_DIM), BF16),),
-        later,
-        scratch=(pltpu.VMEM((HEADS * HEAD_DIM, rows), F32),),
-    )
+    shifted = lax.ppermute(layer_out, "section", [((i - 1) % sections, i) for i in range(sections)])
+    even = call(finish_backward, (kv_shape,) * half, (u, e, qs, ds))
     if by_permutes(size):
         other = swap(odd, 1, size)
         steps = order[half:]
@@ -540,9 +518,10 @@
         places = jnp.argsort(jnp.array(order, jnp.int32) ^ lax.axis_index("seq"))
         summed = lax.psum_scatter(both[places], "seq", scatter_dimension=0, tiled=True)
         received = [summed[0].astype(BF16)]
-    base, forward_next = call(
-        query_back, (shape((rows, width), F32), shape((rows, width), BF16)), (dq, wq, shifted), sems=(), out_hbm=1
-    )
+    base = call(
+        query_back, shape((rows, width), F32), (u, keys, rs, wq), scratch=(pltpu.VMEM((HEADS * HEAD_DIM, rows), F32),)
+    )
+    forward_next = call(deliver, shape((rows, width), BF16), (shifted,), sems=(), out_hbm=1)
     input_grad = call(
         partial(input_back, len(received)), shape((rows, width), BF16), (*received, base, xb, cot, gain, wkv)
     )

time: 42.4 us -> 42.7 us (level)
  waiting for transfers between devices: 16.2 us -> 14 us
  starting transfers between devices: 12.2 us -> 14.3 us
    ppermute x1, waiting for transfers between devices: 6.11 us -> 3.48 us  [on_device(): lax.ppermute(input_grad, 'section', [((i + 1) % sections, i) for i in ran...]
    ppermute x1, starting transfers between devices: 1.79 us -> 3.78 us  [on_device(): lax.ppermute(input_grad, 'section', [((i + 1) % sections, i) for i in ran...]
    ppermute x11, waiting for transfers between devices: 5.92 us -> 7.84 us  [swap(): return lax.ppermute(block, 'seq', [(i, i ^ step) for i in range(size)])]
    ppermute x1, waiting for transfers between devices: 4.19 us -> 2.68 us  [on_device(): lax.ppermute(layer_out, 'section', [((i - 1) % sections, i) for i in rang...]
  transfers between devices with their start and end apart: 13 -> 13, of which waited for: 5 -> 8; matrix products, arithmetic and copies ran while one was open for 0% -> 0% of each run, Pallas kernels for 17% -> 16%
where the time goes in v6:
time: 42.7 us; the launch traced here: 42.6 us
  starting transfers between devices  14.3 us (33%)
  waiting for transfers between devices  14 us (33%)
  Pallas kernels  12.8 us (30%)
  between operations  0.74 us (2%)
  local copies, waits for them, and re-layouts  0.7 us (2%)
    pallas_call x9, Pallas kernels, call(): pl.pallas_call(kernel, out_shape=[pltpu.VMEM(out.shape, out.dtype) for ou...  12.8 us
    ppermute x11, starting transfers between devices, swap(): return lax.ppermute(block, 'seq', [(i, i ^ step) for i in range(size)])  8.77 us
    ppermute x11, waiting for transfers between devices, swap(): return lax.ppermute(block, 'seq', [(i, i ^ step) for i in range(size)])  7.84 us
    ppermute x1, starting transfers between devices, on_device(): lax.ppermute(input_grad, 'section', [((i + 1) % sections, i) for i in ran...  3.78 us
    ppermute x1, waiting for transfers between devices, on_device(): lax.ppermute(input_grad, 'section', [((i + 1) % sections, i) for i in ran...  3.48 us
    ppermute x1, waiting for transfers between devices, on_device(): lax.ppermute(layer_out, 'section', [((i - 1) % sections, i) for i in rang...  2.68 us
    ppermute x1, starting transfers between devices, on_device(): lax.ppermute(layer_out, 'section', [((i - 1) % sections, i) for i in rang...  1.78 us
  transfers between devices with their start and end apart: 13, of which 8 were waited for; matrix products, arithmetic and copies ran while one was open for 0% of the time, Pallas kernels for 16%

profile of v6, /device:TPU:0, one launch (start us, length us, event | category | flops | bytes accessed | tf_op | source)
XLA Modules:
  0.0 42.6 jit_solution(2918912288537688088)
XLA Ops:
  0.6 1.6 %shard_map.113 = (bf16[128,512]{1,0:T(8,128)(2,1)S(1)}, f32[1,1024]{1,0:T(1,128)S(1)}, bf16[128,1024]{1,0:T(8,128)(2,1)S(1)}, bf16[128,1024]{1,0:T(8,128)(2,1)S(1)}, bf16[1024,256]{1,0:T(8,128)(2,1)S(1)}) custom-call(f32[1,1024]{1,0:T(1,128)} %gain_hbm.1, bf16[128,1024]{1,0:T(8,128)(2,1)} %bitcast.15, bf16[128,1024]{1,0:T(8,128)(2,1)} %bitcast.16, ...), custom_call_target="tpu_custom_call" | custom-call | tf_op jit(solution)/shard_map/pallas_call | solution.py:382
  2.3 4.0 %collective-permute-start.4 = (bf16[128,512]{1,0:T(8,128)(2,1)S(1)}, bf16[128,512]{1,0:T(8,128)(2,1)S(1)}, u32[]{:S(2)}, u32[]{:S(2)}) collective-permute-start(bf16[128,512]{1,0:T(8,128)(2,1)S(1)} %get-tuple-element.35.own_ref.refs_15_), channel_id=1, source_target_pairs={{0,6},{1,7},{2,4},{3,5},{4,2},{5,3},{6,0},{7,1},{8,14},{9,15},{10,... | collective-permute-start | bytes 393224 | tf_op jit(solution)/shard_map/ppermute | solution.py:396
  6.2 0.5 %collective-permute-start.2 = (bf16[128,512]{1,0:T(8,128)(2,1)S(1)}, bf16[128,512]{1,0:T(8,128)(2,1)S(1)}, u32[]{:S(2)}, u32[]{:S(2)}) collective-permute-start(bf16[128,512]{1,0:T(8,128)(2,1)S(1)} %get-tuple-element.35.own_ref.refs_15_), channel_id=1, source_target_pairs={{0,4},{1,5},{2,6},{3,7},{4,0},{5,1},{6,2},{7,3},{8,12},{9,13},{10,... | collective-permute-start | bytes 393224 | tf_op jit(solution)/shard_map/ppermute | solution.py:396
  6.7 0.1 collective-permute-start
  6.9 0.0 collective-permute-start.6
  6.9 3.2 %collective-permute-done.4.refs_4_ = bf16[128,512]{1,0:T(8,128)(2,1)S(1)} collective-permute-done((bf16[128,512]{1,0:T(8,128)(2,1)S(1)}, bf16[128,512]{1,0:T(8,128)(2,1)S(1)}, u32[]{:S(2)}, u32[]{:S(2)}) %collective-permute-start.4) | collective-permute-done | bytes 131104 | tf_op jit(solution)/shard_map/ppermute | solution.py:396
  10.1 0.0 collective-permute-start.5
  10.1 2.4 %collective-permute-done.2.refs_3_ = bf16[128,512]{1,0:T(8,128)(2,1)S(1)} collective-permute-done((bf16[128,512]{1,0:T(8,128)(2,1)S(1)}, bf16[128,512]{1,0:T(8,128)(2,1)S(1)}, u32[]{:S(2)}, u32[]{:S(2)}) %collective-permute-start.2) | collective-permute-done | bytes 131104 | tf_op jit(solution)/shard_map/ppermute | solution.py:396
  12.5 0.0 collective-permute-start.3
  12.5 0.2 collective-permute-done.near_ref.refs_14_
  12.8 0.3 collective-permute-start.1
  13.1 2.6 %shard_map.114 = (bf16[1024,128]{1,0:T(8,128)(2,1)S(1)}, bf16[1024,128]{1,0:T(8,128)(2,1)S(1)}, bf16[1024,128]{1,0:T(8,128)(2,1)S(1)}, f32[1024,128]{1,0:T(8,128...) custom-call(s32[1]{0:T(128)} %bitcast.4.me_ref, ...), custom_call_target="tpu_custom_call" | custom-call | tf_op jit(solution)/shard_map/pallas_call | solution.py:382
  15.6 0.0 collective-permute-done.6.far_ref.refs_13_
  15.7 1.5 %shard_map.115 = (f32[4,256]{1,0:T(4,128)S(1)}, f32[4,80,256]{2,1,0:T(8,128)S(1)}, f32[8,1024]{1,0:T(8,128)S(1)}, bf16[384,1024]{1,0:T(8,128)(2,1)S(1)}, f32[384,1024]{1,0:T(8,128)S(1)}) custom-call(bf16[128,512]{1,0:T(8,128)(2,1)S(1)} %collective-permute-done.6.far_ref.refs_13_, bf16[128,512]{1,0:T(8,128)(2,1)S(1)} %collective-permute-done.near_ref.refs_14_, ...), custom_call_target="tpu_custom_call" | custom-call | tf_op jit(solution)/shard_map/pallas_call | solution.py:382
  17.1 0.0 collective-permute-done.5.refs_2_
  17.1 0.0 collective-permute-done.3.refs_1_
  17.2 0.0 collective-permute-done.1.refs_0_
  17.2 4.3 %shard_map.116 = (bf16[128,1024]{1,0:T(8,128)(2,1)S(1)}, bf16[4,128,256]{2,1,0:T(8,128)(2,1)S(1)}, bf16[1024,1024]{1,0:T(8,128)(2,1)S(1)}, bf16[1024,1024]{1,0:T...) custom-call(bf16[128,512]{1,0:T(8,128)(2,1)S(1)} %collective-permute, ...), custom_call_target="tpu_custom_call" | custom-call | tf_op jit(solution)/shard_map/pallas_call | solution.py:382
  21.5 0.3 collective-permute-start.8
  21.8 0.7 %shard_map.118 = (bf16[128,256]{1,0:T(8,128)(2,1)S(1)}, bf16[128,256]{1,0:T(8,128)(2,1)S(1)}, bf16[128,256]{1,0:T(8,128)(2,1)S(1)}, bf16[128,256]{1,0:T(8,128)(2,1)S(1)}) custom-call(bf16[1024,1024]{1,0:T(8,128)(2,1)S(1)} %get-tuple-element.50.u_ref, bf16[1024,1024]{1,0:T(8,128)(2,1)S(1)} %get-tuple-element.51.e_ref, ...), custom_call_target="tpu_custom_call" | custom-call | tf_op jit(solution)/shard_map/pallas_call | solution.py:382
  22.5 0.6 %collective-permute-done.8.refs_4_ = bf16[4,128,256]{2,1,0:T(8,128)(2,1)S(1)} collective-permute-done((bf16[4,128,256]{2,1,0:T(8,128)(2,1)S(1)}, bf16[4,128,256]{2,1,0:T(8,128)(2,1)S(1)}, u32[]{:S(2)}, u32[]{:S(2)}) %collective-permute-start.8) | collective-permute-done | bytes 262176 | tf_op jit(solution)/shard_map/ppermute | solution.py:396
  23.1 0.1 shard_map.119
  23.1 1.8 %collective-permute-start.9 = (bf16[128,256]{1,0:T(8,128)(2,1)S(1)}, bf16[128,256]{1,0:T(8,128)(2,1)S(1)}, u32[]{:S(2)}, u32[]{:S(2)}) collective-permute-start(bf16[128,256]{1,0:T(8,128)(2,1)S(1)} %get-tuple-element.60), channel_id=1, source_target_pairs={{0,2},{1,3},{2,0},{3,1},{4,6},{5,7},{6,4},{7,5},{8,10},{9,11},{10,... | collective-permute-start | bytes 196616 | tf_op jit(solution)/shard_map/ppermute | solution.py:396
  24.9 0.7 %collective-permute-start.10 = (bf16[128,256]{1,0:T(8,128)(2,1)S(1)}, bf16[128,256]{1,0:T(8,128)(2,1)S(1)}, u32[]{:S(2)}, u32[]{:S(2)}) collective-permute-start(bf16[128,256]{1,0:T(8,128)(2,1)S(1)} %get-tuple-element.61), channel_id=1, source_target_pairs={{0,4},{1,5},{2,6},{3,7},{4,0},{5,1},{6,2},{7,3},{8,12},{9,13},{10,... | collective-permute-start | bytes 196616 | tf_op jit(solution)/shard_map/ppermute | solution.py:396
  25.6 1.1 %collective-permute-start.11 = (bf16[128,256]{1,0:T(8,128)(2,1)S(1)}, bf16[128,256]{1,0:T(8,128)(2,1)S(1)}, u32[]{:S(2)}, u32[]{:S(2)}) collective-permute-start(bf16[128,256]{1,0:T(8,128)(2,1)S(1)} %get-tuple-element.62), channel_id=1, source_target_pairs={{0,6},{1,7},{2,4},{3,5},{4,2},{5,3},{6,0},{7,1},{8,14},{9,15},{10,... | collective-permute-start | bytes 196616 | tf_op jit(solution)/shard_map/ppermute | solution.py:396
  26.7 1.8 %collective-permute-start.7 = (bf16[128,1024]{1,0:T(8,128)(2,1)S(1)}, bf16[128,1024]{1,0:T(8,128)(2,1)S(1)}, u32[]{:S(2)}, u32[]{:S(2)}) collective-permute-start(bf16[128,1024]{1,0:T(8,128)(2,1)S(1)} %get-tuple-element.49), channel_id=1, source_target_pairs={{24,0},{0,8},{8,16},{16,24},{25,1},{1,9},{9,17},{17,25},{26,2},{2,... | collective-permute-start | bytes 786440 | tf_op jit(solution)/shard_map/ppermute | solution.py:509
  28.5 0.9 %shard_map.120.refs_4_ = f32[128,1024]{1,0:T(8,128)S(1)} custom-call(bf16[1024,1024]{1,0:T(8,128)(2,1)S(1)} %get-tuple-element.50.u_ref, bf16[1024,128]{1,0:T(8,128)(2,1)S(1)} %get-tuple-element.63.keys_ref, f32[8,1024]{1,0:T(8,128)S(1)} %get-tuple-element.64.rs_ref, bf16[1024,512]{1,0:T(8,128)(2,1)S(1)} %get-tuple-element.65.wq_ref), custom_call_target="tpu_custom_call" | custom-call | tf_op jit(solution)/shard_map/pallas_call | solution.py:382
  29.4 0.0 collective-permute-done.9.refs_1_
  29.4 0.5 %collective-permute-done.10.refs_2_ = bf16[128,256]{1,0:T(8,128)(2,1)S(1)} collective-permute-done((bf16[128,256]{1,0:T(8,128)(2,1)S(1)}, bf16[128,256]{1,0:T(8,128)(2,1)S(1)}, u32[]{:S(2)}, u32[]{:S(2)}) %collective-permute-start.10) | collective-permute-done | bytes 65568 | tf_op jit(solution)/shard_map/ppermute | solution.py:396
  29.9 0.9 %collective-permute-done.11.refs_3_ = bf16[128,256]{1,0:T(8,128)(2,1)S(1)} collective-permute-done((bf16[128,256]{1,0:T(8,128)(2,1)S(1)}, bf16[128,256]{1,0:T(8,128)(2,1)S(1)}, u32[]{:S(2)}, u32[]{:S(2)}) %collective-permute-start.11) | collective-permute-done | bytes 65568 | tf_op jit(solution)/shard_map/ppermute | solution.py:396
  30.8 0.4 %shard_map.121 = bf16[128,1024]{1,0:T(8,128)(2,1)S(1)} custom-call(bf16[128,256]{1,0:T(8,128)(2,1)S(1)} %get-tuple-element.59.refs_0_, bf16[128,256]{1,0:T(8,128)(2,1)S(1)} %collective-permute-done.9.refs_1_, bf16[128,256]{1,0:T(8,128)(2,1)S(1)} %collective-permute-done.10.refs_2_, bf16[128,256]{1,0:T(8,128)(2,1)S(1)} %collective-permute-done.11.refs_3_, ...), custom_call_target="tpu_custom_call" | custom-call | tf_op jit(solution)/shard_map/pallas_call | solution.py:382
  31.2 3.8 %collective-permute-start.12 = (bf16[128,1024]{1,0:T(8,128)(2,1)S(1)}, bf16[128,1024]{1,0:T(8,128)(2,1)S(1)}, u32[]{:S(2)}, u32[]{:S(2)}) collective-permute-start(bf16[128,1024]{1,0:T(8,128)(2,1)S(1)} %shard_map.121), channel_id=1, source_target_pairs={{8,0},{16,8},{24,16},{0,24},{9,1},{17,9},{25,17},{1,25},{10,2},{18... | collective-permute-start | bytes 786440 | tf_op jit(solution)/shard_map/ppermute | solution.py:528
  35.0 2.7 %collective-permute-done.7.in_ref = bf16[128,1024]{1,0:T(8,128)(2,1)S(1)} collective-permute-done((bf16[128,1024]{1,0:T(8,128)(2,1)S(1)}, bf16[128,1024]{1,0:T(8,128)(2,1)S(1)}, u32[]{:S(2)}, u32[]{:S(2)}) %collective-permute-start.7) | collective-permute-done | bytes 262176 | tf_op jit(solution)/shard_map/ppermute | solution.py:509
  37.7 0.7 %shard_map.117 = bf16[128,1024]{1,0:T(8,128)(2,1)} custom-call(bf16[128,1024]{1,0:T(8,128)(2,1)S(1)} %collective-permute-done.7.in_ref), custom_call_target="tpu_custom_call" | custom-call | tf_op jit(solution)/shard_map/pallas_call | solution.py:382
  38.4 3.5 %collective-permute-done.12 = bf16[128,1024]{1,0:T(8,128)(2,1)S(1)} collective-permute-done((bf16[128,1024]{1,0:T(8,128)(2,1)S(1)}, bf16[128,1024]{1,0:T(8,128)(2,1)S(1)}, u32[]{:S(2)}, u32[]{:S(2)}) %collective-permute-start.12) | collective-permute-done | bytes 262176 | tf_op jit(solution)/shard_map/ppermute | solution.py:528
  41.9 0.7 %copy.13 = bf16[1,128,1024]{2,1,0:T(8,128)(2,1)} copy(bf16[1,128,1024]{2,1,0:T(8,128)(2,1)S(1)} %bitcast.14) | data formatting | bytes 524288
Async XLA Ops:
  2.3 7.9 %collective-permute-start.4 = (bf16[128,512]{1,0:T(8,128)(2,1)S(1)}, bf16[128,512]{1,0:T(8,128)(2,1)S(1)}, u32[]{:S(2)}, u32[]{:S(2)}) collective-permute-start(bf16[128,512]{1,0:T(8,128)(2,1)S(1)} %get-tuple-element.35.own_ref.refs_15_), channel_id=1, source_target_pairs={{0,6},{1,7},{2,4},{3,5},{4,2},{5,3},{6,0},{7,1},{8,14},{9,15},{10,... | collective-permute-start | bytes 393224 | tf_op jit(solution)/shard_map/ppermute | solution.py:396
  6.2 6.3 %collective-permute-start.2 = (bf16[128,512]{1,0:T(8,128)(2,1)S(1)}, bf16[128,512]{1,0:T(8,128)(2,1)S(1)}, u32[]{:S(2)}, u32[]{:S(2)}) collective-permute-start(bf16[128,512]{1,0:T(8,128)(2,1)S(1)} %get-tuple-element.35.own_ref.refs_15_), channel_id=1, source_target_pairs={{0,4},{1,5},{2,6},{3,7},{4,0},{5,1},{6,2},{7,3},{8,12},{9,13},{10,... | collective-permute-start | bytes 393224 | tf_op jit(solution)/shard_map/ppermute | solution.py:396
  6.7 6.0 %collective-permute-start = (bf16[128,512]{1,0:T(8,128)(2,1)S(1)}, bf16[128,512]{1,0:T(8,128)(2,1)S(1)}, u32[]{:S(2)}, u32[]{:S(2)}) collective-permute-start(bf16[128,512]{1,0:T(8,128)(2,1)S(1)} %get-tuple-element.35.own_ref.refs_15_), channel_id=1, source_target_pairs={{0,2},{1,3},{2,0},{3,1},{4,6},{5,7},{6,4},{7,5},{8,10},{9,11},{10,... | collective-permute-start | bytes 393224 | tf_op jit(solution)/shard_map/ppermute | solution.py:396
  6.9 8.8 %collective-permute-start.6 = (bf16[128,512]{1,0:T(8,128)(2,1)S(1)}, bf16[128,512]{1,0:T(8,128)(2,1)S(1)}, u32[]{:S(2)}, u32[]{:S(2)}) collective-permute-start(bf16[128,512]{1,0:T(8,128)(2,1)S(1)} %get-tuple-element.35.own_ref.refs_15_), channel_id=1, source_target_pairs={{0,1},{1,0},{2,3},{3,2},{4,5},{5,4},{6,7},{7,6},{8,9},{9,8},{10,11... | collective-permute-start | bytes 393224 | tf_op jit(solution)/shard_map/ppermute | solution.py:396
  10.1 7.0 %collective-permute-start.5 = (bf16[128,512]{1,0:T(8,128)(2,1)S(1)}, bf16[128,512]{1,0:T(8,128)(2,1)S(1)}, u32[]{:S(2)}, u32[]{:S(2)}) collective-permute-start(bf16[128,512]{1,0:T(8,128)(2,1)S(1)} %collective-permute-done.4.refs_4_), channel_id=1, source_target_pairs={{0,1},{1,0},{2,3},{3,2},{4,5},{5,4},{6,7},{7,6},{8,9},{9,8},{10,11... | collective-permute-start | bytes 393224 | tf_op jit(solution)/shard_map/ppermute | solution.py:396
  12.5 4.6 %collective-permute-start.3 = (bf16[128,512]{1,0:T(8,128)(2,1)S(1)}, bf16[128,512]{1,0:T(8,128)(2,1)S(1)}, u32[]{:S(2)}, u32[]{:S(2)}) collective-permute-start(bf16[128,512]{1,0:T(8,128)(2,1)S(1)} %collective-permute-done.2.refs_3_), channel_id=1, source_target_pairs={{0,1},{1,0},{2,3},{3,2},{4,5},{5,4},{6,7},{7,6},{8,9},{9,8},{10,11... | collective-permute-start | bytes 393224 | tf_op jit(solution)/shard_map/ppermute | solution.py:396
  12.8 4.4 %collective-permute-start.1 = (bf16[128,512]{1,0:T(8,128)(2,1)S(1)}, bf16[128,512]{1,0:T(8,128)(2,1)S(1)}, u32[]{:S(2)}, u32[]{:S(2)}) collective-permute-start(bf16[128,512]{1,0:T(8,128)(2,1)S(1)} %collective-permute-done.near_ref.refs_14_), channel_id=1, source_target_pairs={{0,1},{1,0},{2,3},{3,2},{4,5},{5,4},{6,7},{7,6},{8,9},{9,8},{10,11... | collective-permute-start | bytes 393224 | tf_op jit(solution)/shard_map/ppermute | solution.py:396
  21.5 1.6 %collective-permute-start.8 = (bf16[4,128,256]{2,1,0:T(8,128)(2,1)S(1)}, bf16[4,128,256]{2,1,0:T(8,128)(2,1)S(1)}, u32[]{:S(2)}, u32[]{:S(2)}) collective-permute-start(bf16[4,128,256]{2,1,0:T(8,128)(2,1)S(1)} %get-tuple-element.58), channel_id=1, source_target_pairs={{0,1},{1,0},{2,3},{3,2},{4,5},{5,4},{6,7},{7,6},{8,9},{9,8},{10,11... | collective-permute-start | bytes 786440 | tf_op jit(solution)/shard_map/ppermute | solution.py:396
  23.1 6.3 %collective-permute-start.9 = (bf16[128,256]{1,0:T(8,128)(2,1)S(1)}, bf16[128,256]{1,0:T(8,128)(2,1)S(1)}, u32[]{:S(2)}, u32[]{:S(2)}) collective-permute-start(bf16[128,256]{1,0:T(8,128)(2,1)S(1)} %get-tuple-element.60), channel_id=1, source_target_pairs={{0,2},{1,3},{2,0},{3,1},{4,6},{5,7},{6,4},{7,5},{8,10},{9,11},{10,... | collective-permute-start | bytes 196616 | tf_op jit(solution)/shard_map/ppermute | solution.py:396
  24.9 5.0 %collective-permute-start.10 = (bf16[128,256]{1,0:T(8,128)(2,1)S(1)}, bf16[128,256]{1,0:T(8,128)(2,1)S(1)}, u32[]{:S(2)}, u32[]{:S(2)}) collective-permute-start(bf16[128,256]{1,0:T(8,128)(2,1)S(1)} %get-tuple-element.61), channel_id=1, source_target_pairs={{0,4},{1,5},{2,6},{3,7},{4,0},{5,1},{6,2},{7,3},{8,12},{9,13},{10,... | collective-permute-start | bytes 196616 | tf_op jit(solution)/shard_map/ppermute | solution.py:396
  25.6 5.2 %collective-permute-start.11 = (bf16[128,256]{1,0:T(8,128)(2,1)S(1)}, bf16[128,256]{1,0:T(8,128)(2,1)S(1)}, u32[]{:S(2)}, u32[]{:S(2)}) collective-permute-start(bf16[128,256]{1,0:T(8,128)(2,1)S(1)} %get-tuple-element.62), channel_id=1, source_target_pairs={{0,6},{1,7},{2,4},{3,5},{4,2},{5,3},{6,0},{7,1},{8,14},{9,15},{10,... | collective-permute-start | bytes 196616 | tf_op jit(solution)/shard_map/ppermute | solution.py:396
  26.7 11.0 %collective-permute-start.7 = (bf16[128,1024]{1,0:T(8,128)(2,1)S(1)}, bf16[128,1024]{1,0:T(8,128)(2,1)S(1)}, u32[]{:S(2)}, u32[]{:S(2)}) collective-permute-start(bf16[128,1024]{1,0:T(8,128)(2,1)S(1)} %get-tuple-element.49), channel_id=1, source_target_pairs={{24,0},{0,8},{8,16},{16,24},{25,1},{1,9},{9,17},{17,25},{26,2},{2,... | collective-permute-start | bytes 786440 | tf_op jit(solution)/shard_map/ppermute | solution.py:509
  31.2 10.7 %collective-permute-start.12 = (bf16[128,1024]{1,0:T(8,128)(2,1)S(1)}, bf16[128,1024]{1,0:T(8,128)(2,1)S(1)}, u32[]{:S(2)}, u32[]{:S(2)}) collective-permute-start(bf16[128,1024]{1,0:T(8,128)(2,1)S(1)} %shard_map.121), channel_id=1, source_target_pairs={{8,0},{16,8},{24,16},{0,24},{9,1},{17,9},{25,17},{1,25},{10,2},{18... | collective-permute-start | bytes 786440 | tf_op jit(solution)/shard_map/ppermute | solution.py:528
